TPU v7x, 256 devices: a whole 4x4x8 slice. The times are simulated.
256 devices in a mesh: blk: 16 (over x, y_lo, core), grp: 16 (over z, y_hi).
Axes of the slice: x: 4, y: 4 (y_hi: 2, y_lo: 2; y = y_hi * 2 + y_lo), z: 8, core: 2. Of those that a mesh axis runs over, the one named last changes fastest.
Arguments:
- phase_space: float32 [6, 32768], P(None, 'blk'), may hold values from -3.5 to 3.5
- force_rates: float32 [6, 32768], P(None, 'blk'), may hold values from -4 to 4
- irregular: float32 [6, 32768], P(None, 'blk'), may hold values from -3 to 3
- stellar_masses: float32 [32768], P('blk'), may hold values from 9.155274e-06 to 9.1552734e-05
- levels: int32 [256], P('blk'), may hold values from 0 to 3, as said below
- active: int32 [4, 256], P(None, 'blk'), may hold values from 0 to 1, as said below
- partner: int32 [256], P('blk'), may hold values from 0 to 255, as said below
Outputs:
- kinematics: float32 [6, 32768], P(None, 'blk')
- combined_force: float32 [6, 32768], P(None, 'blk')
- irregular_force: float32 [6, 32768], P(None, 'blk')
Inputs may be any that keep to these rules, and one draw needn't show every extreme that they name: levels of 0 to 3; in every shard 2 to 4 blocks have level 0, at most 6 level 1 or less and at most 8 level 2 or less, and some shard has exactly 4, 6 and 8. active[n, b] is 1 exactly when n + 1 is a multiple of 2 ** levels[b]. partner is mutual (the partner of partner[b] is b) and has the same place within its shard; the blocks of one shard have exactly 1 partner on each shard, their own shard included, where the one block is its own partner.
All inputs are finite; a program needn't handle non-finite values.
Results may differ from a plain program's by a relative error of at most 0.0003.
Values sent between devices are 32-bit elements; how exact they have to be, the bound alone decides.
No kernel may reach another device: no remote copies, remote signals or barrier semaphores. Data moves between devices by JAX's collectives and lax.ppermute only.
A program may use at most 64 MiB of HBM per device.

v0:
```python
import jax
import jax.numpy as jnp
from jax import lax
from jax.sharding import PartitionSpec as P

STEPS = 4
MOST = 1


soft_wide = 0.04
soft_close = 0.0001
time_tick = 0.125


def pair_terms(targets, sources, soften):
    offset = sources[0:3][..., None, :] - targets[0:3][..., :, None]
    motion = sources[3:6][..., None, :] - targets[3:6][..., :, None]
    distance = jnp.sum(offset * offset, axis=0) + soften
    inverse = lax.rsqrt(distance)
    weight = sources[6][..., None, :] * inverse * inverse * inverse
    radial = jnp.sum(offset * motion, axis=0) / distance
    acceleration = jnp.sum(weight * offset, axis=-1)
    jerk_term = jnp.sum(weight * (motion - 3.0 * radial * offset), axis=-1)
    return jnp.concatenate([acceleration, jerk_term], axis=0)


def predict_orbits(kinematic, slopes, interval):
    half_square = interval * interval * 0.5
    cube_sixth = interval * interval * interval / 6.0
    position = (
        kinematic[0:3]
        + kinematic[3:6] * interval
        + slopes[0:3] * half_square
        + slopes[3:6] * cube_sixth
    )
    velocity = kinematic[3:6] + slopes[0:3] * interval + slopes[3:6] * half_square
    return jnp.concatenate([position, velocity], axis=0)


def correct(kinematic, slopes, renewed, interval):
    velocity = (
        kinematic[3:6]
        + (slopes[0:3] + renewed[0:3]) * (interval * 0.5)
        + (slopes[3:6] - renewed[3:6]) * (interval * interval / 12.0)
    )
    position = (
        kinematic[0:3]
        + (kinematic[3:6] + velocity) * (interval * 0.5)
        + (slopes[0:3] - renewed[0:3]) * (interval * interval / 12.0)
    )
    return jnp.concatenate([position, velocity], axis=0)


def write_back(current, renewed, packed_layout, live_flag, block_members):
    layout = current.reshape(current.shape[0], -1, block_members)
    previous = layout[:, packed_layout, :]
    update = jnp.where(live_flag[None, :, None] > 0, renewed, previous)
    return layout.at[:, packed_layout, :].set(update).reshape(current.shape[0], -1)


def body(phase_space, force_rates, irregular, stellar_masses, levels, active, partner):
    block_list = levels.shape[0]
    block_members = phase_space.shape[1] // block_list
    cycle_size = lax.axis_size("blk")
    own_shard = lax.axis_index("blk")
    columns = lax.axis_size("grp")
    column = lax.axis_index("grp")
    slice_width = phase_space.shape[1] // columns
    limits = [block_list // 4, 3 * block_list // 8, block_list // 2, block_list]
    kinematics, combined_force, irregular_force = (phase_space, force_rates, irregular)
    for moment in range(STEPS):
        number = moment + 1
        capacity = limits[min((number & -number).bit_length() - 1, 3)]
        period = jnp.power(2, levels)
        updated = moment // period * period
        block_interval = (number - updated).astype(jnp.float32) * time_tick
        extrapolated_state = predict_orbits(
            kinematics, combined_force, jnp.repeat(block_interval, block_members)
        )
        star_registry = jnp.concatenate([extrapolated_state, stellar_masses[None, :]], axis=0)
        catalog_grid = star_registry.reshape(7, block_list, block_members)
        packed_layout = jnp.argsort(1 - active[moment], stable=True)[:capacity]
        live_flag = active[moment][packed_layout]
        incoming_stars = extrapolated_state.reshape(6, block_list, block_members)[
            :, packed_layout, :
        ].reshape(6, capacity * block_members)
        sources = lax.dynamic_slice_in_dim(star_registry, column * slice_width, slice_width, 1)
        regular_part = pair_terms(
            incoming_stars, lax.all_gather(sources, "blk", axis=1, tiled=True), soft_wide
        )
        wanted = partner[packed_layout]
        holder = wanted // block_list
        inside = wanted % block_list
        foreign = holder != own_shard
        position_idx = jnp.arange(capacity)
        earlier = (holder[:, None] == holder[None, :]) & (
            position_idx[:, None] > position_idx[None, :]
        )
        bucket = jnp.sum(earlier.astype(jnp.int32), axis=1)
        request = (
            jnp.full((cycle_size, MOST), -1, jnp.int32)
            .at[holder, bucket]
            .set(jnp.where((live_flag > 0) & foreign, inside, -1))
        )
        requested = lax.all_to_all(request, "blk", split_axis=0, concat_axis=0, tiled=True)
        located = catalog_grid[:, jnp.clip(requested, 0, block_list - 1), :]
        located = jnp.where(requested[None, :, :, None] >= 0, located, 0.0)
        answered = lax.all_to_all(located, "blk", split_axis=1, concat_axis=1, tiled=True)
        partner_rows = answered[:, holder, bucket, :]
        nearby = jnp.concatenate([catalog_grid[:, packed_layout, :], partner_rows], axis=2)
        previous_state = kinematics.reshape(6, block_list, block_members)[
            :, packed_layout, :
        ].reshape(6, -1)
        previous_slope = combined_force.reshape(6, block_list, block_members)[
            :, packed_layout, :
        ].reshape(6, -1)
        interval_star = jnp.repeat(block_interval[packed_layout], block_members)
        regular_total = lax.psum(regular_part, "grp")
        targets = incoming_stars.reshape(6, capacity, block_members)
        close_part = (
            pair_terms(targets, nearby, soft_close) - pair_terms(targets, nearby, soft_wide)
        ).reshape(6, -1)
        combined = regular_total + close_part
        renewed = correct(previous_state, previous_slope, combined, interval_star)
        kinematics = write_back(
            kinematics,
            renewed.reshape(6, capacity, block_members),
            packed_layout,
            live_flag,
            block_members,
        )
        combined_force = write_back(
            combined_force,
            combined.reshape(6, capacity, block_members),
            packed_layout,
            live_flag,
            block_members,
        )
        irregular_force = write_back(
            irregular_force,
            close_part.reshape(6, capacity, block_members),
            packed_layout,
            live_flag,
            block_members,
        )
    return (kinematics, combined_force, irregular_force)


def solution(mesh):
    in_specs = (
        P(None, "blk"),
        P(None, "blk"),
        P(None, "blk"),
        P("blk"),
        P("blk"),
        P(None, "blk"),
        P("blk"),
    )
    out_specs = (P(None, "blk"), P(None, "blk"), P(None, "blk"))
    return jax.shard_map(body, mesh=mesh, in_specs=in_specs, out_specs=out_specs, check_vma=False)
```

profile of v0, /device:TPU:2, one launch (start us, length us, event | category | flops | bytes accessed | tf_op | source)
XLA Modules:
  0.0 570.0 jit_solution(3351264058275297556)
XLA Ops:
  0.7 0.8 copy.212
  1.5 0.8 copy.213
  2.3 0.8 copy.214
  3.2 0.8 broadcast_subtract_fusion.2
  4.0 0.8 slice_bitcast_fusion.16
  4.9 1.2 sort.59
  6.1 1.2 sort.61
  10.1 5.9 %all-to-all-start = ((s32[16,1,1]{2,1,0:T(1,128)}), s32[16,1,1]{2,1,0:T(1,128)S(1)}, u32[]{:S(2)}, u32[]{:S(2)}) async-start(s32[16,1,1]{2,1,0:T(1,128)} %copy.93), calls=%async_computation | async-start | bytes 16384 | tf_op jit(solution)/shard_map/all_to_all | solution.py:105
  16.0 0.8 fusion.137
  17.9 17.5 %all_gather.12 = f32[7,2048]{1,0:T(8,128)S(1)} all-gather(f32[7,128]{1,0:T(8,128)S(1)} %fusion.126), channel_id=1, replica_groups=mesh['blk'=16,'grp'=16] {'blk'}, dimensions={1}, use_global_device_ids=true | all-gather | bytes 60928 | tf_op jit(solution)/shard_map/all_gather | solution.py:89
  36.3 1.3 sort.60
  40.4 1.3 sort.62
  44.2 4.0 fusion.14
  48.1 1.9 divide_multiply_fusion.3
  50.0 4.7 fusion.15
  54.8 79.9 %psum.28 = f32[6,512]{1,0:T(8,128)S(1)} all-reduce(f32[6,512]{1,0:T(8,128)S(1)} %pad_maximum_fusion.13), channel_id=1, replica_groups=mesh['blk'=16,'grp'=16] {'grp'}, use_global_device_ids=true, to_apply=%region_5.6 | all-reduce | flops 3072 | bytes 24576 | tf_op jit(solution)/shard_map/psum | solution.py:118
  143.4 6.0 %all-to-all-start.2 = ((s32[16,1,1]{2,1,0:T(1,128)}), s32[16,1,1]{2,1,0:T(1,128)S(1)}, u32[]{:S(2)}, u32[]{:S(2)}) async-start(s32[16,1,1]{2,1,0:T(1,128)} %copy.100), calls=%async_computation.2 | async-start | bytes 16384 | tf_op jit(solution)/shard_map/all_to_all | solution.py:105
  149.7 4.3 all-to-all-done.2
  154.0 4.7 all-to-all-start.4
  159.7 3.7 all-to-all-done.4
  163.4 4.7 all-to-all-start.6
  170.5 2.4 all-to-all-done.6
  173.0 5.3 all-to-all-start.1
  179.1 3.9 all-to-all-done.1
  184.4 2.0 fusion.45
  188.3 16.0 %all_gather.13 = f32[7,2048]{1,0:T(8,128)S(1)} all-gather(f32[7,128]{1,0:T(8,128)S(1)} %fusion.124), channel_id=1, replica_groups=mesh['blk'=16,'grp'=16] {'blk'}, dimensions={1}, use_global_device_ids=true | all-gather | bytes 60928 | tf_op jit(solution)/shard_map/all_gather | solution.py:89
  205.7 6.0 %all-to-all-start.3 = ((f32[7,16,1,128]{3,2,0,1:T(1,128)}), f32[7,16,1,128]{3,2,0,1:T(1,128)S(1)}, u32[]{:S(2)}, u32[]{:S(2)}) async-start(f32[7,16,1,128]{3,2,0,1:T(1,128)} %copy.101), calls=%async_computation.3 | async-start | bytes 114688 | tf_op jit(solution)/shard_map/all_to_all | solution.py:108
  212.3 6.3 %fusion.7 = (f32[768,2048]{1,0:T(8,128)S(1)}, f32[768,2048]{1,0:T(8,128)S(1)}) fusion(f32[3,768]{1,0:T(4,128)S(1)} %get-tuple-element.157, f32[3,2048]{1,0:T(4,128)S(1)} %get-tuple-element.143, f32[3,768]{1,0:T(4,128)S(1)} %get-tuple-element.158, f32[3,2048]{1,0:T(4,128)S(1)} %get-tuple-element.142), kind=kLoop, calls=%fused_computation.81 | loop fusion | flops 25165824 | bytes 12650496 | tf_op jit(solution)/shard_map/reduce_sum | solution.py:18
  218.6 3.0 divide_multiply_fusion.1
  221.6 7.2 %fusion.8 = (f32[3,768]{1,0:T(4,128)S(1)}, f32[3,768]{1,0:T(4,128)S(1)}) fusion(f32[768,2048]{1,0:T(8,128)S(1)} %get-tuple-element.93, f32[3,768]{1,0:T(4,128)S(1)} %get-tuple-element.157, f32[3,2048]{1,0:T(4,128)S(1)} %get-tuple-element.143, f32[768,2048]{1,0:T(8,128)S(1)} %get-tuple-element.92, f32[3,768]{1,0:T(4,128)S(1)} %get-tuple-element.158, ...), kind=kLoop, calls=%fused_computation.82 | loop fusion | flops 37744128 | bytes 12668928 | tf_op jit(solution)/shard_map/reduce_sum | solution.py:22
  231.8 71.9 %psum.29 = f32[6,768]{1,0:T(8,128)S(1)} all-reduce(f32[6,768]{1,0:T(8,128)S(1)} %pad_maximum_fusion.10), channel_id=1, replica_groups=mesh['blk'=16,'grp'=16] {'grp'}, use_global_device_ids=true, to_apply=%region_21.22 | all-reduce | flops 4608 | bytes 36864 | tf_op jit(solution)/shard_map/psum | solution.py:118
  304.3 0.9 fusion.32
  305.7 3.0 fusion.33
  310.8 17.6 %all_gather.14 = f32[7,2048]{1,0:T(8,128)S(1)} all-gather(f32[7,128]{1,0:T(8,128)S(1)} %fusion.122), channel_id=1, replica_groups=mesh['blk'=16,'grp'=16] {'blk'}, dimensions={1}, use_global_device_ids=true | all-gather | bytes 60928 | tf_op jit(solution)/shard_map/all_gather | solution.py:89
  329.8 6.2 %all-to-all-start.5 = ((f32[7,16,1,128]{3,2,0,1:T(1,128)}), f32[7,16,1,128]{3,2,0,1:T(1,128)S(1)}, u32[]{:S(2)}, u32[]{:S(2)}) async-start(f32[7,16,1,128]{3,2,0,1:T(1,128)} %copy.108), calls=%async_computation.5 | async-start | bytes 114688 | tf_op jit(solution)/shard_map/all_to_all | solution.py:108
  336.6 4.0 fusion.17
  340.6 1.9 divide_multiply_fusion.2
  342.4 4.7 fusion.18
  350.2 73.7 %psum.30 = f32[6,512]{1,0:T(8,128)S(1)} all-reduce(f32[6,512]{1,0:T(8,128)S(1)} %pad_maximum_fusion.14), channel_id=1, replica_groups=mesh['blk'=16,'grp'=16] {'grp'}, use_global_device_ids=true, to_apply=%region_37.38 | all-reduce | flops 3072 | bytes 24576 | tf_op jit(solution)/shard_map/psum | solution.py:118
  425.3 2.0 fusion.49
  429.2 17.0 %all_gather.15 = f32[7,2048]{1,0:T(8,128)S(1)} all-gather(f32[7,128]{1,0:T(8,128)S(1)} %fusion.120), channel_id=1, replica_groups=mesh['blk'=16,'grp'=16] {'blk'}, dimensions={1}, use_global_device_ids=true | all-gather | bytes 60928 | tf_op jit(solution)/shard_map/all_gather | solution.py:89
  447.6 6.0 %all-to-all-start.7 = ((f32[7,16,1,128]{3,2,0,1:T(1,128)}), f32[7,16,1,128]{3,2,0,1:T(1,128)S(1)}, u32[]{:S(2)}, u32[]{:S(2)}) async-start(f32[7,16,1,128]{3,2,0,1:T(1,128)} %copy.115), calls=%async_computation.7 | async-start | bytes 114688 | tf_op jit(solution)/shard_map/all_to_all | solution.py:108
  454.1 13.7 %fusion.2 = (f32[1024,2048]{1,0:T(8,128)}, f32[1024,2048]{1,0:T(8,128)}) fusion(f32[3,1024]{1,0:T(4,128)S(1)} %get-tuple-element.149, f32[3,2048]{1,0:T(4,128)S(1)} %get-tuple-element.139, f32[3,1024]{1,0:T(4,128)S(1)} %get-tuple-element.150, f32[3,2048]{1,0:T(4,128)S(1)} %get-tuple-element.138), kind=kLoop, calls=%fused_computation.76 | loop fusion | flops 33554432 | bytes 16850944 | tf_op jit(solution)/shard_map/reduce_sum | solution.py:18
  467.9 7.0 %divide_multiply_fusion = (f32[1024,2048]{1,0:T(8,128)S(1)}, f32[1024,2048]{1,0:T(8,128)S(1)}) fusion(f32[1024,2048]{1,0:T(8,128)} %get-tuple-element.40, f32[1024,2048]{1,0:T(8,128)} %get-tuple-element.39, f32[2048]{0:T(1024)S(1)} %bitcast.628), kind=kLoop, calls=%fused_computation.104 | loop fusion | flops 12582912 | bytes 33562624 | tf_op jit(solution)/shard_map/mul | solution.py:23
  474.8 9.4 %fusion.3 = (f32[3,1024]{1,0:T(4,128)S(1)}, f32[3,1024]{1,0:T(4,128)S(1)}) fusion(f32[1024,2048]{1,0:T(8,128)S(1)} %get-tuple-element.91, f32[3,1024]{1,0:T(4,128)S(1)} %get-tuple-element.149, f32[3,2048]{1,0:T(4,128)S(1)} %get-tuple-element.139, f32[1024,2048]{1,0:T(8,128)S(1)} %get-tuple-element.90, f32[3,1024]{1,0:T(4,128)S(1)} %get-tuple-element.150, ...), kind=kLoop, calls=%fused_computation.77 | loop fusion | flops 50325504 | bytes 16875520 | tf_op jit(solution)/shard_map/reduce_sum | solution.py:22
  487.2 72.8 %psum.31 = f32[6,1024]{1,0:T(8,128)S(1)} all-reduce(f32[6,1024]{1,0:T(8,128)S(1)} %pad_maximum_fusion.8), channel_id=1, replica_groups=mesh['blk'=16,'grp'=16] {'grp'}, use_global_device_ids=true, to_apply=%region_53.54 | all-reduce | flops 6144 | bytes 49152 | tf_op jit(solution)/shard_map/psum | solution.py:118
  560.7 1.2 fusion.24
  562.5 4.0 fusion.25
  (262 shorter events, 51.0 us)
Async XLA Ops:
  0.6 7.4 %copy-start = (s32[16]{0:T(128)S(1)}, s32[16]{0:T(128)}, u32[]{:S(2)}) copy-start(s32[16]{0:T(128)} %param.13) | copy-start | bytes 196
  0.6 42.3 %copy-start.5 = (f32[2048]{0:T(1024)S(1)}, f32[2048]{0:T(1024)}, u32[]{:S(2)}) copy-start(f32[2048]{0:T(1024)} %param.10) | copy-start | bytes 24580
  10.1 133.2 %all-to-all-start = ((s32[16,1,1]{2,1,0:T(1,128)}), s32[16,1,1]{2,1,0:T(1,128)S(1)}, u32[]{:S(2)}, u32[]{:S(2)}) async-start(s32[16,1,1]{2,1,0:T(1,128)} %copy.93), calls=%async_computation | async-start | bytes 16384 | tf_op jit(solution)/shard_map/all_to_all | solution.py:105
  143.4 10.7 %all-to-all-start.2 = ((s32[16,1,1]{2,1,0:T(1,128)}), s32[16,1,1]{2,1,0:T(1,128)S(1)}, u32[]{:S(2)}, u32[]{:S(2)}) async-start(s32[16,1,1]{2,1,0:T(1,128)} %copy.100), calls=%async_computation.2 | async-start | bytes 16384 | tf_op jit(solution)/shard_map/all_to_all | solution.py:105
  154.0 9.4 %all-to-all-start.4 = ((s32[16,1,1]{2,1,0:T(1,128)}), s32[16,1,1]{2,1,0:T(1,128)S(1)}, u32[]{:S(2)}, u32[]{:S(2)}) async-start(s32[16,1,1]{2,1,0:T(1,128)} %copy.107), calls=%async_computation.4 | async-start | bytes 16384 | tf_op jit(solution)/shard_map/all_to_all | solution.py:105
  163.4 9.5 %all-to-all-start.6 = ((s32[16,1,1]{2,1,0:T(1,128)}), s32[16,1,1]{2,1,0:T(1,128)S(1)}, u32[]{:S(2)}, u32[]{:S(2)}) async-start(s32[16,1,1]{2,1,0:T(1,128)} %copy.114), calls=%async_computation.6 | async-start | bytes 16384 | tf_op jit(solution)/shard_map/all_to_all | solution.py:105
  173.0 10.0 %all-to-all-start.1 = ((f32[7,16,1,128]{3,2,0,1:T(1,128)}), f32[7,16,1,128]{3,2,0,1:T(1,128)S(1)}, u32[]{:S(2)}, u32[]{:S(2)}) async-start(f32[7,16,1,128]{3,2,0,1:T(1,128)} %copy.94), calls=%async_computation.1 | async-start | bytes 114688 | tf_op jit(solution)/shard_map/all_to_all | solution.py:108
  205.7 97.9 %all-to-all-start.3 = ((f32[7,16,1,128]{3,2,0,1:T(1,128)}), f32[7,16,1,128]{3,2,0,1:T(1,128)S(1)}, u32[]{:S(2)}, u32[]{:S(2)}) async-start(f32[7,16,1,128]{3,2,0,1:T(1,128)} %copy.101), calls=%async_computation.3 | async-start | bytes 114688 | tf_op jit(solution)/shard_map/all_to_all | solution.py:108
  329.8 94.1 %all-to-all-start.5 = ((f32[7,16,1,128]{3,2,0,1:T(1,128)}), f32[7,16,1,128]{3,2,0,1:T(1,128)S(1)}, u32[]{:S(2)}, u32[]{:S(2)}) async-start(f32[7,16,1,128]{3,2,0,1:T(1,128)} %copy.108), calls=%async_computation.5 | async-start | bytes 114688 | tf_op jit(solution)/shard_map/all_to_all | solution.py:108
  447.6 112.5 %all-to-all-start.7 = ((f32[7,16,1,128]{3,2,0,1:T(1,128)}), f32[7,16,1,128]{3,2,0,1:T(1,128)S(1)}, u32[]{:S(2)}, u32[]{:S(2)}) async-start(f32[7,16,1,128]{3,2,0,1:T(1,128)} %copy.115), calls=%async_computation.7 | async-start | bytes 114688 | tf_op jit(solution)/shard_map/all_to_all | solution.py:108
  561.9 7.9 %copy-start.1 = (s32[16]{0:T(128)S(1)}, s32[16]{0:T(128)}, u32[]{:S(2)}) copy-start(s32[16]{0:T(128)} %param.13) | copy-start | bytes 196
  567.5 1.6 copy-start.4
  568.2 0.9 copy-start.3
  569.1 0.6 copy-start.2
where the time goes:
time: 578 us; the launch traced here: 570 us
  blocking collectives  366 us (63%)
  other arithmetic  97.7 us (17%)
  starting transfers between devices  44.8 us (8%)
  local copies, waits for them, and re-layouts  44.3 us (8%)
  waiting for transfers between devices  14.4 us (2%)
    psum x4, blocking collectives, body(): regular_total = lax.psum(regular_part, 'grp')  298 us
    all_gather x4, blocking collectives, body(): lax.all_gather(sources, 'blk', axis=1, tiled=True)  68.1 us
    reduce_sum x8, other arithmetic, pair_terms(): acceleration = jnp.sum(weight * offset, axis=-1)  37.3 us
    reduce_sum x8, other arithmetic, pair_terms(): distance = jnp.sum(offset * offset, axis=0) + soften  31 us
    all_to_all x4, starting transfers between devices, body(): lax.all_to_all(located, 'blk', split_axis=1, concat_axis=1, tiled=True)  23.5 us
    all_to_all x4, starting transfers between devices, body(): lax.all_to_all(request, 'blk', split_axis=0, concat_axis=0, tiled=True)  21.3 us
    mul x4, other arithmetic, pair_terms(): jerk_term = jnp.sum(weight * (motion - 3.0 * radial * offset), axis=-1)  13.7 us
  transfers between devices with their start and end apart: 8, of which 4 were waited for; matrix products, arithmetic and copies ran while one was open for 18% of the time, Pallas kernels for 0%

commit v1 on v0

v1 whole, which is shorter than its diff:
```python
import functools
import jax
import jax.numpy as jnp
from jax import lax
from jax.experimental import pallas as pl
from jax.experimental.pallas import tpu as pltpu
from jax.sharding import PartitionSpec as P

WIDE = 0.04
CLOSE = 0.0001
TICK = 0.125
NB = 16
BS = 128
W = NB * BS
F32 = jnp.float32
CAPS = (4, 6, 4, 8)
TOP = (0, 1, 0, 2)
SENT = (-1, 0, 1, 1)
SLOTS = (0, 4, 8, 8)

VMEM = pl.BlockSpec(memory_space=pltpu.VMEM)
SMEM = pl.BlockSpec(memory_space=pltpu.SMEM)


def pair(target, source, mass, soften, acc):
    r = [source[c] - target[c] for c in range(3)]
    w = [source[c] - target[c] for c in range(3, 6)]
    d = (r[0] * r[0] + soften) + r[1] * r[1] + r[2] * r[2]
    s = lax.rsqrt(d)
    s2 = s * s
    weight = (mass * s) * s2
    q = (r[0] * w[0] + r[1] * w[1] + r[2] * w[2]) * (s2 * 3.0)
    acc = list(acc)
    for c in range(3):
        acc[c] = acc[c] + weight * r[c]
        acc[3 + c] = acc[3 + c] + weight * (w[c] - q * r[c])
    return tuple(acc)


def pair_split(target, source, mass, acc):
    r = [source[c] - target[c] for c in range(3)]
    w = [source[c] - target[c] for c in range(3, 6)]
    dd = r[0] * r[0] + r[1] * r[1] + r[2] * r[2]
    rw = (r[0] * w[0] + r[1] * w[1] + r[2] * w[2]) * 3.0
    acc = list(acc)
    for soften, sign in ((CLOSE, 1.0), (WIDE, -1.0)):
        s = lax.rsqrt(dd + soften)
        s2 = s * s
        weight = (mass * s) * (s2 * sign)
        q = rw * s2
        for c in range(3):
            acc[c] = acc[c] + weight * r[c]
            acc[3 + c] = acc[3 + c] + weight * (w[c] - q * r[c])
    return tuple(acc)


def zeros():
    return tuple(jnp.zeros((8, 128), F32) for _ in range(6))


def fill_slots(lev, top, slots):
    for s in range(24):
        slots[0, s] = 0
        slots[1, s] = -1000
        slots[2, s] = 0
    count = jnp.int32(0)
    ones = [jnp.int32(0), jnp.int32(4)]
    for k in range(NB):
        level = lev[k]
        live = level <= top
        place = jnp.where(level == 0, ones[0], jnp.where(level == 1, ones[1], -1000))
        slots[0, count] = k
        slots[1, count] = jnp.where(live, place, -1000)
        slots[2, count] = jnp.where(live, level, 0)
        count = count + live.astype(jnp.int32)
        ones[0] = ones[0] + (level == 0).astype(jnp.int32)
        ones[1] = ones[1] + (level == 1).astype(jnp.int32)
    return count


def span_of(level):
    return jnp.where(level == 0, TICK, jnp.where(level == 1, 2 * TICK, 4 * TICK)).astype(F32)


XS, MS, VS, AS, JS = (0, 1, 2), 3, (4, 5, 6), (8, 9, 10), (12, 13, 14)


def columns(tile):
    return tuple(
        [tile[:, c : c + 1] for c in group] for group in (XS, VS, AS, JS)
    )


def forecast(x, v, a, j, t):
    t2 = t * t * 0.5
    t3 = t * t * t * (1.0 / 6.0)
    xp = [x[c] + v[c] * t + a[c] * t2 + j[c] * t3 for c in range(3)]
    vp = [v[c] + a[c] * t + j[c] * t2 for c in range(3)]
    return xp + vp


def fill_sources(table, predicted, t, sent):
    row = lax.broadcasted_iota(jnp.int32, (8, 128), 0)
    t2 = t * t * 0.5
    t3 = t * t * t / 6.0
    low = row < 3
    high = (row > 3) & (row < 7)
    zero = jnp.zeros((8, 128), F32)
    c1 = jnp.where(low, t, zero)
    c2 = jnp.where(low | high, t2, zero)
    c3 = jnp.where(low, t3, jnp.where(high, t, zero))

    def shard(b, _):
        for k in range(NB):
            at = pl.ds(k * BS, BS)
            first = table[b, 0:8, at]
            second = table[b, 8:16, at]
            other = pltpu.roll(first, 4, 0)
            value = first + c1 * other + c2 * second + c3 * pltpu.roll(second, 4, 0)
            value = jnp.where(row == 7, other, value)
            if sent >= 0:
                value = jnp.where((row == 3) & (other < sent + 0.5), 0.0, value)
            predicted[b, :, at] = value
        return 0

    lax.fori_loop(0, table.shape[0], shard, 0)


def fill_targets(state, slots, cap, targets):
    for s in range(cap):
        x, v, a, j = columns(state[slots[0, s]])
        t = span_of(slots[2, s])
        for c, value in enumerate(forecast(x, v, a, j, t)):
            targets[s, c] = jnp.broadcast_to(value, (8, 128))


def broad(row):
    return jnp.broadcast_to(row, (8, 128))


def table_tile(predicted, b, k):
    at = pl.ds(k * BS, BS)
    rows = [broad(predicted[b, r : r + 1, at]) for r in (0, 1, 2, 4, 5, 6)]
    return rows, broad(predicted[b, 3:4, at])


def sweep_table(predicted, targets, cap, regular):
    shards = predicted.shape[0]

    def two(p, _):
        goal = [[targets[2 * p + e, c] for c in range(6)] for e in range(2)]

        def shard(b, acc):
            for k in range(NB):
                rows, mass = table_tile(predicted, b, k)
                acc = tuple(pair(goal[e], rows, mass, WIDE, acc[e]) for e in range(2))
            return acc

        acc = lax.fori_loop(0, shards, shard, (zeros(), zeros()))
        for e in range(2):
            for c in range(6):
                regular[2 * p + e, c] = acc[e][c]
        return 0

    lax.fori_loop(0, cap // 2, two, 0)


def close_table(predicted, targets, slots, cap, own, levall, partner, sent, irregular):
    for s in range(cap):
        k = slots[0, s]
        q = partner[k] // NB
        goal = [targets[s, c] for c in range(6)]
        acc = zeros()
        for b, wanted in ((own, None), (q, q != own)):
            here = jnp.bool_(True) if wanted is None else wanted
            if sent >= 0:
                level = slots[2, s] if wanted is None else levall[q * NB + k]
                here = here & (level > sent)
            at = pl.ds(pl.multiple_of(k * BS, BS), BS)
            rows = [broad(predicted[b, r : r + 1, at]) for r in (0, 1, 2, 4, 5, 6)]
            mass = broad(predicted[b, 7:8, at]) * jnp.where(here, 1.0, 0.0).astype(F32)
            acc = pair_split(goal, rows, mass, acc)
        for c in range(6):
            irregular[s, c] = acc[c]


def fill_received(got, turned):
    senders, _, lanes = got.shape
    for t in range(lanes // 128):
        for half in range(senders // 128):
            part = got[pl.ds(half * 128, 128), 0, pl.ds(t * 128, 128)]
            turned[pl.ds(t * 16, 16), :, pl.ds(half * 128, 128)] = part.T.reshape(16, 8, 128)


def sweep_received(turned, mass, slots_in, targets, cap, regular):
    halves = turned.shape[2] // 128

    def two(p, _):
        goal = [[targets[2 * p + e, c] for c in range(6)] for e in range(2)]

        def slot(s, acc):
            for i in range(8):
                for half in range(halves):
                    at = pl.ds(half * 128, 128)
                    rows = [broad(turned[f * slots_in + s, i : i + 1, at]) for f in range(6)]
                    m = broad(mass[s, i : i + 1, at])
                    acc = tuple(pair(goal[e], rows, m, WIDE, acc[e]) for e in range(2))
            return acc

        start = tuple(tuple(regular[2 * p + e, c] for c in range(6)) for e in range(2))
        acc = lax.fori_loop(0, slots_in, slot, start)
        for e in range(2):
            for c in range(6):
                regular[2 * p + e, c] = acc[e][c]
        return 0

    lax.fori_loop(0, cap // 2, two, 0)


def close_received(turned, mass, slots_in, targets, slots, cap, own, levall, partner, sent, irregular):
    lane = lax.broadcasted_iota(jnp.int32, (8, 128), 1)
    row = lax.broadcasted_iota(jnp.int32, (8, 128), 0)
    keep = lane // 16 == row
    for s in range(cap):
        k = slots[0, s]
        q = partner[k] // NB
        goal = [targets[s, c] for c in range(6)]
        acc = tuple(irregular[s, c] for c in range(6))
        for b, wanted in ((own, None), (q, q != own)):
            if wanted is None:
                here = slots[2, s] <= sent
                place = slots[1, s]
            else:
                level = levall[q * NB + k]
                here = wanted & (level <= sent)
                place = jnp.where(level == 0, 0, 4)
                for e in range(NB):
                    same = (levall[q * NB + e] == level) & (e < k)
                    place = place + same.astype(jnp.int32)
            place = jnp.clip(jnp.where(here, place, 0), 0, slots_in - 1)
            at = pl.ds(pl.multiple_of((b // 8) * 128, 128), 128)
            shift = lax.rem(128 - lax.rem(b, 8) * 16, 128)

            def gather(tile):
                tile = pltpu.roll(pltpu.roll(tile, shift, 1), 0, 1, stride=16, stride_axis=0)
                return broad(jnp.sum(jnp.where(keep, tile, 0.0), axis=0, keepdims=True))

            rows = [gather(turned[f * slots_in + place, :, at]) for f in range(6)]
            m = gather(mass[place, :, at]) * jnp.where(here, 1.0, 0.0).astype(F32)
            acc = pair_split(goal, rows, m, acc)
        for c in range(6):
            irregular[s, c] = acc[c]


def place_tiles(parts, count, width):
    per = 128 // width
    tiles = [jnp.zeros((8, 128), F32) for _ in range(count // per)]
    lane = lax.broadcasted_iota(jnp.int32, (8, 128), 1)
    for f, slot, column in parts:
        t = f // per
        tiles[t] = jnp.where(lane == (f % per) * width + slot * 8, column, tiles[t])
    out = []
    for tile in tiles:
        tile = pltpu.roll(tile, 0, 1, stride=1, stride_axis=0)
        out.append(jnp.sum(tile, axis=0, keepdims=True))
    return out


def send(tiles, pay):
    for t, tile in enumerate(tiles):
        full = jnp.broadcast_to(tile[None], (pay.shape[0], 1, 128))
        pay[:, :, pl.ds(t * 128, 128)] = full


def finish(step, state, slots, count, cap, regular, irregular, pay, lev):
    lane = lax.broadcasted_iota(jnp.int32, (8, 128), 1)
    parts = []
    for s in range(cap):
        k = slots[0, s]
        level = slots[2, s]
        place = slots[1, s]
        t = span_of(level)
        tile = state[k]
        x, v, a, j = columns(tile)
        close = [jnp.sum(irregular[s, c], axis=1, keepdims=True) for c in range(6)]
        total = [jnp.sum(regular[s, c], axis=1, keepdims=True) + close[c] for c in range(6)]
        half = t * 0.5
        twelfth = t * t * (1.0 / 12.0)
        v1 = [v[c] + (a[c] + total[c]) * half + (j[c] - total[3 + c]) * twelfth for c in range(3)]
        x1 = [x[c] + (v[c] + v1[c]) * half + (a[c] - total[c]) * twelfth for c in range(3)]
        if step == 3:
            mark = jnp.where(s < count, s, -1000)
            for f, column in enumerate(x1 + v1 + total + close):
                parts.append((f, s, column))
            continue
        fresh = tile
        for at, column in zip(XS + VS + AS + JS, x1 + v1 + total):
            fresh = jnp.where(lane == at, column, fresh)

        @pl.when(s < count)
        def _(k=k, fresh=fresh):
            state[k] = fresh

        ahead = forecast(x1, v1, total[:3], total[3:], TICK)
        for f, column in enumerate(ahead):
            parts.append((f, place, column))
        if step == 0:
            parts.append((6, place, tile[:, MS : MS + 1]))
    if step == 0:
        seen = jnp.int32(0)
        for k in range(NB):
            one = lev[k] == 1
            parts.append((7, jnp.where(one, seen, -1000), state[k][:, MS : MS + 1]))
            seen = seen + one.astype(jnp.int32)
        send(place_tiles(parts, 8, 32), pay)
    elif step == 1:
        send(place_tiles(parts, 6, 64), pay)
    elif step == 2:
        seen = jnp.int32(4)
        for k in range(NB):
            one = lev[k] == 1
            mark = jnp.where(one, seen, -1000)
            x, v, a, j = columns(state[k])
            for f, column in enumerate(forecast(x, v, a, j, 2 * TICK)):
                parts.append((f, mark, column))
            seen = seen + one.astype(jnp.int32)
        send(place_tiles(parts, 6, 64), pay)
    else:
        send(place_tiles(parts, 18, 64), pay)


def pack_kernel(ps, fr, mass, lev, out):
    out[0:3, :] = ps[0:3, :]
    out[3:4, :] = mass[...]
    out[4:7, :] = ps[3:6, :]
    for k in range(NB):
        out[7:8, pl.ds(k * BS, BS)] = jnp.full((1, BS), lev[k].astype(F32))
    out[8:11, :] = fr[0:3, :]
    out[11:12, :] = jnp.zeros((1, W), F32)
    out[12:15, :] = fr[3:6, :]
    out[15:16, :] = jnp.zeros((1, W), F32)


def first_kernel(own, table, lev, partner, state, pay, predicted, targets, regular, irregular, turned, slots):
    me = own[0]
    col = own[1]
    count = fill_slots(lev, TOP[0], slots)
    for k in range(NB):
        turned[:, 0:16] = table[me, :, pl.ds(k * BS, BS)].T
        state[k] = jnp.zeros((8, 128), F32)
        state[k, :, 0:16] = turned[pl.ds(pl.multiple_of(col * 8, 8), 8), 0:16]
    fill_sources(table, predicted, TICK, -1)
    fill_targets(state, slots, CAPS[0], targets)
    sweep_table(predicted, targets, CAPS[0], regular)
    close_table(predicted, targets, slots, CAPS[0], me, None, partner, -1, irregular)
    finish(0, state, slots, count, CAPS[0], regular, irregular, pay, lev)


def ahead_kernel(step, own, table, lev, levall, partner, state, regular, irregular, predicted, targets, slots):
    fill_slots(lev, TOP[step], slots)
    fill_sources(table, predicted, (step + 1) * TICK, SENT[step])
    fill_targets(state, slots, CAPS[step], targets)
    sweep_table(predicted, targets, CAPS[step], regular)
    close_table(predicted, targets, slots, CAPS[step], own[0], levall, partner, SENT[step], irregular)


def after_kernel(step, own, got, lev, levall, partner, state_in, reg_in, irr_in, *rest):
    if step == 1:
        state, pay, masses, regular, irregular, targets, turned, slots = rest
    elif step == 2:
        masses, state, pay, regular, irregular, targets, turned, slots = rest
    else:
        masses, pay, regular, irregular, targets, turned, slots = rest
        state = state_in
    count = fill_slots(lev, TOP[step], slots)
    cap = CAPS[step]
    if step < 3:
        state[...] = state_in[...]
    regular[...] = reg_in[...]
    irregular[...] = irr_in[...]
    fill_received(got, turned)
    if step == 1:
        masses[0:4] = turned[24:28]
        masses[4:8] = turned[28:32]
    fill_targets(state, slots, cap, targets)
    sweep_received(turned, masses, SLOTS[step], targets, cap, regular)
    close_received(turned, masses, SLOTS[step], targets, slots, cap, own[0], levall, partner, SENT[step], irregular)
    finish(step, state, slots, count, cap, regular, irregular, pay, lev)


def last_kernel(got, ps, fr, irr, lev, kin, comb, close, slots):
    count = fill_slots(lev, TOP[3], slots)
    kin[...] = ps[...]
    comb[...] = fr[...]
    close[...] = irr[...]
    senders = got.shape[0]
    lane = lax.broadcasted_iota(jnp.int32, (senders, 128), 1)
    row = lax.broadcasted_iota(jnp.int32, (senders, 128), 0)
    keep = lane // 8 == row
    for t in range(9):
        tile = got[:, 0, pl.ds(t * 128, 128)]
        for e in range(2):
            f = 2 * t + e
            out = (kin, comb, close)[f // 6]
            for s in range(CAPS[3]):
                shift = (128 - (e * 64 + s * 8)) % 128
                moved = pltpu.roll(pltpu.roll(tile, shift, 1), 0, 1, stride=8, stride_axis=0)
                value = jnp.sum(jnp.where(keep, moved, 0.0), axis=0, keepdims=True)
                at = pl.ds(pl.multiple_of(slots[0, s] * BS, BS), BS)

                @pl.when(s < count)
                def _(out=out, f=f, at=at, value=value):
                    out[f % 6 : f % 6 + 1, at] = value


def body(phase_space, force_rates, irregular, stellar_masses, levels, active, partner):
    shards = lax.axis_size("blk")
    columns_ = lax.axis_size("grp")
    everyone = shards * columns_
    own = jnp.stack([lax.axis_index("blk"), lax.axis_index("grp")]).astype(jnp.int32)
    packed = pl.pallas_call(
        pack_kernel,
        out_shape=jax.ShapeDtypeStruct((16, W), F32),
        in_specs=[VMEM, VMEM, VMEM, SMEM],
        out_specs=VMEM,
        name="pack",
    )(phase_space, force_rates, stellar_masses[None, :], levels)
    table = lax.all_gather(packed, "blk", axis=0, tiled=False)
    levall = table[:, 7, ::BS].astype(jnp.int32).reshape(shards * NB)

    def exchange(pay, axis):
        return lax.all_to_all(pay, axis, split_axis=0, concat_axis=0, tiled=True)

    sums = lambda cap: pltpu.VMEM((cap, 6, 8, 128), F32)
    slots = pltpu.SMEM((3, 24), jnp.int32)
    state_shape = jax.ShapeDtypeStruct((NB, 8, 128), F32)
    predicted = pltpu.VMEM((shards, 8, W), F32)
    state, pay = pl.pallas_call(
        first_kernel,
        out_shape=(state_shape, jax.ShapeDtypeStruct((everyone, 1, 256), F32)),
        in_specs=[SMEM, VMEM, SMEM, SMEM],
        out_specs=(VMEM, VMEM),
        scratch_shapes=[
            predicted, sums(4), sums(4), sums(4), pltpu.VMEM((128, 128), F32), slots,
        ],
        name="first",
    )(own, table, levels, partner)
    masses = None
    for step in (1, 2, 3):
        cap = CAPS[step]
        lanes = (0, 256, 384, 384)[step]
        got = exchange(pay, ("blk", "grp"))
        sum_shape = jax.ShapeDtypeStruct((cap, 6, 8, 128), F32)
        reg, irr = pl.pallas_call(
            functools.partial(ahead_kernel, step),
            out_shape=(sum_shape, sum_shape),
            in_specs=[SMEM, VMEM, SMEM, SMEM, SMEM, VMEM],
            out_specs=(VMEM, VMEM),
            scratch_shapes=[predicted, sums(cap), slots],
            name=f"ahead{step}",
        )(own, table, levels, levall, partner, state)
        mass_shape = jax.ShapeDtypeStruct((8, 8, everyone), F32)
        wide = (0, 384, 384, 1152)[step]
        pay_shape = jax.ShapeDtypeStruct((everyone if step < 3 else columns_, 1, wide), F32)
        out_shape = {1: (state_shape, pay_shape, mass_shape), 2: (state_shape, pay_shape), 3: (pay_shape,)}[step]
        ins = (own, got, levels, levall, partner, state, reg, irr) + (() if step == 1 else (masses,))
        outs = pl.pallas_call(
            functools.partial(after_kernel, step),
            out_shape=out_shape,
            in_specs=[SMEM, VMEM, SMEM, SMEM, SMEM] + [VMEM] * (len(ins) - 5),
            out_specs=tuple(VMEM for _ in out_shape),
            scratch_shapes=[
                sums(cap), sums(cap), sums(cap), pltpu.VMEM((lanes // 8, 8, everyone), F32), slots,
            ],
            name=f"after{step}",
        )(*ins)
        if step == 1:
            state, pay, masses = outs
        elif step == 2:
            state, pay = outs
        else:
            (pay,) = outs
    got = exchange(pay, "grp")
    shape = jax.ShapeDtypeStruct((6, W), F32)
    return tuple(
        pl.pallas_call(
            last_kernel,
            out_shape=(shape, shape, shape),
            in_specs=[VMEM, VMEM, VMEM, VMEM, SMEM],
            out_specs=(VMEM, VMEM, VMEM),
            scratch_shapes=[slots],
            name="last",
        )(got, phase_space, force_rates, irregular, levels)
    )


def solution(mesh):
    in_specs = (
        P(None, "blk"), P(None, "blk"), P(None, "blk"), P("blk"), P("blk"), P(None, "blk"), P("blk"),
    )
    out_specs = (P(None, "blk"), P(None, "blk"), P(None, "blk"))
    return jax.shard_map(body, mesh=mesh, in_specs=in_specs, out_specs=out_specs, check_vma=False)
```

time: 578 us -> 217 us (0.38)
  the two profiles are of different devices: /device:TPU:2 before, /device:TPU:1 now
where the time goes in v1:
time: 217 us; the launch traced here: 216 us
  Pallas kernels  95.5 us (44%)
  waiting for transfers between devices  55.4 us (26%)
  starting transfers between devices  29.7 us (14%)
  blocking collectives  16.3 us (8%)
  between operations  14.1 us (6%)
  local copies, waits for them, and re-layouts  4.2 us (2%)
    all_gather x1, waiting for transfers between devices, body(): table = lax.all_gather(packed, 'blk', axis=0, tiled=False)  40.8 us
    pallas_call x3, Pallas kernels, body(): pl.pallas_call(functools.partial(ahead_kernel, step), out_shape=(sum_shap...  35.8 us
    all_to_all x3, starting transfers between devices, exchange(): return lax.all_to_all(pay, axis, split_axis=0, concat_axis=0, tiled=True)  29.7 us
    pallas_call x3, Pallas kernels, body(): pl.pallas_call(functools.partial(after_kernel, step), out_shape=out_shape...  25.3 us
    pallas_call x1, Pallas kernels, body(): pl.pallas_call(last_kernel, out_shape=(shape, shape, shape), in_specs=[VM...  22.1 us
    all_to_all x1, blocking collectives, exchange(): return lax.all_to_all(pay, axis, split_axis=0, concat_axis=0, tiled=True)  16.3 us
    all_to_all x3, waiting for transfers between devices, exchange(): return lax.all_to_all(pay, axis, split_axis=0, concat_axis=0, tiled=True)  14.6 us
    pallas_call x1, Pallas kernels, body(): pl.pallas_call(first_kernel, out_shape=(state_shape, jax.ShapeDtypeStruct...  10.7 us
  transfers between devices with their start and end apart: 4, of which 4 were waited for; matrix products, arithmetic and copies ran while one was open for 1% of the time, Pallas kernels for 17%

profile of v1, /device:TPU:1, one launch (start us, length us, event | category | flops | bytes accessed | tf_op | source)
XLA Modules:
  0.0 215.8 jit_solution(15695186845442333119)
XLA Ops:
  7.2 0.0 all-gather.3.cloned.1.call-start
  7.2 1.6 pack.1
  8.8 0.0 all-gather.3.cloned.1.call-update
  8.8 0.6 pad_add_fusion.own
  9.4 40.8 %all-gather.3.cloned.1.call-done = f32[256,2048]{1,0:T(8,128)} async-done(((f32[16,2048]{1,0:T(8,128)}), f32[256,2048]{1,0:T(8,128)}) %all-gather.3.cloned.1.call-update) | async-done | bytes 2097168 | tf_op jit(solution)/shard_map/all_gather | solution.py:428
  50.2 10.7 %first.1 = (f32[16,8,128]{2,1,0:T(8,128)}, f32[256,1,256]{2,1,0:T(1,128)}) custom-call(s32[2]{0:T(128)} %pad_add_fusion.own, f32[16,16,2048]{2,1,0:T(8,128)} %bitcast.4, s32[16]{0:T(128)} %lev.17, s32[16]{0:T(128)} %partner.13), custom_call_target="tpu_custom_call" | custom-call | tf_op jit(solution)/shard_map/first/pallas_call | solution.py:438
  61.0 11.7 %all-to-all-start = ((f32[256,1,256]{2,1,0:T(1,128)}), f32[256,1,256]{2,1,0:T(1,128)S(1)}, u32[]{:S(2)}, u32[]{:S(2)}) async-start(f32[256,1,256]{2,1,0:T(1,128)} %get-tuple-element.16), calls=%async_computation | async-start | bytes 524288 | tf_op jit(solution)/shard_map/all_to_all | solution.py:432
  72.6 1.3 slice.3
  74.0 0.7 convert_element_type.8.levall
  74.7 11.9 %ahead1.1 = (f32[6,6,8,128]{3,2,1,0:T(8,128)}, f32[6,6,8,128]{3,2,1,0:T(8,128)}) custom-call(s32[2]{0:T(128)} %pad_add_fusion.own, f32[16,16,2048]{2,1,0:T(8,128)} %bitcast.6, s32[16]{0:T(128)} %lev.17, s32[256]{0:T(256)} %convert_element_type.8.levall, s32[16]{0:T(128)} %partner.13, f32[16,8,128]{2,1,0:T(8,128)} %get-tuple-element.17.state.state_in), custom_call_target="tpu_custom_call" | custom-call | tf_op jit(solution)/shard_map/ahead1/pallas_call | solution.py:454
  86.6 1.6 all-to-all-done.got
  88.2 0.0 copy-start.2
  88.2 0.7 copy-done.2
  88.9 7.4 %after1.1 = (f32[16,8,128]{2,1,0:T(8,128)}, f32[256,1,384]{2,1,0:T(1,128)}, f32[8,8,256]{2,1,0:T(8,128)}) custom-call(s32[2]{0:T(128)} %pad_add_fusion.own, f32[256,1,256]{2,1,0:T(1,128)} %copy-done.2, s32[16]{0:T(128)} %lev.17, s32[256]{0:T(256)} %convert_element_type.8.levall, s32[16]{0:T(128)} %partner.13, ...), custom_call_target="tpu_custom_call" | custom-call | tf_op jit(solution)/shard_map/after1/pallas_call | solution.py:467
  96.3 12.1 %all-to-all-start.1 = ((f32[256,1,384]{2,1,0:T(1,128)}), f32[256,1,384]{2,1,0:T(1,128)S(1)}, u32[]{:S(2)}, u32[]{:S(2)}) async-start(f32[256,1,384]{2,1,0:T(1,128)} %get-tuple-element.20), calls=%async_computation.1 | async-start | bytes 786432 | tf_op jit(solution)/shard_map/all_to_all | solution.py:432
  108.4 9.0 %ahead2.1 = (f32[4,6,8,128]{3,2,1,0:T(8,128)}, f32[4,6,8,128]{3,2,1,0:T(8,128)}) custom-call(s32[2]{0:T(128)} %pad_add_fusion.own, f32[16,16,2048]{2,1,0:T(8,128)} %bitcast.7, s32[16]{0:T(128)} %lev.17, s32[256]{0:T(256)} %convert_element_type.8.levall, s32[16]{0:T(128)} %partner.13, f32[16,8,128]{2,1,0:T(8,128)} %get-tuple-element.21.state.state_in), custom_call_target="tpu_custom_call" | custom-call | tf_op jit(solution)/shard_map/ahead2/pallas_call | solution.py:454
  117.4 9.4 %all-to-all-done.1.got = f32[256,1,384]{2,1,0:T(1,128)S(1)} async-done(((f32[256,1,384]{2,1,0:T(1,128)}), f32[256,1,384]{2,1,0:T(1,128)S(1)}, u32[]{:S(2)}, u32[]{:S(2)}) %all-to-all-start.1) | async-done | bytes 393248 | tf_op jit(solution)/shard_map/all_to_all | solution.py:432
  126.8 0.0 copy-start.1
  126.8 0.8 copy-done.1
  127.5 7.4 %after2.1 = (f32[16,8,128]{2,1,0:T(8,128)}, f32[256,1,384]{2,1,0:T(1,128)}) custom-call(s32[2]{0:T(128)} %pad_add_fusion.own, f32[256,1,384]{2,1,0:T(1,128)} %copy-done.1, s32[16]{0:T(128)} %lev.17, s32[256]{0:T(256)} %convert_element_type.8.levall, s32[16]{0:T(128)} %partner.13, f32[16,8,128]{2,1,0:T(8,128)} %get-tuple-element.21.state.state_in, ...), custom_call_target="tpu_custom_call" | custom-call | tf_op jit(solution)/shard_map/after2/pallas_call | solution.py:467
  135.0 5.9 %all-to-all-start.2 = ((f32[256,1,384]{2,1,0:T(1,128)}), f32[256,1,384]{2,1,0:T(1,128)S(1)}, u32[]{:S(2)}, u32[]{:S(2)}) async-start(f32[256,1,384]{2,1,0:T(1,128)} %get-tuple-element.25), calls=%async_computation.2 | async-start | bytes 786432 | tf_op jit(solution)/shard_map/all_to_all | solution.py:432
  140.9 14.9 %ahead3.1 = (f32[8,6,8,128]{3,2,1,0:T(8,128)}, f32[8,6,8,128]{3,2,1,0:T(8,128)}) custom-call(s32[2]{0:T(128)} %pad_add_fusion.own, f32[16,16,2048]{2,1,0:T(8,128)} %bitcast.8, s32[16]{0:T(128)} %lev.17, s32[256]{0:T(256)} %convert_element_type.8.levall, s32[16]{0:T(128)} %partner.13, f32[16,8,128]{2,1,0:T(8,128)} %get-tuple-element.26.state.state_in), custom_call_target="tpu_custom_call" | custom-call | tf_op jit(solution)/shard_map/ahead3/pallas_call | solution.py:454
  155.8 3.6 %all-to-all-done.2.got = f32[256,1,384]{2,1,0:T(1,128)S(1)} async-done(((f32[256,1,384]{2,1,0:T(1,128)}), f32[256,1,384]{2,1,0:T(1,128)S(1)}, u32[]{:S(2)}, u32[]{:S(2)}) %all-to-all-start.2) | async-done | bytes 393248 | tf_op jit(solution)/shard_map/all_to_all | solution.py:432
  159.4 0.0 copy-start
  159.4 0.7 copy-done
  160.1 10.5 %after3.1 = f32[16,1,1152]{2,1,0:T(1,128)} custom-call(s32[2]{0:T(128)} %pad_add_fusion.own, f32[256,1,384]{2,1,0:T(1,128)} %copy-done, s32[16]{0:T(128)} %lev.17, s32[256]{0:T(256)} %convert_element_type.8.levall, s32[16]{0:T(128)} %partner.13, f32[16,8,128]{2,1,0:T(8,128)} %get-tuple-element.26.state.state_in, f32[8,6,8,128]{3,2,1,0:T(8,128)} %get-tuple-element.27.reg_in, ...), custom_call_target="tpu_custom_call" | custom-call | tf_op jit(solution)/shard_map/after3/pallas_call | solution.py:467
  170.6 16.3 %all_to_all.20.got = f32[16,1,1152]{2,1,0:T(1,128)} all-to-all(f32[16,1,1152]{2,1,0:T(1,128)} %after3.1), channel_id=1, replica_groups=mesh['blk'=16,'grp'=16] {'grp'}, dimensions={0} | all-to-all | bytes 147456 | tf_op jit(solution)/shard_map/all_to_all | solution.py:432
  186.9 22.1 %last.1 = (f32[6,2048]{1,0:T(8,128)}, f32[6,2048]{1,0:T(8,128)}, f32[6,2048]{1,0:T(8,128)}) custom-call(f32[16,1,1152]{2,1,0:T(1,128)} %all_to_all.20.got, f32[6,2048]{1,0:T(8,128)} %ps.3, f32[6,2048]{1,0:T(8,128)} %fr.3, f32[6,2048]{1,0:T(8,128)} %irr.1, s32[16]{0:T(128)} %lev.17), custom_call_target="tpu_custom_call" | custom-call | tf_op jit(solution)/shard_map/last/pallas_call | solution.py:486
  (1 shorter events, 0.0 us)
Async XLA Ops:
  7.2 43.1 %all-gather.3.cloned.1.call-start = ((), (), s32[]{:S(2)}) async-start(), calls=%async_computation.4 | async-start | bytes 2228224 | tf_op jit(solution)/shard_map/all_gather | solution.py:428
  61.0 27.2 %all-to-all-start = ((f32[256,1,256]{2,1,0:T(1,128)}), f32[256,1,256]{2,1,0:T(1,128)S(1)}, u32[]{:S(2)}, u32[]{:S(2)}) async-start(f32[256,1,256]{2,1,0:T(1,128)} %get-tuple-element.16), calls=%async_computation | async-start | bytes 524288 | tf_op jit(solution)/shard_map/all_to_all | solution.py:432
  88.2 0.7 copy-start.2
  96.3 30.5 %all-to-all-start.1 = ((f32[256,1,384]{2,1,0:T(1,128)}), f32[256,1,384]{2,1,0:T(1,128)S(1)}, u32[]{:S(2)}, u32[]{:S(2)}) async-start(f32[256,1,384]{2,1,0:T(1,128)} %get-tuple-element.20), calls=%async_computation.1 | async-start | bytes 786432 | tf_op jit(solution)/shard_map/all_to_all | solution.py:432
  126.8 0.8 copy-start.1
  135.0 24.4 %all-to-all-start.2 = ((f32[256,1,384]{2,1,0:T(1,128)}), f32[256,1,384]{2,1,0:T(1,128)S(1)}, u32[]{:S(2)}, u32[]{:S(2)}) async-start(f32[256,1,384]{2,1,0:T(1,128)} %get-tuple-element.25), calls=%async_computation.2 | async-start | bytes 786432 | tf_op jit(solution)/shard_map/all_to_all | solution.py:432
  159.4 0.7 copy-start
Sparse Core Ops, SparseCore 0:
  9.8 40.3 all-gather.2

commit v2 on v1

--- a/solution.py
+++ b/solution.py
@@ -82,7 +82,7 @@
     return jnp.where(level == 0, TICK, jnp.where(level == 1, 2 * TICK, 4 * TICK)).astype(F32)
 
 
-XS, MS, VS, AS, JS = (0, 1, 2), 3, (4, 5, 6), (8, 9, 10), (12, 13, 14)
+XS, MS, VS, AS, JS = (0, 1, 2), 3, (4, 5, 6), (8, 9, 10), (11, 12, 13)
 
 
 def columns(tile):
@@ -99,31 +99,51 @@
     return xp + vp
 
 
-def fill_sources(table, predicted, t, sent):
-    row = lax.broadcasted_iota(jnp.int32, (8, 128), 0)
-    t2 = t * t * 0.5
-    t3 = t * t * t / 6.0
-    low = row < 3
-    high = (row > 3) & (row < 7)
-    zero = jnp.zeros((8, 128), F32)
-    c1 = jnp.where(low, t, zero)
-    c2 = jnp.where(low | high, t2, zero)
-    c3 = jnp.where(low, t3, jnp.where(high, t, zero))
-
-    def shard(b, _):
+ROWS = 14 * NB
+RATES = 8 * (NB // 2)
+
+
+def first_row(k):
+    return k * 8 + (6 * NB if k >= NB // 2 else 0)
+
+
+class Forecast:
+    def __init__(self, t):
+        row = lax.broadcasted_iota(jnp.int32, (8, 128), 0)
+        zero = jnp.zeros((8, 128), F32)
+        low = row < 3
+        high = (row > 3) & (row < 7)
+        self.low = lambda value: jnp.where(low, value, zero)
+        self.high = lambda value: jnp.where(high, value, zero)
+        t2 = t * t * 0.5
+        t3 = t * t * t / 6.0
+        self.c = (self.low(t), self.low(t2), self.low(t3), self.high(t), self.high(t2))
+
+    def __call__(self, table, b, at, rates):
+        first = table[b, at, :]
+        second = [table[b, pl.ds(rates + o, 8), :] for o in (0, 3, -4, -1)]
+        value = first + self.c[0] * pltpu.roll(first, 4, 0)
+        for c, part in zip(self.c[1:], second):
+            value = value + c * part
+        return value
+
+
+def fill_sources(table, predicted, ahead, levall, sent):
+    def shard(b, count):
         for k in range(NB):
-            at = pl.ds(k * BS, BS)
-            first = table[b, 0:8, at]
-            second = table[b, 8:16, at]
-            other = pltpu.roll(first, 4, 0)
-            value = first + c1 * other + c2 * second + c3 * pltpu.roll(second, 4, 0)
-            value = jnp.where(row == 7, other, value)
+            tile = ahead(table, b, pl.ds(first_row(k), 8), RATES + 6 * k)
+            predicted[count] = tile
             if sent >= 0:
-                value = jnp.where((row == 3) & (other < sent + 0.5), 0.0, value)
-            predicted[b, :, at] = value
-        return 0
-
-    lax.fori_loop(0, table.shape[0], shard, 0)
+                count = count + (levall[b * NB + k] > sent).astype(jnp.int32)
+            else:
+                count = count + 1
+        return count
+
+    count = lax.fori_loop(0, table.shape[0], shard, jnp.int32(0))
+    if sent >= 0:
+        for e in range(NB):
+            predicted[count + e] = jnp.zeros((8, 128), F32)
+    return count
 
 
 def fill_targets(state, slots, cap, targets):
@@ -138,25 +158,22 @@
     return jnp.broadcast_to(row, (8, 128))
 
 
-def table_tile(predicted, b, k):
-    at = pl.ds(k * BS, BS)
-    rows = [broad(predicted[b, r : r + 1, at]) for r in (0, 1, 2, 4, 5, 6)]
-    return rows, broad(predicted[b, 3:4, at])
-
-
-def sweep_table(predicted, targets, cap, regular):
-    shards = predicted.shape[0]
-
+def tile_rows(tiles, at):
+    rows = [broad(tiles[at, r : r + 1, :]) for r in (0, 1, 2, 4, 5, 6)]
+    return rows, broad(tiles[at, 3:4, :])
+
+
+def sweep_table(predicted, count, targets, cap, regular):
     def two(p, _):
         goal = [[targets[2 * p + e, c] for c in range(6)] for e in range(2)]
 
-        def shard(b, acc):
+        def group(b, acc):
             for k in range(NB):
-                rows, mass = table_tile(predicted, b, k)
+                rows, mass = tile_rows(predicted, b * NB + k)
                 acc = tuple(pair(goal[e], rows, mass, WIDE, acc[e]) for e in range(2))
             return acc
 
-        acc = lax.fori_loop(0, shards, shard, (zeros(), zeros()))
+        acc = lax.fori_loop(0, (count + NB - 1) // NB, group, (zeros(), zeros()))
         for e in range(2):
             for c in range(6):
                 regular[2 * p + e, c] = acc[e][c]
@@ -165,23 +182,36 @@
     lax.fori_loop(0, cap // 2, two, 0)
 
 
-def close_table(predicted, targets, slots, cap, own, levall, partner, sent, irregular):
+def close_table(table, ahead, near, targets, slots, cap, own, levall, partner, sent, irregular):
+    for s in range(cap):
+        k = slots[0, s]
+        at = pl.ds(pl.multiple_of(k * 8 + jnp.where(k >= NB // 2, 6 * NB, 0), 8), 8)
+        for e, b in enumerate((own, partner[k] // NB)):
+            near[2 * s + e] = ahead(table, b, at, RATES + 6 * k)
     for s in range(cap):
         k = slots[0, s]
         q = partner[k] // NB
         goal = [targets[s, c] for c in range(6)]
         acc = zeros()
-        for b, wanted in ((own, None), (q, q != own)):
+        for e, wanted in enumerate((None, q != own)):
             here = jnp.bool_(True) if wanted is None else wanted
             if sent >= 0:
                 level = slots[2, s] if wanted is None else levall[q * NB + k]
                 here = here & (level > sent)
-            at = pl.ds(pl.multiple_of(k * BS, BS), BS)
-            rows = [broad(predicted[b, r : r + 1, at]) for r in (0, 1, 2, 4, 5, 6)]
-            mass = broad(predicted[b, 7:8, at]) * jnp.where(here, 1.0, 0.0).astype(F32)
-            acc = pair_split(goal, rows, mass, acc)
+            rows, mass = tile_rows(near, 2 * s + e)
+            acc = pair_split(goal, rows, mass * jnp.where(here, 1.0, 0.0).astype(F32), acc)
         for c in range(6):
             irregular[s, c] = acc[c]
+
+
+def sum_up(regular, irregular, cap, sums):
+    lane = lax.broadcasted_iota(jnp.int32, (8, 128), 1)
+    for s in range(cap):
+        tile = jnp.zeros((8, 128), F32)
+        for at, part in ((0, regular), (8, irregular)):
+            for c in range(6):
+                tile = jnp.where(lane == at + c, jnp.sum(part[s, c], axis=1, keepdims=True), tile)
+        sums[s] = tile
 
 
 def fill_received(got, turned):
@@ -192,7 +222,7 @@
             turned[pl.ds(t * 16, 16), :, pl.ds(half * 128, 128)] = part.T.reshape(16, 8, 128)
 
 
-def sweep_received(turned, mass, slots_in, targets, cap, regular):
+def sweep_received(turned, mass, slots_in, used, targets, cap, regular):
     halves = turned.shape[2] // 128
 
     def two(p, _):
@@ -207,8 +237,7 @@
                     acc = tuple(pair(goal[e], rows, m, WIDE, acc[e]) for e in range(2))
             return acc
 
-        start = tuple(tuple(regular[2 * p + e, c] for c in range(6)) for e in range(2))
-        acc = lax.fori_loop(0, slots_in, slot, start)
+        acc = lax.fori_loop(0, used, slot, (zeros(), zeros()))
         for e in range(2):
             for c in range(6):
                 regular[2 * p + e, c] = acc[e][c]
@@ -225,7 +254,7 @@
         k = slots[0, s]
         q = partner[k] // NB
         goal = [targets[s, c] for c in range(6)]
-        acc = tuple(irregular[s, c] for c in range(6))
+        acc = zeros()
         for b, wanted in ((own, None), (q, q != own)):
             if wanted is None:
                 here = slots[2, s] <= sent
@@ -272,7 +301,7 @@
         pay[:, :, pl.ds(t * 128, 128)] = full
 
 
-def finish(step, state, slots, count, cap, regular, irregular, pay, lev):
+def finish(step, state, slots, count, cap, regular, irregular, sums, pay, lev):
     lane = lax.broadcasted_iota(jnp.int32, (8, 128), 1)
     parts = []
     for s in range(cap):
@@ -283,7 +312,12 @@
         tile = state[k]
         x, v, a, j = columns(tile)
         close = [jnp.sum(irregular[s, c], axis=1, keepdims=True) for c in range(6)]
-        total = [jnp.sum(regular[s, c], axis=1, keepdims=True) + close[c] for c in range(6)]
+        total = [jnp.sum(regular[s, c], axis=1, keepdims=True) for c in range(6)]
+        if sums is not None:
+            before = sums[s]
+            close = [close[c] + before[:, 8 + c : 9 + c] for c in range(6)]
+            total = [total[c] + before[:, c : c + 1] for c in range(6)]
+        total = [total[c] + close[c] for c in range(6)]
         half = t * 0.5
         twelfth = t * t * (1.0 / 12.0)
         v1 = [v[c] + (a[c] + total[c]) * half + (j[c] - total[3 + c]) * twelfth for c in range(3)]
@@ -330,62 +364,85 @@
 
 
 def pack_kernel(ps, fr, mass, lev, out):
-    out[0:3, :] = ps[0:3, :]
-    out[3:4, :] = mass[...]
-    out[4:7, :] = ps[3:6, :]
+    lane = lax.broadcasted_iota(jnp.int32, (1, BS), 1)
+    levels = jnp.zeros((1, BS), F32)
     for k in range(NB):
-        out[7:8, pl.ds(k * BS, BS)] = jnp.full((1, BS), lev[k].astype(F32))
-    out[8:11, :] = fr[0:3, :]
-    out[11:12, :] = jnp.zeros((1, W), F32)
-    out[12:15, :] = fr[3:6, :]
-    out[15:16, :] = jnp.zeros((1, W), F32)
-
-
-def first_kernel(own, table, lev, partner, state, pay, predicted, targets, regular, irregular, turned, slots):
+        levels = jnp.where(lane == k, lev[k].astype(F32), levels)
+    for k in range(NB):
+        at = pl.ds(k * BS, BS)
+        first = first_row(k)
+        out[first : first + 3, :] = ps[0:3, at]
+        out[first + 3 : first + 4, :] = mass[:, at]
+        out[first + 4 : first + 7, :] = ps[3:6, at]
+        out[first + 7 : first + 8, :] = levels
+        out[RATES + 6 * k : RATES + 6 * k + 6, :] = fr[:, at]
+
+
+def first_kernel(own, table, lev, partner, state, pay, predicted, near, targets, regular, irregular, turned, slots):
     me = own[0]
-    col = own[1]
+    col = pl.multiple_of(own[1] * 8, 8)
     count = fill_slots(lev, TOP[0], slots)
     for k in range(NB):
-        turned[:, 0:16] = table[me, :, pl.ds(k * BS, BS)].T
-        state[k] = jnp.zeros((8, 128), F32)
-        state[k, :, 0:16] = turned[pl.ds(pl.multiple_of(col * 8, 8), 8), 0:16]
-    fill_sources(table, predicted, TICK, -1)
+        turned[k, :, 0:8] = table[me, pl.ds(first_row(k), 8), :].T
+        turned[k, :, 8:16] = table[me, pl.ds(RATES + 6 * k, 8), :].T
+    for k in range(NB):
+        state[k] = turned[k, pl.ds(col, 8), :]
+    ahead = Forecast(TICK)
+    used = fill_sources(table, predicted, ahead, None, -1)
     fill_targets(state, slots, CAPS[0], targets)
-    sweep_table(predicted, targets, CAPS[0], regular)
-    close_table(predicted, targets, slots, CAPS[0], me, None, partner, -1, irregular)
-    finish(0, state, slots, count, CAPS[0], regular, irregular, pay, lev)
-
-
-def ahead_kernel(step, own, table, lev, levall, partner, state, regular, irregular, predicted, targets, slots):
+    sweep_table(predicted, used, targets, CAPS[0], regular)
+    close_table(table, ahead, near, targets, slots, CAPS[0], me, None, partner, -1, irregular)
+    finish(0, state, slots, count, CAPS[0], regular, irregular, None, pay, lev)
+
+
+def ahead_kernel(step, own, table, lev, levall, partner, state, sums, *rest):
+    if step == 1:
+        ones, predicted, near, targets, regular, irregular, slots = rest
+    else:
+        predicted, near, targets, regular, irregular, slots = rest
+    cap = CAPS[step]
     fill_slots(lev, TOP[step], slots)
-    fill_sources(table, predicted, (step + 1) * TICK, SENT[step])
-    fill_targets(state, slots, CAPS[step], targets)
-    sweep_table(predicted, targets, CAPS[step], regular)
-    close_table(predicted, targets, slots, CAPS[step], own[0], levall, partner, SENT[step], irregular)
-
-
-def after_kernel(step, own, got, lev, levall, partner, state_in, reg_in, irr_in, *rest):
+    ahead = Forecast((step + 1) * TICK)
+    used = fill_sources(table, predicted, ahead, levall, SENT[step])
+    fill_targets(state, slots, cap, targets)
+    sweep_table(predicted, used, targets, cap, regular)
+    close_table(table, ahead, near, targets, slots, cap, own[0], levall, partner, SENT[step], irregular)
+    sum_up(regular, irregular, cap, sums)
+    if step == 1:
+
+        def shard(b, most):
+            here = jnp.int32(0)
+            for k in range(NB):
+                here = here + (levall[b * NB + k] == 1).astype(jnp.int32)
+            return jnp.maximum(most, here)
+
+        ones[0] = lax.fori_loop(0, table.shape[0], shard, jnp.int32(0))
+
+
+def after_kernel(step, own, got, lev, levall, partner, state_in, sums, *rest):
     if step == 1:
         state, pay, masses, regular, irregular, targets, turned, slots = rest
-    elif step == 2:
-        masses, state, pay, regular, irregular, targets, turned, slots = rest
+        used = SLOTS[step]
     else:
-        masses, pay, regular, irregular, targets, turned, slots = rest
-        state = state_in
+        masses, ones, *rest = rest
+        used = jnp.minimum(4 + ones[0], SLOTS[step])
+        if step == 2:
+            state, pay, regular, irregular, targets, turned, slots = rest
+        else:
+            pay, regular, irregular, targets, turned, slots = rest
+            state = state_in
     count = fill_slots(lev, TOP[step], slots)
     cap = CAPS[step]
     if step < 3:
         state[...] = state_in[...]
-    regular[...] = reg_in[...]
-    irregular[...] = irr_in[...]
     fill_received(got, turned)
     if step == 1:
         masses[0:4] = turned[24:28]
         masses[4:8] = turned[28:32]
     fill_targets(state, slots, cap, targets)
-    sweep_received(turned, masses, SLOTS[step], targets, cap, regular)
+    sweep_received(turned, masses, SLOTS[step], used, targets, cap, regular)
     close_received(turned, masses, SLOTS[step], targets, slots, cap, own[0], levall, partner, SENT[step], irregular)
-    finish(step, state, slots, count, cap, regular, irregular, pay, lev)
+    finish(step, state, slots, count, cap, regular, irregular, sums, pay, lev)
 
 
 def last_kernel(got, ps, fr, irr, lev, kin, comb, close, slots):
@@ -396,21 +453,22 @@
     senders = got.shape[0]
     lane = lax.broadcasted_iota(jnp.int32, (senders, 128), 1)
     row = lax.broadcasted_iota(jnp.int32, (senders, 128), 0)
-    keep = lane // 8 == row
-    for t in range(9):
-        tile = got[:, 0, pl.ds(t * 128, 128)]
-        for e in range(2):
-            f = 2 * t + e
-            out = (kin, comb, close)[f // 6]
-            for s in range(CAPS[3]):
-                shift = (128 - (e * 64 + s * 8)) % 128
-                moved = pltpu.roll(pltpu.roll(tile, shift, 1), 0, 1, stride=8, stride_axis=0)
-                value = jnp.sum(jnp.where(keep, moved, 0.0), axis=0, keepdims=True)
-                at = pl.ds(pl.multiple_of(slots[0, s] * BS, BS), BS)
-
-                @pl.when(s < count)
-                def _(out=out, f=f, at=at, value=value):
-                    out[f % 6 : f % 6 + 1, at] = value
+    spread = [pltpu.roll(got[:, 0, pl.ds(t * 128, 128)], 0, 1, stride=8, stride_axis=0) for t in range(9)]
+    for s in range(CAPS[3]):
+        rows = []
+        for f in range(18):
+            t, e = divmod(f, 2)
+            start = e * 64 + s * 8
+            keep = (lane + (128 - start)) % 128 // 8 == row
+            value = jnp.sum(jnp.where(keep, spread[t], 0.0), axis=0, keepdims=True)
+            rows.append(pltpu.roll(value, (128 - start) % 128, 1))
+        at = pl.ds(pl.multiple_of(slots[0, s] * BS, BS), BS)
+
+        @pl.when(s < count)
+        def _(at=at, rows=rows):
+            for f, value in enumerate(rows):
+                out = (kin, comb, close)[f // 6]
+                out[f % 6 : f % 6 + 1, at] = value
 
 
 def body(phase_space, force_rates, irregular, stellar_masses, levels, active, partner):
@@ -420,57 +478,66 @@
     own = jnp.stack([lax.axis_index("blk"), lax.axis_index("grp")]).astype(jnp.int32)
     packed = pl.pallas_call(
         pack_kernel,
-        out_shape=jax.ShapeDtypeStruct((16, W), F32),
+        out_shape=jax.ShapeDtypeStruct((ROWS, BS), F32),
         in_specs=[VMEM, VMEM, VMEM, SMEM],
         out_specs=VMEM,
         name="pack",
     )(phase_space, force_rates, stellar_masses[None, :], levels)
     table = lax.all_gather(packed, "blk", axis=0, tiled=False)
-    levall = table[:, 7, ::BS].astype(jnp.int32).reshape(shards * NB)
+    levall = table[:, 7, :NB].astype(jnp.int32).reshape(shards * NB)
 
     def exchange(pay, axis):
         return lax.all_to_all(pay, axis, split_axis=0, concat_axis=0, tiled=True)
 
-    sums = lambda cap: pltpu.VMEM((cap, 6, 8, 128), F32)
+    parts = lambda cap: pltpu.VMEM((cap, 6, 8, 128), F32)
+    tiles = lambda count: pltpu.VMEM((count, 8, 128), F32)
     slots = pltpu.SMEM((3, 24), jnp.int32)
     state_shape = jax.ShapeDtypeStruct((NB, 8, 128), F32)
-    predicted = pltpu.VMEM((shards, 8, W), F32)
+    predicted = tiles(shards * NB + NB)
     state, pay = pl.pallas_call(
         first_kernel,
         out_shape=(state_shape, jax.ShapeDtypeStruct((everyone, 1, 256), F32)),
         in_specs=[SMEM, VMEM, SMEM, SMEM],
         out_specs=(VMEM, VMEM),
         scratch_shapes=[
-            predicted, sums(4), sums(4), sums(4), pltpu.VMEM((128, 128), F32), slots,
+            predicted, tiles(8), parts(4), parts(4), parts(4), pltpu.VMEM((NB, 128, 128), F32), slots,
         ],
         name="first",
     )(own, table, levels, partner)
-    masses = None
+    masses = ones = None
     for step in (1, 2, 3):
         cap = CAPS[step]
         lanes = (0, 256, 384, 384)[step]
         got = exchange(pay, ("blk", "grp"))
-        sum_shape = jax.ShapeDtypeStruct((cap, 6, 8, 128), F32)
-        reg, irr = pl.pallas_call(
+        sums_shape = jax.ShapeDtypeStruct((cap, 8, 128), F32)
+        outs = pl.pallas_call(
             functools.partial(ahead_kernel, step),
-            out_shape=(sum_shape, sum_shape),
+            out_shape=(sums_shape, jax.ShapeDtypeStruct((1,), jnp.int32)) if step == 1 else sums_shape,
             in_specs=[SMEM, VMEM, SMEM, SMEM, SMEM, VMEM],
-            out_specs=(VMEM, VMEM),
-            scratch_shapes=[predicted, sums(cap), slots],
+            out_specs=(VMEM, SMEM) if step == 1 else VMEM,
+            scratch_shapes=[predicted, tiles(2 * cap), parts(cap), parts(cap), parts(cap), slots],
             name=f"ahead{step}",
         )(own, table, levels, levall, partner, state)
+        if step == 1:
+            sums, ones = outs
+        else:
+            sums = outs
         mass_shape = jax.ShapeDtypeStruct((8, 8, everyone), F32)
         wide = (0, 384, 384, 1152)[step]
         pay_shape = jax.ShapeDtypeStruct((everyone if step < 3 else columns_, 1, wide), F32)
         out_shape = {1: (state_shape, pay_shape, mass_shape), 2: (state_shape, pay_shape), 3: (pay_shape,)}[step]
-        ins = (own, got, levels, levall, partner, state, reg, irr) + (() if step == 1 else (masses,))
+        ins = (own, got, levels, levall, partner, state, sums)
+        specs = [SMEM, VMEM, SMEM, SMEM, SMEM, VMEM, VMEM]
+        if step > 1:
+            ins += (masses, ones)
+            specs += [VMEM, SMEM]
         outs = pl.pallas_call(
             functools.partial(after_kernel, step),
             out_shape=out_shape,
-            in_specs=[SMEM, VMEM, SMEM, SMEM, SMEM] + [VMEM] * (len(ins) - 5),
+            in_specs=specs,
             out_specs=tuple(VMEM for _ in out_shape),
             scratch_shapes=[
-                sums(cap), sums(cap), sums(cap), pltpu.VMEM((lanes // 8, 8, everyone), F32), slots,
+                parts(cap), parts(cap), parts(cap), pltpu.VMEM((lanes // 8, 8, everyone), F32), slots,
             ],
             name=f"after{step}",
         )(*ins)

time: 217 us -> 194 us (0.89)
  Pallas kernels: 95.5 us -> 72.5 us
  waiting for transfers between devices: 55.4 us -> 60.6 us
  blocking collectives: 16.3 us -> 13.7 us
    pallas_call x1, Pallas kernels: 22.1 us -> 2.54 us  [body(): pl.pallas_call(last_kernel, out_shape=(shape, shape, shape), in_specs=[VM...]
    all_to_all x3, waiting for transfers between devices: 14.6 us -> 20.1 us  [exchange(): return lax.all_to_all(pay, axis, split_axis=0, concat_axis=0, tiled=True)]
    pallas_call x4, Pallas kernels: 37.3 us -> 32.3 us  [the longest x3 30.7 us: body(): pl.pallas_call(functools.partial(ahead_kernel, step), out_shape=(sums_sha...]
    all_to_all x1, blocking collectives: 16.3 us -> 13.7 us  [exchange(): return lax.all_to_all(pay, axis, split_axis=0, concat_axis=0, tiled=True)]
  transfers between devices with their start and end apart: 4 -> 4, of which waited for: 4 -> 4; matrix products, arithmetic and copies ran while one was open for 1% -> 1% of each run, Pallas kernels for 17% -> 16%
where the time goes in v2:
time: 194 us
  Pallas kernels  72.5 us (37%)
  waiting for transfers between devices  60.6 us (31%)
  starting transfers between devices  28.4 us (15%)
  between operations  14.1 us (7%)
  blocking collectives  13.7 us (7%)
  local copies, waits for them, and re-layouts  2.79 us (1%)
    all_gather x1, waiting for transfers between devices, body(): table = lax.all_gather(packed, 'blk', axis=0, tiled=False)  40.5 us
    pallas_call x3, Pallas kernels, body(): pl.pallas_call(functools.partial(ahead_kernel, step), out_shape=(sums_sha...  30.7 us
    all_to_all x3, starting transfers between devices, exchange(): return lax.all_to_all(pay, axis, split_axis=0, concat_axis=0, tiled=True)  28.3 us
    pallas_call x3, Pallas kernels, body(): pl.pallas_call(functools.partial(after_kernel, step), out_shape=out_shape...  26.4 us
    all_to_all x3, waiting for transfers between devices, exchange(): return lax.all_to_all(pay, axis, split_axis=0, concat_axis=0, tiled=True)  20.1 us
    all_to_all x1, blocking collectives, exchange(): return lax.all_to_all(pay, axis, split_axis=0, concat_axis=0, tiled=True)  13.7 us
    pallas_call x1, Pallas kernels, body(): pl.pallas_call(first_kernel, out_shape=(state_shape, jax.ShapeDtypeStruct...  11.3 us
  transfers between devices with their start and end apart: 4, of which 4 were waited for; matrix products, arithmetic and copies ran while one was open for 1% of the time, Pallas kernels for 16%

profile of v2, /device:TPU:1, one launch (start us, length us, event | category | flops | bytes accessed | tf_op | source)
XLA Modules:
  0.0 193.6 jit_solution(13480372104038845584)
XLA Ops:
  7.2 0.0 all-gather.3.cloned.1.call-start
  7.2 1.6 pack.1
  8.8 0.0 all-gather.3.cloned.1.call-update
  8.8 0.6 pad_add_fusion.own
  9.5 40.5 %all-gather.3.cloned.1.call-done = f32[3584,128]{1,0:T(8,128)} async-done(((f32[224,128]{1,0:T(8,128)}), f32[3584,128]{1,0:T(8,128)}) %all-gather.3.cloned.1.call-update) | async-done | bytes 1835024 | tf_op jit(solution)/shard_map/all_gather | solution.py:486
  49.9 11.3 %first.1 = (f32[16,8,128]{2,1,0:T(8,128)}, f32[256,1,256]{2,1,0:T(1,128)}) custom-call(s32[2]{0:T(128)} %pad_add_fusion.own, f32[16,224,128]{2,1,0:T(8,128)} %bitcast.4, s32[16]{0:T(128)} %lev.17, s32[16]{0:T(128)} %partner.13), custom_call_target="tpu_custom_call" | custom-call | tf_op jit(solution)/shard_map/first/pallas_call | solution.py:497
  61.2 11.7 %all-to-all-start = ((f32[256,1,256]{2,1,0:T(1,128)}), f32[256,1,256]{2,1,0:T(1,128)S(1)}, u32[]{:S(2)}, u32[]{:S(2)}) async-start(f32[256,1,256]{2,1,0:T(1,128)} %get-tuple-element.12), calls=%async_computation | async-start | bytes 524288 | tf_op jit(solution)/shard_map/all_to_all | solution.py:490
  73.0 0.9 fusion
  73.8 0.6 convert_element_type.8.levall
  74.4 10.9 %ahead1.1 = (f32[6,8,128]{2,1,0:T(8,128)}, s32[1]{0:T(128)}) custom-call(s32[2]{0:T(128)} %pad_add_fusion.own, f32[16,224,128]{2,1,0:T(8,128)} %bitcast.6, s32[16]{0:T(128)} %lev.17, s32[256]{0:T(256)} %convert_element_type.8.levall, s32[16]{0:T(128)} %partner.13, f32[16,8,128]{2,1,0:T(8,128)} %get-tuple-element.13.state.state_in), custom_call_target="tpu_custom_call" | custom-call | tf_op jit(solution)/shard_map/ahead1/pallas_call | solution.py:513
  85.4 3.1 %all-to-all-done.got = f32[256,1,256]{2,1,0:T(1,128)S(1)} async-done(((f32[256,1,256]{2,1,0:T(1,128)}), f32[256,1,256]{2,1,0:T(1,128)S(1)}, u32[]{:S(2)}, u32[]{:S(2)}) %all-to-all-start) | async-done | bytes 262176 | tf_op jit(solution)/shard_map/all_to_all | solution.py:490
  88.5 0.0 copy-start.2
  88.5 0.7 copy-done.2
  89.2 8.1 %after1.1 = (f32[16,8,128]{2,1,0:T(8,128)}, f32[256,1,384]{2,1,0:T(1,128)}, f32[8,8,256]{2,1,0:T(8,128)}) custom-call(s32[2]{0:T(128)} %pad_add_fusion.own, f32[256,1,256]{2,1,0:T(1,128)} %copy-done.2, s32[16]{0:T(128)} %lev.17, s32[256]{0:T(256)} %convert_element_type.8.levall, s32[16]{0:T(128)} %partner.13, ...), custom_call_target="tpu_custom_call" | custom-call | tf_op jit(solution)/shard_map/after1/pallas_call | solution.py:534
  97.3 10.6 %all-to-all-start.1 = ((f32[256,1,384]{2,1,0:T(1,128)}), f32[256,1,384]{2,1,0:T(1,128)S(1)}, u32[]{:S(2)}, u32[]{:S(2)}) async-start(f32[256,1,384]{2,1,0:T(1,128)} %get-tuple-element.15), calls=%async_computation.1 | async-start | bytes 786432 | tf_op jit(solution)/shard_map/all_to_all | solution.py:490
  107.9 7.7 %ahead2.1.sums = f32[4,8,128]{2,1,0:T(8,128)} custom-call(s32[2]{0:T(128)} %pad_add_fusion.own, f32[16,224,128]{2,1,0:T(8,128)} %bitcast.7, s32[16]{0:T(128)} %lev.17, s32[256]{0:T(256)} %convert_element_type.8.levall, s32[16]{0:T(128)} %partner.13, f32[16,8,128]{2,1,0:T(8,128)} %get-tuple-element.16.state.state_in), custom_call_target="tpu_custom_call" | custom-call | tf_op jit(solution)/shard_map/ahead2/pallas_call | solution.py:513
  115.5 10.7 %all-to-all-done.1.got = f32[256,1,384]{2,1,0:T(1,128)S(1)} async-done(((f32[256,1,384]{2,1,0:T(1,128)}), f32[256,1,384]{2,1,0:T(1,128)S(1)}, u32[]{:S(2)}, u32[]{:S(2)}) %all-to-all-start.1) | async-done | bytes 393248 | tf_op jit(solution)/shard_map/all_to_all | solution.py:490
  126.2 0.0 copy-start.1
  126.2 0.7 copy-done.1
  126.9 7.8 %after2.1 = (f32[16,8,128]{2,1,0:T(8,128)}, f32[256,1,384]{2,1,0:T(1,128)}) custom-call(s32[2]{0:T(128)} %pad_add_fusion.own, f32[256,1,384]{2,1,0:T(1,128)} %copy-done.1, s32[16]{0:T(128)} %lev.17, s32[256]{0:T(256)} %convert_element_type.8.levall, s32[16]{0:T(128)} %partner.13, f32[16,8,128]{2,1,0:T(8,128)} %get-tuple-element.16.state.state_in, ...), custom_call_target="tpu_custom_call" | custom-call | tf_op jit(solution)/shard_map/after2/pallas_call | solution.py:534
  134.7 6.0 %all-to-all-start.2 = ((f32[256,1,384]{2,1,0:T(1,128)}), f32[256,1,384]{2,1,0:T(1,128)S(1)}, u32[]{:S(2)}, u32[]{:S(2)}) async-start(f32[256,1,384]{2,1,0:T(1,128)} %get-tuple-element.19), calls=%async_computation.2 | async-start | bytes 786432 | tf_op jit(solution)/shard_map/all_to_all | solution.py:490
  140.7 12.1 %ahead3.1.sums = f32[8,8,128]{2,1,0:T(8,128)} custom-call(s32[2]{0:T(128)} %pad_add_fusion.own, f32[16,224,128]{2,1,0:T(8,128)} %bitcast.8, s32[16]{0:T(128)} %lev.17, s32[256]{0:T(256)} %convert_element_type.8.levall, s32[16]{0:T(128)} %partner.13, f32[16,8,128]{2,1,0:T(8,128)} %get-tuple-element.20.state.state_in), custom_call_target="tpu_custom_call" | custom-call | tf_op jit(solution)/shard_map/ahead3/pallas_call | solution.py:513
  152.9 6.3 %all-to-all-done.2.got = f32[256,1,384]{2,1,0:T(1,128)S(1)} async-done(((f32[256,1,384]{2,1,0:T(1,128)}), f32[256,1,384]{2,1,0:T(1,128)S(1)}, u32[]{:S(2)}, u32[]{:S(2)}) %all-to-all-start.2) | async-done | bytes 393248 | tf_op jit(solution)/shard_map/all_to_all | solution.py:490
  159.2 0.0 copy-start
  159.2 0.7 copy-done
  159.9 10.5 %after3.1 = f32[16,1,1152]{2,1,0:T(1,128)} custom-call(s32[2]{0:T(128)} %pad_add_fusion.own, f32[256,1,384]{2,1,0:T(1,128)} %copy-done, s32[16]{0:T(128)} %lev.17, s32[256]{0:T(256)} %convert_element_type.8.levall, s32[16]{0:T(128)} %partner.13, f32[16,8,128]{2,1,0:T(8,128)} %get-tuple-element.20.state.state_in, f32[8,8,128]{2,1,0:T(8,128)} %ahead3.1.sums, ...), custom_call_target="tpu_custom_call" | custom-call | tf_op jit(solution)/shard_map/after3/pallas_call | solution.py:534
  170.5 13.7 %all_to_all.20.got = f32[16,1,1152]{2,1,0:T(1,128)} all-to-all(f32[16,1,1152]{2,1,0:T(1,128)} %after3.1), channel_id=1, replica_groups=mesh['blk'=16,'grp'=16] {'grp'}, dimensions={0} | all-to-all | bytes 147456 | tf_op jit(solution)/shard_map/all_to_all | solution.py:490
  184.2 2.5 %last.1 = (f32[6,2048]{1,0:T(8,128)}, f32[6,2048]{1,0:T(8,128)}, f32[6,2048]{1,0:T(8,128)}) custom-call(f32[16,1,1152]{2,1,0:T(1,128)} %all_to_all.20.got, f32[6,2048]{1,0:T(8,128)} %ps.3, f32[6,2048]{1,0:T(8,128)} %fr.3, f32[6,2048]{1,0:T(8,128)} %irr.1, s32[16]{0:T(128)} %lev.17), custom_call_target="tpu_custom_call" | custom-call | tf_op jit(solution)/shard_map/last/pallas_call | solution.py:553
Async XLA Ops:
  7.2 42.7 %all-gather.3.cloned.1.call-start = ((), (), s32[]{:S(2)}) async-start(), calls=%async_computation.4 | async-start | bytes 1949696 | tf_op jit(solution)/shard_map/all_gather | solution.py:486
  61.2 27.3 %all-to-all-start = ((f32[256,1,256]{2,1,0:T(1,128)}), f32[256,1,256]{2,1,0:T(1,128)S(1)}, u32[]{:S(2)}, u32[]{:S(2)}) async-start(f32[256,1,256]{2,1,0:T(1,128)} %get-tuple-element.12), calls=%async_computation | async-start | bytes 524288 | tf_op jit(solution)/shard_map/all_to_all | solution.py:490
  88.5 0.7 copy-start.2
  97.3 28.9 %all-to-all-start.1 = ((f32[256,1,384]{2,1,0:T(1,128)}), f32[256,1,384]{2,1,0:T(1,128)S(1)}, u32[]{:S(2)}, u32[]{:S(2)}) async-start(f32[256,1,384]{2,1,0:T(1,128)} %get-tuple-element.15), calls=%async_computation.1 | async-start | bytes 786432 | tf_op jit(solution)/shard_map/all_to_all | solution.py:490
  126.2 0.7 copy-start.1
  134.7 24.5 %all-to-all-start.2 = ((f32[256,1,384]{2,1,0:T(1,128)}), f32[256,1,384]{2,1,0:T(1,128)S(1)}, u32[]{:S(2)}, u32[]{:S(2)}) async-start(f32[256,1,384]{2,1,0:T(1,128)} %get-tuple-element.19), calls=%async_computation.2 | async-start | bytes 786432 | tf_op jit(solution)/shard_map/all_to_all | solution.py:490
  159.2 0.7 copy-start
Sparse Core Ops, SparseCore 0:
  9.8 40.0 all-gather.2

commit v3 on v2

v3 whole, which is shorter than its diff:
```python
import functools
import jax
import jax.numpy as jnp
from jax import lax
from jax.experimental import pallas as pl
from jax.experimental.pallas import tpu as pltpu
from jax.sharding import PartitionSpec as P

WIDE = 0.04
CLOSE = 0.0001
TICK = 0.125
NB = 16
BS = 128
W = NB * BS
F32 = jnp.float32
CAPS = (4, 6, 4, 8)
TOP = (0, 1, 0, 2)
SENT = (-1, 0, 1, 1)
SLOTS = (0, 4, 8, 8)

VMEM = pl.BlockSpec(memory_space=pltpu.VMEM)
SMEM = pl.BlockSpec(memory_space=pltpu.SMEM)


def pair(target, source, mass, soften, acc):
    r = [source[c] - target[c] for c in range(3)]
    w = [source[c] - target[c] for c in range(3, 6)]
    d = (r[0] * r[0] + soften) + r[1] * r[1] + r[2] * r[2]
    s = lax.rsqrt(d)
    s2 = s * s
    weight = (mass * s) * s2
    q = (r[0] * w[0] + r[1] * w[1] + r[2] * w[2]) * (s2 * 3.0)
    acc = list(acc)
    for c in range(3):
        acc[c] = acc[c] + weight * r[c]
        acc[3 + c] = acc[3 + c] + weight * (w[c] - q * r[c])
    return tuple(acc)


def pair_split(target, source, mass, acc):
    r = [source[c] - target[c] for c in range(3)]
    w = [source[c] - target[c] for c in range(3, 6)]
    dd = r[0] * r[0] + r[1] * r[1] + r[2] * r[2]
    rw = (r[0] * w[0] + r[1] * w[1] + r[2] * w[2]) * 3.0
    acc = list(acc)
    for soften, sign in ((CLOSE, 1.0), (WIDE, -1.0)):
        s = lax.rsqrt(dd + soften)
        s2 = s * s
        weight = (mass * s) * (s2 * sign)
        q = rw * s2
        for c in range(3):
            acc[c] = acc[c] + weight * r[c]
            acc[3 + c] = acc[3 + c] + weight * (w[c] - q * r[c])
    return tuple(acc)


def zeros():
    return tuple(jnp.zeros((8, 128), F32) for _ in range(6))


BLOCK, PLACE, LEVEL, SHARD, ROW, HERE, COUNT = range(7)


def fill_slots(lev, top, cap, plan):
    for s in range(cap):
        plan[BLOCK, s] = 0
        plan[PLACE, s] = -1000
        plan[LEVEL, s] = 0
    count = jnp.int32(0)
    ones = [jnp.int32(0), jnp.int32(4)]
    for k in range(NB):
        level = lev[k]
        live = level <= top
        place = jnp.where(level == 0, ones[0], jnp.where(level == 1, ones[1], -1000))
        plan[BLOCK, count] = k
        plan[PLACE, count] = jnp.where(live, place, -1000)
        plan[LEVEL, count] = jnp.where(live, level, 0)
        count = count + live.astype(jnp.int32)
        ones[0] = ones[0] + (level == 0).astype(jnp.int32)
        ones[1] = ones[1] + (level == 1).astype(jnp.int32)
    plan[COUNT, 0] = count


def fill_near(plan, cap, own, levall, partner, sent):
    for s in range(cap):
        k = plan[BLOCK, s]
        q = partner[k] // NB
        level = levall[q * NB + k]
        place = jnp.where(level == 0, 0, 4)
        for e in range(NB):
            same = (levall[q * NB + e] == level) & (e < k)
            place = place + same.astype(jnp.int32)
        ours = plan[LEVEL, s] <= sent
        theirs = (q != own) & (level <= sent)
        for e, (b, row, here) in enumerate(((own, plan[PLACE, s], ours), (q, place, theirs))):
            plan[SHARD, 2 * s + e] = b
            plan[ROW, 2 * s + e] = jnp.clip(jnp.where(here, row, 0), 0, 3 if sent == 0 else 7)
            plan[HERE, 2 * s + e] = here.astype(jnp.int32)


def span_of(level):
    return jnp.where(level == 0, TICK, jnp.where(level == 1, 2 * TICK, 4 * TICK)).astype(F32)


XS, MS, VS, AS, JS = (0, 1, 2), 3, (4, 5, 6), (8, 9, 10), (11, 12, 13)


def columns(tile):
    return tuple(
        [tile[:, c : c + 1] for c in group] for group in (XS, VS, AS, JS)
    )


def forecast(x, v, a, j, t):
    t2 = t * t * 0.5
    t3 = t * t * t * (1.0 / 6.0)
    xp = [x[c] + v[c] * t + a[c] * t2 + j[c] * t3 for c in range(3)]
    vp = [v[c] + a[c] * t + j[c] * t2 for c in range(3)]
    return xp + vp


class Forecast:
    def __init__(self, t):
        row = lax.broadcasted_iota(jnp.int32, (8, 128), 0)
        zero = jnp.zeros((8, 128), F32)
        low = row < 3
        high = (row > 3) & (row < 7)
        self.low = lambda value: jnp.where(low, value, zero)
        self.high = lambda value: jnp.where(high, value, zero)
        t2 = t * t * 0.5
        t3 = t * t * t / 6.0
        self.c = (self.low(t), self.low(t2), self.low(t3), self.high(t), self.high(t2))

    def __call__(self, table, rates, b, k):
        first = table[b, pl.ds(7 * k, 8), :]
        value = first + self.c[0] * pltpu.roll(first, 4, 0)
        for c, o in zip(self.c[1:], (4, 7, 0, 3)):
            value = value + c * rates[b, pl.ds(6 * k + o, 8), :]
        return value


def fill_sources(table, rates, predicted, ahead, levall, sent):
    def shard(b, count):
        for k in range(NB):
            predicted[count] = ahead(table, rates, b, k)
            count = count + (levall[b * NB + k] > sent).astype(jnp.int32)
        return count

    count = lax.fori_loop(0, table.shape[0], shard, jnp.int32(0))
    for e in range(NB):
        predicted[count + e] = jnp.zeros((8, 128), F32)
    return count


def fill_targets(state, plan, cap, targets):
    for s in range(cap):
        x, v, a, j = columns(state[plan[BLOCK, s]])
        t = span_of(plan[LEVEL, s])
        for c, value in enumerate(forecast(x, v, a, j, t)):
            targets[s, c] = jnp.broadcast_to(value, (8, 128))


def broad(row):
    return jnp.broadcast_to(row, (8, 128))


def tile_rows(tiles, at, start=0):
    rows = [broad(tiles[at, pl.ds(start + r, 1), :]) for r in (0, 1, 2, 4, 5, 6)]
    return rows, broad(tiles[at, pl.ds(start + 3, 1), :])


def sweep_table(groups, load, targets, cap, regular):
    def two(p, _):
        goal = [[targets[2 * p + e, c] for c in range(6)] for e in range(2)]

        def group(b, acc):
            for k in range(NB):
                rows, mass = load(b, k)
                acc = tuple(pair(goal[e], rows, mass, WIDE, acc[e]) for e in range(2))
            return acc

        acc = lax.fori_loop(0, groups, group, (zeros(), zeros()))
        for e in range(2):
            for c in range(6):
                regular[2 * p + e, c] = acc[e][c]
        return 0

    lax.fori_loop(0, cap // 2, two, 0)


def close_pairs(load, wanted, targets, cap, irregular):
    for s in range(cap):
        goal = [targets[s, c] for c in range(6)]
        acc = zeros()
        for e in range(2):
            rows, mass = load(s, e)
            acc = pair_split(goal, rows, mass * jnp.where(wanted(s, e), 1.0, 0.0).astype(F32), acc)
        for c in range(6):
            irregular[s, c] = acc[c]


def sum_up(regular, irregular, cap, sums):
    lane = lax.broadcasted_iota(jnp.int32, (8, 128), 1)
    for s in range(cap):
        tile = jnp.zeros((8, 128), F32)
        for at, part in ((0, regular), (8, irregular)):
            for c in range(6):
                tile = jnp.where(lane == at + c, jnp.sum(part[s, c], axis=1, keepdims=True), tile)
        sums[s] = tile


def fill_received(got, turned):
    senders, _, lanes = got.shape
    for t in range(lanes // 128):
        for half in range(senders // 128):
            part = got[pl.ds(half * 128, 128), 0, pl.ds(t * 128, 128)]
            turned[pl.ds(t * 16, 16), :, pl.ds(half * 128, 128)] = part.T.reshape(16, 8, 128)


def sweep_received(turned, mass, slots_in, used, targets, plan, near, cap, regular):
    halves = turned.shape[2] // 128
    lane = lax.broadcasted_iota(jnp.int32, (8, 128), 1)
    row = lax.broadcasted_iota(jnp.int32, (8, 128), 0)
    keep = lane // 16 == row

    def two(p, _):
        goal = [[targets[2 * p + e, c] for c in range(6)] for e in range(2)]

        def slot(s, acc):
            item = 4 * p + lax.rem(s, 4)
            b = plan[SHARD, item]
            place = plan[ROW, item]
            half = pl.ds(pl.multiple_of((b // 8) * 128, 128), 128)
            shift = lax.rem(128 - lax.rem(b, 8) * 16, 128)
            here = plan[HERE, item].astype(F32)
            for r, f in ((0, 0), (1, 1), (2, 2), (4, 3), (5, 4), (6, 5), (3, None)):
                tile = mass[place, :, half] * here if f is None else turned[f * slots_in + place, :, half]
                tile = pltpu.roll(pltpu.roll(tile, shift, 1), 0, 1, stride=16, stride_axis=0)
                near[item, r : r + 1, :] = jnp.sum(jnp.where(keep, tile, 0.0), axis=0, keepdims=True)
            for i in range(8):
                for half in range(halves):
                    at = pl.ds(half * 128, 128)
                    rows = [broad(turned[f * slots_in + s, i : i + 1, at]) for f in range(6)]
                    m = broad(mass[s, i : i + 1, at])
                    acc = tuple(pair(goal[e], rows, m, WIDE, acc[e]) for e in range(2))
            return acc

        acc = lax.fori_loop(0, used, slot, (zeros(), zeros()))
        for e in range(2):
            for c in range(6):
                regular[2 * p + e, c] = acc[e][c]
        return 0

    lax.fori_loop(0, cap // 2, two, 0)


def fill_tiles(parts, tiles, width):
    per = 128 // width
    tiles = list(tiles)
    lane = lax.broadcasted_iota(jnp.int32, (8, 128), 1)
    for f, slot, column in parts:
        t = f // per
        tiles[t] = jnp.where(lane == (f % per) * width + slot * 8, column, tiles[t])
    return tiles


def blank(count):
    return [jnp.zeros((8, 128), F32) for _ in range(count)]


def place_tiles(tiles):
    tiles = [pltpu.roll(tile, 0, 1, stride=1, stride_axis=0) for tile in tiles]
    return [jnp.sum(tile, axis=0, keepdims=True) for tile in tiles]


def send(tiles, pay):
    for t, tile in enumerate(tiles):
        full = jnp.broadcast_to(tile[None], (pay.shape[0], 1, 128))
        pay[:, :, pl.ds(t * 128, 128)] = full


def finish(step, state, plan, cap, regular, irregular, sums, later, pay, lev):
    lane = lax.broadcasted_iota(jnp.int32, (8, 128), 1)
    count = plan[COUNT, 0]
    parts = []
    for s in range(cap):
        k = plan[BLOCK, s]
        level = plan[LEVEL, s]
        place = plan[PLACE, s]
        t = span_of(level)
        tile = state[k]
        x, v, a, j = columns(tile)
        close = [jnp.sum(irregular[s, c], axis=1, keepdims=True) for c in range(6)]
        total = [jnp.sum(regular[s, c], axis=1, keepdims=True) for c in range(6)]
        if sums is not None:
            before = sums[s]
            close = [close[c] + before[:, 8 + c : 9 + c] for c in range(6)]
            total = [total[c] + before[:, c : c + 1] for c in range(6)]
        total = [total[c] + close[c] for c in range(6)]
        half = t * 0.5
        twelfth = t * t * (1.0 / 12.0)
        v1 = [v[c] + (a[c] + total[c]) * half + (j[c] - total[3 + c]) * twelfth for c in range(3)]
        x1 = [x[c] + (v[c] + v1[c]) * half + (a[c] - total[c]) * twelfth for c in range(3)]
        if step == 3:
            for f, column in enumerate(x1 + v1 + total + close):
                parts.append((f, s, column))
            continue
        fresh = tile
        for at, column in zip(XS + VS + AS + JS, x1 + v1 + total):
            fresh = jnp.where(lane == at, column, fresh)

        @pl.when(s < count)
        def _(k=k, fresh=fresh):
            state[k] = fresh

        ahead = forecast(x1, v1, total[:3], total[3:], TICK)
        for f, column in enumerate(ahead):
            parts.append((f, place, column))
        if step == 0:
            parts.append((6, place, tile[:, MS : MS + 1]))
    if step == 0:
        seen = jnp.int32(0)
        for k in range(NB):
            one = lev[k] == 1
            parts.append((7, jnp.where(one, seen, -1000), state[k][:, MS : MS + 1]))
            seen = seen + one.astype(jnp.int32)
        send(place_tiles(fill_tiles(parts, blank(2), 32)), pay)
    elif step == 1:
        send(place_tiles(fill_tiles(parts, blank(3), 64)), pay)
    elif step == 2:
        send(place_tiles(fill_tiles(parts, [later[t] for t in range(3)], 64)), pay)
    else:
        send(place_tiles(fill_tiles(parts, blank(9), 64)), pay)


def fill_later(state, lev, later):
    parts = []
    seen = jnp.int32(4)
    for k in range(NB):
        one = lev[k] == 1
        mark = jnp.where(one, seen, -1000)
        x, v, a, j = columns(state[k])
        for f, column in enumerate(forecast(x, v, a, j, 2 * TICK)):
            parts.append((f, mark, column))
        seen = seen + one.astype(jnp.int32)
    for t, tile in enumerate(fill_tiles(parts, blank(3), 64)):
        later[t] = tile


def pack_kernel(ps, fr, mass, lev, first, rates, own):
    x, v, a, j = ps[0:3, :], ps[3:6, :], fr[0:3, :], fr[3:6, :]
    t2 = TICK * TICK * 0.5
    xp = x + v * TICK + a * t2 + j * (TICK * TICK * TICK / 6.0)
    vp = v + a * TICK + j * t2
    ap = a + j * TICK
    lane = lax.broadcasted_iota(jnp.int32, (8, BS), 1)
    levels = jnp.zeros((8, BS), F32)
    for k in range(NB):
        levels = jnp.where(lane == k, lev[k].astype(F32), levels)
    first[7 * NB : 7 * NB + 8, :] = levels
    rates[0:8, :] = jnp.zeros((8, BS), F32)
    rates[96:112, :] = jnp.zeros((16, BS), F32)
    for k in range(NB):
        at = slice(k * BS, k * BS + BS)
        first[7 * k : 7 * k + 3, :] = xp[:, at]
        first[7 * k + 3 : 7 * k + 4, :] = mass[:, at]
        first[7 * k + 4 : 7 * k + 7, :] = vp[:, at]
        rates[6 * k + 4 : 6 * k + 7, :] = ap[:, at]
        rates[6 * k + 7 : 6 * k + 10, :] = j[:, at]
        own[k] = jnp.zeros((16, BS), F32)
        own[k, 0:3, :] = x[:, at]
        own[k, 3:4, :] = mass[:, at]
        own[k, 4:7, :] = v[:, at]
        own[k, 8:14, :] = fr[:, at]


def first_kernel(own, table, mine, lev, partner, state, pay, targets, regular, irregular, turned, plan):
    me = own[0]
    col = pl.multiple_of(own[1] * 8, 8)
    cap = CAPS[0]
    fill_slots(lev, TOP[0], cap, plan)
    for k in range(NB):
        turned[k, :, 0:16] = mine[k].T
    for k in range(NB):
        state[k] = turned[k, pl.ds(col, 8), :]
    fill_targets(state, plan, cap, targets)
    sweep_table(table.shape[0], lambda b, k: tile_rows(table, b, 7 * k), targets, cap, regular)

    def shard(s, e):
        return partner[plan[BLOCK, s]] // NB if e else me

    close_pairs(
        lambda s, e: tile_rows(table, shard(s, e), 7 * plan[BLOCK, s]),
        lambda s, e: shard(s, e) != me if e else jnp.bool_(True),
        targets, cap, irregular,
    )
    finish(0, state, plan, cap, regular, irregular, None, None, pay, lev)


def ahead_kernel(step, own, table, rates, lev, levall, partner, state, sums, plan, *rest):
    later = None
    if step == 2:
        later, *rest = rest
    predicted, near, targets, regular, irregular = rest
    cap = CAPS[step]
    sent = SENT[step]
    fill_slots(lev, TOP[step], cap, plan)
    fill_near(plan, cap, own[0], levall, partner, sent)
    ahead = Forecast(step * TICK)
    used = fill_sources(table, rates, predicted, ahead, levall, sent)
    fill_targets(state, plan, cap, targets)
    for s in range(cap):
        for e in range(2):
            near[2 * s + e] = ahead(table, rates, plan[SHARD, 2 * s + e], plan[BLOCK, s])
    sweep_table((used + NB - 1) // NB, lambda b, k: tile_rows(predicted, b * NB + k), targets, cap, regular)

    def wanted(s, e):
        other = plan[SHARD, 2 * s + 1] != own[0] if e else jnp.bool_(True)
        return other & (plan[HERE, 2 * s + e] == 0)

    close_pairs(lambda s, e: tile_rows(near, 2 * s + e), wanted, targets, cap, irregular)
    sum_up(regular, irregular, cap, sums)
    if step == 2:
        fill_later(state, lev, later)
    if step == 1:

        def shard(b, most):
            here = jnp.int32(0)
            for k in range(NB):
                here = here + (levall[b * NB + k] == 1).astype(jnp.int32)
            return jnp.maximum(most, here)

        plan[COUNT, 1] = lax.fori_loop(0, table.shape[0], shard, jnp.int32(0))


def after_kernel(step, got, lev, state_in, sums, plan, *rest):
    later = None
    used = SLOTS[step]
    if step > 1:
        masses, before, *rest = rest
        used = jnp.minimum(4 + before[COUNT, 1], used)
    if step == 2:
        later, *rest = rest
    if step == 3:
        state = state_in
    else:
        state, *rest = rest
        state[...] = state_in[...]
    pay, *rest = rest
    if step == 1:
        masses, *rest = rest
    regular, irregular, targets, near, turned = rest
    cap = CAPS[step]
    fill_received(got, turned)
    if step == 1:
        masses[0:4] = turned[24:28]
        masses[4:8] = turned[28:32]
    fill_targets(state, plan, cap, targets)
    sweep_received(turned, masses, SLOTS[step], used, targets, plan, near, cap, regular)
    close_pairs(
        lambda s, e: tile_rows(near, 2 * s + e),
        lambda s, e: plan[HERE, 2 * s + e] == 1,
        targets, cap, irregular,
    )
    finish(step, state, plan, cap, regular, irregular, sums, later, pay, lev)


def last_kernel(got, ps, fr, irr, plan, kin, comb, close):
    count = plan[COUNT, 0]
    kin[...] = ps[...]
    comb[...] = fr[...]
    close[...] = irr[...]
    senders = got.shape[0]
    lane = lax.broadcasted_iota(jnp.int32, (senders, 128), 1)
    row = lax.broadcasted_iota(jnp.int32, (senders, 128), 0)
    spread = [pltpu.roll(got[:, 0, pl.ds(t * 128, 128)], 0, 1, stride=8, stride_axis=0) for t in range(9)]
    for s in range(CAPS[3]):
        rows = []
        for f in range(18):
            t, e = divmod(f, 2)
            start = e * 64 + s * 8
            keep = (lane + (128 - start)) % 128 // 8 == row
            value = jnp.sum(jnp.where(keep, spread[t], 0.0), axis=0, keepdims=True)
            rows.append(pltpu.roll(value, (128 - start) % 128, 1))
        at = pl.ds(pl.multiple_of(plan[BLOCK, s] * BS, BS), BS)

        @pl.when(s < count)
        def _(at=at, rows=rows):
            for f, value in enumerate(rows):
                out = (kin, comb, close)[f // 6]
                out[f % 6 : f % 6 + 1, at] = value


def body(phase_space, force_rates, irregular, stellar_masses, levels, active, partner):
    shards = lax.axis_size("blk")
    columns_ = lax.axis_size("grp")
    everyone = shards * columns_
    own = jnp.stack([lax.axis_index("blk"), lax.axis_index("grp")]).astype(jnp.int32)
    tiles = lambda count: pltpu.VMEM((count, 8, 128), F32)
    parts = lambda cap: pltpu.VMEM((cap, 6, 8, 128), F32)
    array = lambda *shape: jax.ShapeDtypeStruct(shape, F32)
    plan_shape = jax.ShapeDtypeStruct((8, 32), jnp.int32)
    state_shape = array(NB, 8, 128)

    def exchange(pay, axis):
        return lax.all_to_all(pay, axis, split_axis=0, concat_axis=0, tiled=True)

    packed, rates, mine = pl.pallas_call(
        pack_kernel,
        out_shape=(array(7 * NB + 8, BS), array(7 * NB, BS), array(NB, 16, BS)),
        in_specs=[VMEM, VMEM, VMEM, SMEM],
        out_specs=(VMEM, VMEM, VMEM),
        name="pack",
    )(phase_space, force_rates, stellar_masses[None, :], levels)
    table = lax.all_gather(packed, "blk", axis=0, tiled=False)
    levall = table[:, 7 * NB, :NB].astype(jnp.int32).reshape(shards * NB)
    rates = exchange(jnp.broadcast_to(rates[None], (shards, 7 * NB, BS)), "blk")
    state, pay = pl.pallas_call(
        first_kernel,
        out_shape=(state_shape, array(everyone, 1, 256)),
        in_specs=[SMEM, VMEM, VMEM, SMEM, SMEM],
        out_specs=(VMEM, VMEM),
        scratch_shapes=[
            parts(4), parts(4), parts(4), pltpu.VMEM((NB, 128, 128), F32), pltpu.SMEM((8, 32), jnp.int32),
        ],
        name="first",
    )(own, table, mine, levels, partner)
    masses = before = None
    for step in (1, 2, 3):
        cap = CAPS[step]
        lanes = (0, 256, 384, 384)[step]
        got = exchange(pay, ("blk", "grp"))
        outs = pl.pallas_call(
            functools.partial(ahead_kernel, step),
            out_shape=(array(cap, 8, 128), plan_shape) + ((array(3, 8, 128),) if step == 2 else ()),
            in_specs=[SMEM, VMEM, VMEM, SMEM, SMEM, SMEM, VMEM],
            out_specs=(VMEM, SMEM) + ((VMEM,) if step == 2 else ()),
            scratch_shapes=[tiles(shards * NB + NB), tiles(2 * cap), parts(cap), parts(cap), parts(cap)],
            name=f"ahead{step}",
        )(own, table, rates, levels, levall, partner, state)
        sums, plan = outs[:2]
        ins = (got, levels, state, sums, plan)
        specs = [VMEM, SMEM, VMEM, VMEM, SMEM]
        if step > 1:
            ins += (masses, before)
            specs += [VMEM, SMEM]
        if step == 2:
            ins += (outs[2],)
            specs += [VMEM]
        pay_shape = array(everyone if step < 3 else columns_, 1, (0, 384, 384, 1152)[step])
        out_shape = {
            1: (state_shape, pay_shape, array(8, 8, everyone)), 2: (state_shape, pay_shape), 3: (pay_shape,),
        }[step]
        outs = pl.pallas_call(
            functools.partial(after_kernel, step),
            out_shape=out_shape,
            in_specs=specs,
            out_specs=tuple(VMEM for _ in out_shape),
            scratch_shapes=[
                parts(cap), parts(cap), parts(cap), tiles(2 * cap), pltpu.VMEM((lanes // 8, 8, everyone), F32),
            ],
            name=f"after{step}",
        )(*ins)
        if step == 1:
            state, pay, masses = outs
            before = plan
        elif step == 2:
            state, pay = outs
        else:
            (pay,) = outs
    got = exchange(pay, "grp")
    shape = array(6, W)
    return tuple(
        pl.pallas_call(
            last_kernel,
            out_shape=(shape, shape, shape),
            in_specs=[VMEM, VMEM, VMEM, VMEM, SMEM],
            out_specs=(VMEM, VMEM, VMEM),
            name="last",
        )(got, phase_space, force_rates, irregular, plan)
    )


def solution(mesh):
    in_specs = (
        P(None, "blk"), P(None, "blk"), P(None, "blk"), P("blk"), P("blk"), P(None, "blk"), P("blk"),
    )
    out_specs = (P(None, "blk"), P(None, "blk"), P(None, "blk"))
    return jax.shard_map(body, mesh=mesh, in_specs=in_specs, out_specs=out_specs, check_vma=False)
```

time: 194 us -> 184 us (0.948)
  waiting for transfers between devices: 60.6 us -> 19.2 us
  blocking collectives: 13.7 us -> 44.5 us
  between operations: 14.1 us -> 0.69 us
  starting transfers between devices: 28.4 us -> 35.9 us
  Pallas kernels: 72.5 us -> 76.4 us
    all_gather x1 -> x0, waiting for transfers between devices: 40.5 us -> none  [body(): table = lax.all_gather(packed, 'blk', axis=0, tiled=False)]
    all_gather x0 -> x1, blocking collectives: none -> 30.7 us  [body(): table = lax.all_gather(packed, 'blk', axis=0, tiled=False)]
    all_to_all x3 -> x4, starting transfers between devices: 28.3 us -> 35.9 us  [exchange(): return lax.all_to_all(pay, axis, split_axis=0, concat_axis=0, tiled=True)]
    pallas_call x3, Pallas kernels: 26.4 us -> 30.6 us  [body(): pl.pallas_call(functools.partial(after_kernel, step), out_shape=out_shape...]
    all_to_all x3 -> x4, waiting for transfers between devices: 20.1 us -> 19.2 us  [exchange(): return lax.all_to_all(pay, axis, split_axis=0, concat_axis=0, tiled=True)]
  transfers between devices with their start and end apart: 4 -> 4, of which waited for: 4 -> 3; matrix products, arithmetic and copies ran while one was open for 1% -> 1% of each run, Pallas kernels for 16% -> 23%
where the time goes in v3:
time: 184 us; the launch traced here: 183 us
  Pallas kernels  76.4 us (42%)
  blocking collectives  44.5 us (24%)
  starting transfers between devices  35.9 us (20%)
  waiting for transfers between devices  19.2 us (10%)
  local copies, waits for them, and re-layouts  4.71 us (3%)
    all_to_all x4, starting transfers between devices, exchange(): return lax.all_to_all(pay, axis, split_axis=0, concat_axis=0, tiled=True)  35.9 us
    pallas_call x3, Pallas kernels, body(): pl.pallas_call(functools.partial(ahead_kernel, step), out_shape=(array(ca...  31.6 us
    all_gather x1, blocking collectives, body(): table = lax.all_gather(packed, 'blk', axis=0, tiled=False)  30.7 us
    pallas_call x3, Pallas kernels, body(): pl.pallas_call(functools.partial(after_kernel, step), out_shape=out_shape...  30.6 us
    all_to_all x4, waiting for transfers between devices, exchange(): return lax.all_to_all(pay, axis, split_axis=0, concat_axis=0, tiled=True)  19.2 us
    all_to_all x1, blocking collectives, exchange(): return lax.all_to_all(pay, axis, split_axis=0, concat_axis=0, tiled=True)  13.9 us
    pallas_call x1, Pallas kernels, body(): pl.pallas_call(first_kernel, out_shape=(state_shape, array(everyone, 1, 2...  10.1 us
  transfers between devices with their start and end apart: 4, of which 3 were waited for; matrix products, arithmetic and copies ran while one was open for 1% of the time, Pallas kernels for 23%

profile of v3, /device:TPU:1, one launch (start us, length us, event | category | flops | bytes accessed | tf_op | source)
XLA Modules:
  0.0 183.0 jit_solution(13117305801300109323)
XLA Ops:
  0.6 1.6 pack.1
  2.3 1.9 %broadcast_in_dim.10 = f32[16,112,128]{2,1,0:T(8,128)} broadcast(f32[112,128]{1,0:T(8,128)} %get-tuple-element.24), dimensions={1,2} | broadcast | bytes 974848 | tf_op jit(solution)/shard_map/broadcast_in_dim | solution.py:517
  4.1 0.0 copy-start.4
  4.1 6.9 %all-to-all-start.1 = ((f32[16,112,128]{2,1,0:T(8,128)}), f32[16,112,128]{2,1,0:T(8,128)S(1)}, u32[]{:S(2)}, u32[]{:S(2)}) async-start(f32[16,112,128]{2,1,0:T(8,128)} %broadcast_in_dim.10), calls=%async_computation.1 | async-start | bytes 1835008 | tf_op jit(solution)/shard_map/all_to_all | solution.py:506
  11.1 0.7 pad_add_fusion.own
  11.7 0.0 copy-done.4
  11.7 30.7 %all-gather = f32[1920,128]{1,0:T(8,128)} all-gather(f32[120,128]{1,0:T(8,128)S(1)} %copy-done.4), channel_id=2, replica_groups=mesh['blk'=16,'grp'=16] {'blk'}, dimensions={0}, use_global_device_ids=true | all-gather | bytes 1044480 | tf_op jit(solution)/shard_map/all_gather | solution.py:515
  42.4 10.1 %first.1 = (f32[16,8,128]{2,1,0:T(8,128)}, f32[256,1,256]{2,1,0:T(1,128)}) custom-call(s32[2]{0:T(128)} %pad_add_fusion.own, f32[16,120,128]{2,1,0:T(8,128)} %bitcast.4, f32[16,16,128]{2,1,0:T(8,128)} %get-tuple-element.21.mine, s32[16]{0:T(128)} %lev.15, s32[16]{0:T(128)} %partner.7), custom_call_target="tpu_custom_call" | custom-call | tf_op jit(solution)/shard_map/first/pallas_call | solution.py:518
  52.6 0.0 all-to-all-done.1.rates
  52.6 0.0 copy-start
  52.6 12.1 %all-to-all-start = ((f32[256,1,256]{2,1,0:T(1,128)}), f32[256,1,256]{2,1,0:T(1,128)S(1)}, u32[]{:S(2)}, u32[]{:S(2)}) async-start(f32[256,1,256]{2,1,0:T(1,128)} %get-tuple-element.22), calls=%async_computation | async-start | bytes 524288 | tf_op jit(solution)/shard_map/all_to_all | solution.py:506
  64.7 0.9 fusion
  65.5 0.7 convert_element_type.8.levall
  66.2 0.0 copy-done
  66.2 11.1 %ahead1.1 = (f32[6,8,128]{2,1,0:T(8,128)}, s32[8,32]{1,0:T(8,128)}) custom-call(s32[2]{0:T(128)} %pad_add_fusion.own, f32[16,120,128]{2,1,0:T(8,128)} %bitcast.6, f32[16,112,128]{2,1,0:T(8,128)} %copy-done, s32[16]{0:T(128)} %lev.15, s32[256]{0:T(256)} %convert_element_type.8.levall, s32[16]{0:T(128)} %partner.7, f32[16,8,128]{2,1,0:T(8,128)} %get-tuple-element.23.state.state_in), custom_call_target="tpu_custom_call" | custom-call | tf_op jit(solution)/shard_map/ahead1/pallas_call | solution.py:533
  77.3 2.9 %all-to-all-done.got = f32[256,1,256]{2,1,0:T(1,128)S(1)} async-done(((f32[256,1,256]{2,1,0:T(1,128)}), f32[256,1,256]{2,1,0:T(1,128)S(1)}, u32[]{:S(2)}, u32[]{:S(2)}) %all-to-all-start) | async-done | bytes 262176 | tf_op jit(solution)/shard_map/all_to_all | solution.py:506
  80.2 0.0 copy-start.3
  80.2 0.7 copy-done.3
  80.9 9.5 %after1.1 = (f32[16,8,128]{2,1,0:T(8,128)}, f32[256,1,384]{2,1,0:T(1,128)}, f32[8,8,256]{2,1,0:T(8,128)}) custom-call(f32[256,1,256]{2,1,0:T(1,128)} %copy-done.3, s32[16]{0:T(128)} %lev.15, f32[16,8,128]{2,1,0:T(8,128)} %get-tuple-element.23.state.state_in, f32[6,8,128]{2,1,0:T(8,128)} %get-tuple-element.25.sums, s32[8,32]{1,0:T(8,128)} %get-tuple-element.26.plan.rest_1_), custom_call_target="tpu_custom_call" | custom-call | tf_op jit(solution)/shard_map/after1/pallas_call | solution.py:554
  90.4 10.8 %all-to-all-start.2 = ((f32[256,1,384]{2,1,0:T(1,128)}), f32[256,1,384]{2,1,0:T(1,128)S(1)}, u32[]{:S(2)}, u32[]{:S(2)}) async-start(f32[256,1,384]{2,1,0:T(1,128)} %get-tuple-element.27), calls=%async_computation.2 | async-start | bytes 786432 | tf_op jit(solution)/shard_map/all_to_all | solution.py:506
  101.3 8.0 %ahead2.1 = (f32[4,8,128]{2,1,0:T(8,128)}, s32[8,32]{1,0:T(8,128)}, f32[3,8,128]{2,1,0:T(8,128)}) custom-call(s32[2]{0:T(128)} %pad_add_fusion.own, f32[16,120,128]{2,1,0:T(8,128)} %bitcast.7, f32[16,112,128]{2,1,0:T(8,128)} %copy-done, s32[16]{0:T(128)} %lev.15, s32[256]{0:T(256)} %convert_element_type.8.levall, s32[16]{0:T(128)} %partner.7, ...), custom_call_target="tpu_custom_call" | custom-call | tf_op jit(solution)/shard_map/ahead2/pallas_call | solution.py:533
  109.3 10.3 %all-to-all-done.2.got = f32[256,1,384]{2,1,0:T(1,128)S(1)} async-done(((f32[256,1,384]{2,1,0:T(1,128)}), f32[256,1,384]{2,1,0:T(1,128)S(1)}, u32[]{:S(2)}, u32[]{:S(2)}) %all-to-all-start.2) | async-done | bytes 393248 | tf_op jit(solution)/shard_map/all_to_all | solution.py:506
  119.6 0.0 copy-start.2
  119.6 0.7 copy-done.2
  120.3 8.5 %after2.1 = (f32[16,8,128]{2,1,0:T(8,128)}, f32[256,1,384]{2,1,0:T(1,128)}) custom-call(f32[256,1,384]{2,1,0:T(1,128)} %copy-done.2, s32[16]{0:T(128)} %lev.15, f32[16,8,128]{2,1,0:T(8,128)} %get-tuple-element.28.state.state_in, f32[4,8,128]{2,1,0:T(8,128)} %get-tuple-element.29.sums, s32[8,32]{1,0:T(8,128)} %get-tuple-element.30.plan, ...), custom_call_target="tpu_custom_call" | custom-call | tf_op jit(solution)/shard_map/after2/pallas_call | solution.py:554
  128.9 6.0 %all-to-all-start.3 = ((f32[256,1,384]{2,1,0:T(1,128)}), f32[256,1,384]{2,1,0:T(1,128)S(1)}, u32[]{:S(2)}, u32[]{:S(2)}) async-start(f32[256,1,384]{2,1,0:T(1,128)} %get-tuple-element.33), calls=%async_computation.3 | async-start | bytes 786432 | tf_op jit(solution)/shard_map/all_to_all | solution.py:506
  134.9 12.4 %ahead3.1 = (f32[8,8,128]{2,1,0:T(8,128)}, s32[8,32]{1,0:T(8,128)}) custom-call(s32[2]{0:T(128)} %pad_add_fusion.own, f32[16,120,128]{2,1,0:T(8,128)} %bitcast.8, f32[16,112,128]{2,1,0:T(8,128)} %copy-done, s32[16]{0:T(128)} %lev.15, s32[256]{0:T(256)} %convert_element_type.8.levall, s32[16]{0:T(128)} %partner.7, f32[16,8,128]{2,1,0:T(8,128)} %get-tuple-element.34.state.state_in), custom_call_target="tpu_custom_call" | custom-call | tf_op jit(solution)/shard_map/ahead3/pallas_call | solution.py:533
  147.3 6.0 %all-to-all-done.3.got = f32[256,1,384]{2,1,0:T(1,128)S(1)} async-done(((f32[256,1,384]{2,1,0:T(1,128)}), f32[256,1,384]{2,1,0:T(1,128)S(1)}, u32[]{:S(2)}, u32[]{:S(2)}) %all-to-all-start.3) | async-done | bytes 393248 | tf_op jit(solution)/shard_map/all_to_all | solution.py:506
  153.4 0.0 copy-start.1
  153.4 0.8 copy-done.1
  154.1 12.6 %after3.1 = f32[16,1,1152]{2,1,0:T(1,128)} custom-call(f32[256,1,384]{2,1,0:T(1,128)} %copy-done.1, s32[16]{0:T(128)} %lev.15, f32[16,8,128]{2,1,0:T(8,128)} %get-tuple-element.34.state.state_in, f32[8,8,128]{2,1,0:T(8,128)} %get-tuple-element.35.sums, s32[8,32]{1,0:T(8,128)} %get-tuple-element.36.plan, f32[8,8,256]{2,1,0:T(8,128)} %get-tuple-element.31.rest_0_, ...), custom_call_target="tpu_custom_call" | custom-call | tf_op jit(solution)/shard_map/after3/pallas_call | solution.py:554
  166.7 13.9 %all_to_all.25.got = f32[16,1,1152]{2,1,0:T(1,128)} all-to-all(f32[16,1,1152]{2,1,0:T(1,128)} %after3.1), channel_id=1, replica_groups=mesh['blk'=16,'grp'=16] {'grp'}, dimensions={0} | all-to-all | bytes 147456 | tf_op jit(solution)/shard_map/all_to_all | solution.py:506
  180.6 2.5 %last.1 = (f32[6,2048]{1,0:T(8,128)}, f32[6,2048]{1,0:T(8,128)}, f32[6,2048]{1,0:T(8,128)}) custom-call(f32[16,1,1152]{2,1,0:T(1,128)} %all_to_all.25.got, f32[6,2048]{1,0:T(8,128)} %ps.3, f32[6,2048]{1,0:T(8,128)} %fr.3, f32[6,2048]{1,0:T(8,128)} %irr.1, s32[8,32]{1,0:T(8,128)} %get-tuple-element.36.plan), custom_call_target="tpu_custom_call" | custom-call | tf_op jit(solution)/shard_map/last/pallas_call | solution.py:574
Async XLA Ops:
  4.1 7.6 %copy-start.4 = (f32[120,128]{1,0:T(8,128)S(1)}, f32[120,128]{1,0:T(8,128)}, u32[]{:S(2)}) copy-start(f32[120,128]{1,0:T(8,128)} %get-tuple-element.20) | copy-start | bytes 184324
  4.1 48.4 %all-to-all-start.1 = ((f32[16,112,128]{2,1,0:T(8,128)}), f32[16,112,128]{2,1,0:T(8,128)S(1)}, u32[]{:S(2)}, u32[]{:S(2)}) async-start(f32[16,112,128]{2,1,0:T(8,128)} %broadcast_in_dim.10), calls=%async_computation.1 | async-start | bytes 1835008 | tf_op jit(solution)/shard_map/all_to_all | solution.py:506
  52.6 13.6 %copy-start = (f32[16,112,128]{2,1,0:T(8,128)}, f32[16,112,128]{2,1,0:T(8,128)S(1)}, u32[]{:S(2)}) copy-start(f32[16,112,128]{2,1,0:T(8,128)S(1)} %all-to-all-done.1.rates) | copy-start | bytes 2752516
  52.6 27.7 %all-to-all-start = ((f32[256,1,256]{2,1,0:T(1,128)}), f32[256,1,256]{2,1,0:T(1,128)S(1)}, u32[]{:S(2)}, u32[]{:S(2)}) async-start(f32[256,1,256]{2,1,0:T(1,128)} %get-tuple-element.22), calls=%async_computation | async-start | bytes 524288 | tf_op jit(solution)/shard_map/all_to_all | solution.py:506
  80.2 0.7 copy-start.3
  90.4 29.2 %all-to-all-start.2 = ((f32[256,1,384]{2,1,0:T(1,128)}), f32[256,1,384]{2,1,0:T(1,128)S(1)}, u32[]{:S(2)}, u32[]{:S(2)}) async-start(f32[256,1,384]{2,1,0:T(1,128)} %get-tuple-element.27), calls=%async_computation.2 | async-start | bytes 786432 | tf_op jit(solution)/shard_map/all_to_all | solution.py:506
  119.6 0.7 copy-start.2
  128.9 24.5 %all-to-all-start.3 = ((f32[256,1,384]{2,1,0:T(1,128)}), f32[256,1,384]{2,1,0:T(1,128)S(1)}, u32[]{:S(2)}, u32[]{:S(2)}) async-start(f32[256,1,384]{2,1,0:T(1,128)} %get-tuple-element.33), calls=%async_computation.3 | async-start | bytes 786432 | tf_op jit(solution)/shard_map/all_to_all | solution.py:506
  153.4 0.8 copy-start.1

commit v4 on v3

v4 whole, which is shorter than its diff:
```python
import functools
import jax
import jax.numpy as jnp
from jax import lax
from jax.experimental import pallas as pl
from jax.experimental.pallas import tpu as pltpu
from jax.sharding import PartitionSpec as P

WIDE = 0.04
CLOSE = 0.0001
TICK = 0.125
NB = 16
BS = 128
W = NB * BS
F32 = jnp.float32
CAPS = (4, 6, 4, 8)
TOP = (0, 1, 0, 2)
SENT = (-1, 0, 1, 1)
SLOTS = (0, 4, 8, 8)

VMEM = pl.BlockSpec(memory_space=pltpu.VMEM)
SMEM = pl.BlockSpec(memory_space=pltpu.SMEM)


def pair(target, source, mass, soften, acc):
    r = [source[c] - target[c] for c in range(3)]
    w = [source[c] - target[c] for c in range(3, 6)]
    d = (r[0] * r[0] + soften) + r[1] * r[1] + r[2] * r[2]
    s = lax.rsqrt(d)
    s2 = s * s
    weight = (mass * s) * s2
    q = (r[0] * w[0] + r[1] * w[1] + r[2] * w[2]) * (s2 * 3.0)
    acc = list(acc)
    for c in range(3):
        acc[c] = acc[c] + weight * r[c]
        acc[3 + c] = acc[3 + c] + weight * (w[c] - q * r[c])
    return tuple(acc)


def pair_split(target, source, mass, acc):
    r = [source[c] - target[c] for c in range(3)]
    w = [source[c] - target[c] for c in range(3, 6)]
    dd = r[0] * r[0] + r[1] * r[1] + r[2] * r[2]
    rw = (r[0] * w[0] + r[1] * w[1] + r[2] * w[2]) * 3.0
    acc = list(acc)
    for soften, sign in ((CLOSE, 1.0), (WIDE, -1.0)):
        s = lax.rsqrt(dd + soften)
        s2 = s * s
        weight = (mass * s) * (s2 * sign)
        q = rw * s2
        for c in range(3):
            acc[c] = acc[c] + weight * r[c]
            acc[3 + c] = acc[3 + c] + weight * (w[c] - q * r[c])
    return tuple(acc)


def zeros():
    return tuple(jnp.zeros((8, 128), F32) for _ in range(6))


BLOCK, PLACE, LEVEL, SHARD, ROW, HERE, COUNT = range(7)


def fill_slots(lev, top, cap, plan):
    for s in range(cap):
        plan[BLOCK, s] = 0
        plan[PLACE, s] = -1000
        plan[LEVEL, s] = 0
    count = jnp.int32(0)
    ones = [jnp.int32(0), jnp.int32(4)]
    for k in range(NB):
        level = lev[k]
        live = level <= top
        place = jnp.where(level == 0, ones[0], jnp.where(level == 1, ones[1], -1000))
        plan[BLOCK, count] = k
        plan[PLACE, count] = jnp.where(live, place, -1000)
        plan[LEVEL, count] = jnp.where(live, level, 0)
        count = count + live.astype(jnp.int32)
        ones[0] = ones[0] + (level == 0).astype(jnp.int32)
        ones[1] = ones[1] + (level == 1).astype(jnp.int32)
    plan[COUNT, 0] = count


def fill_near(plan, cap, own, levall, partner, sent):
    def slot(s, _):
        k = plan[BLOCK, s]
        q = partner[k] // NB
        level = levall[q, k]
        place = jnp.where(level == 0, 0, 4)
        for e in range(NB):
            place = place + ((levall[q, e] == level) & (e < k)).astype(jnp.int32)
        ours = plan[LEVEL, s] <= sent
        theirs = (q != own) & (level <= sent)
        for e, (b, row, here) in enumerate(((own, plan[PLACE, s], ours), (q, place, theirs))):
            plan[SHARD, 2 * s + e] = b
            plan[ROW, 2 * s + e] = jnp.clip(jnp.where(here, row, 0), 0, 3 if sent == 0 else 7)
            plan[HERE, 2 * s + e] = here.astype(jnp.int32)
        return 0

    lax.fori_loop(0, cap, slot, 0)


def span_of(level):
    return jnp.where(level == 0, TICK, jnp.where(level == 1, 2 * TICK, 4 * TICK)).astype(F32)


XS, MS, VS, AS, JS = (0, 1, 2), 3, (4, 5, 6), (8, 9, 10), (11, 12, 13)


def columns(tile):
    return tuple(
        [tile[:, c : c + 1] for c in group] for group in (XS, VS, AS, JS)
    )


def forecast(x, v, a, j, t):
    t2 = t * t * 0.5
    t3 = t * t * t * (1.0 / 6.0)
    xp = [x[c] + v[c] * t + a[c] * t2 + j[c] * t3 for c in range(3)]
    vp = [v[c] + a[c] * t + j[c] * t2 for c in range(3)]
    return xp + vp


class Forecast:
    def __init__(self, t):
        row = lax.broadcasted_iota(jnp.int32, (8, 128), 0)
        zero = jnp.zeros((8, 128), F32)
        low = row < 3
        high = (row > 3) & (row < 7)
        t2 = t * t * 0.5
        t3 = t * t * t / 6.0
        self.c1 = jnp.where(low, t, zero)
        self.c2 = jnp.where(low | high, t2, zero)
        self.c3 = jnp.where(low, t3, jnp.where(high, t, zero))

    def __call__(self, table, rates, b, k):
        first = table[b, pl.ds(7 * k, 8), :]
        second = rates[b, pl.ds(pl.multiple_of(8 * k, 8), 8), :]
        value = first + self.c1 * pltpu.roll(first, 4, 0)
        return value + self.c2 * second + self.c3 * pltpu.roll(second, 4, 0)


def fill_sources(table, rates, predicted, ahead, levall, sent):
    def shard(b, count):
        for k in range(NB):
            predicted[count] = ahead(table, rates, b, k)
            count = count + (levall[b, k] > sent).astype(jnp.int32)
        return count

    count = lax.fori_loop(0, table.shape[0], shard, jnp.int32(0))
    for e in range(NB):
        predicted[count + e] = jnp.zeros((8, 128), F32)
    return count


def target_of(state, plan, s):
    x, v, a, j = columns(state[plan[BLOCK, s]])
    ahead = forecast(x, v, a, j, span_of(plan[LEVEL, s]))
    return [jnp.broadcast_to(value, (8, 128)) for value in ahead]


def broad(row):
    return jnp.broadcast_to(row, (8, 128))


def tile_rows(tiles, at, start=0):
    rows = [broad(tiles[at, pl.ds(start + r, 1), :]) for r in (0, 1, 2, 4, 5, 6)]
    return rows, broad(tiles[at, pl.ds(start + 3, 1), :])


def slot_pairs(cap, state, plan, sweep, prepare, close, sink, carry):
    def two(p, carry):
        goal = [target_of(state, plan, 2 * p + e) for e in range(2)]
        prepare(p)
        acc = sweep(goal)
        for e in range(2):
            s = 2 * p + e
            near = zeros()
            for part in range(2):
                rows, mass, wanted = close(s, e, part)
                near = pair_split(goal[e], rows, mass * jnp.where(wanted, 1.0, 0.0).astype(F32), near)
            total, inner = (
                [jnp.sum(value, axis=1, keepdims=True) for value in group] for group in (acc[e], near)
            )
            carry = sink(s, total, inner, carry)
        return carry

    return lax.fori_loop(0, cap // 2, two, carry)


def sweep_table(groups, load):
    def sweep(goal):
        def group(b, acc):
            for k in range(NB):
                rows, mass = load(b, k)
                acc = tuple(pair(goal[e], rows, mass, WIDE, acc[e]) for e in range(2))
            return acc

        return lax.fori_loop(0, groups, group, (zeros(), zeros()))

    return sweep


def fill_received(got, turned):
    senders, _, lanes = got.shape
    for t in range(lanes // 128):
        for half in range(senders // 128):
            part = got[pl.ds(half * 128, 128), 0, pl.ds(t * 128, 128)]
            turned[pl.ds(t * 16, 16), :, pl.ds(half * 128, 128)] = part.T.reshape(16, 8, 128)


def sweep_received(turned, mass, slots_in, used):
    def sweep(goal):
        def slot(s, acc):
            for i in range(8):
                for half in range(turned.shape[2] // 128):
                    at = pl.ds(half * 128, 128)
                    rows = [broad(turned[f * slots_in + s, i : i + 1, at]) for f in range(6)]
                    m = broad(mass[s, i : i + 1, at])
                    acc = tuple(pair(goal[e], rows, m, WIDE, acc[e]) for e in range(2))
            return acc

        return lax.fori_loop(0, used, slot, (zeros(), zeros()))

    return sweep


def gather_blocks(turned, mass, slots_in, plan, near, p):
    lane = lax.broadcasted_iota(jnp.int32, (8, 128), 1)
    row = lax.broadcasted_iota(jnp.int32, (8, 128), 0)
    keep = lane // 16 == row
    for item in range(4):
        b = plan[SHARD, 4 * p + item]
        place = plan[ROW, 4 * p + item]
        half = pl.ds(pl.multiple_of((b // 8) * 128, 128), 128)
        shift = lax.rem(128 - lax.rem(b, 8) * 16, 128)
        for r, f in ((0, 0), (1, 1), (2, 2), (4, 3), (5, 4), (6, 5), (3, None)):
            tile = mass[place, :, half] if f is None else turned[f * slots_in + place, :, half]
            tile = pltpu.roll(pltpu.roll(tile, shift, 1), 0, 1, stride=16, stride_axis=0)
            near[item, r : r + 1, :] = jnp.sum(jnp.where(keep, tile, 0.0), axis=0, keepdims=True)


def fill_tiles(parts, tiles, width):
    per = 128 // width
    tiles = list(tiles)
    lane = lax.broadcasted_iota(jnp.int32, (8, 128), 1)
    for f, slot, column in parts:
        t = f // per
        tiles[t] = jnp.where(lane == (f % per) * width + slot * 8, column, tiles[t])
    return tiles


def blank(count):
    return [jnp.zeros((8, 128), F32) for _ in range(count)]


def place_tiles(tiles):
    tiles = [pltpu.roll(tile, 0, 1, stride=1, stride_axis=0) for tile in tiles]
    return [jnp.sum(tile, axis=0, keepdims=True) for tile in tiles]


def send(tiles, pay):
    for t, tile in enumerate(tiles):
        full = jnp.broadcast_to(tile[None], (pay.shape[0], 1, 128))
        pay[:, :, pl.ds(t * 128, 128)] = full


def corrector(step, state, plan, sums):
    lane = lax.broadcasted_iota(jnp.int32, (8, 128), 1)

    def sink(s, total, inner, carry):
        k = plan[BLOCK, s]
        t = span_of(plan[LEVEL, s])
        tile = state[k]
        x, v, a, j = columns(tile)
        if sums is not None:
            before = sums[s]
            total = [total[c] + before[:, c : c + 1] for c in range(6)]
            inner = [inner[c] + before[:, 8 + c : 9 + c] for c in range(6)]
        total = [total[c] + inner[c] for c in range(6)]
        half = t * 0.5
        twelfth = t * t * (1.0 / 12.0)
        v1 = [v[c] + (a[c] + total[c]) * half + (j[c] - total[3 + c]) * twelfth for c in range(3)]
        x1 = [x[c] + (v[c] + v1[c]) * half + (a[c] - total[c]) * twelfth for c in range(3)]
        if step == 3:
            parts = [(f, s, column) for f, column in enumerate(x1 + v1 + total + inner)]
            return tuple(fill_tiles(parts, carry, 64))
        fresh = tile
        for at, column in zip(XS + VS + AS + JS, x1 + v1 + total):
            fresh = jnp.where(lane == at, column, fresh)
        state[jnp.where(s < plan[COUNT, 0], k, NB)] = fresh
        ahead = forecast(x1, v1, total[:3], total[3:], TICK)
        if step == 0:
            ahead = ahead + [tile[:, MS : MS + 1]]
        parts = [(f, plan[PLACE, s], column) for f, column in enumerate(ahead)]
        return tuple(fill_tiles(parts, carry, 32 if step == 0 else 64))

    return sink


def fill_later(state, lev, later):
    parts = []
    seen = jnp.int32(4)
    for k in range(NB):
        one = lev[k] == 1
        mark = jnp.where(one, seen, -1000)
        x, v, a, j = columns(state[k])
        for f, column in enumerate(forecast(x, v, a, j, 2 * TICK)):
            parts.append((f, mark, column))
        seen = seen + one.astype(jnp.int32)
    for t, tile in enumerate(fill_tiles(parts, blank(3), 64)):
        later[t] = tile


def pack_kernel(ps, fr, mass, lev, first, rates, own):
    x, v, a, j = ps[0:3, :], ps[3:6, :], fr[0:3, :], fr[3:6, :]
    t2 = TICK * TICK * 0.5
    xp = x + v * TICK + a * t2 + j * (TICK * TICK * TICK / 6.0)
    vp = v + a * TICK + j * t2
    ap = a + j * TICK
    lane = lax.broadcasted_iota(jnp.int32, (8, BS), 1)
    levels = jnp.zeros((8, BS), F32)
    for k in range(NB):
        levels = jnp.where(lane == k, lev[k].astype(F32), levels)
    first[7 * NB : 7 * NB + 8, :] = levels
    blank_row = jnp.zeros((1, BS), F32)
    for k in range(NB):
        at = slice(k * BS, k * BS + BS)
        first[7 * k : 7 * k + 3, :] = xp[:, at]
        first[7 * k + 3 : 7 * k + 4, :] = mass[:, at]
        first[7 * k + 4 : 7 * k + 7, :] = vp[:, at]
        rates[0, 8 * k : 8 * k + 3, :] = ap[:, at]
        rates[0, 8 * k + 3 : 8 * k + 4, :] = blank_row
        rates[0, 8 * k + 4 : 8 * k + 7, :] = j[:, at]
        rates[0, 8 * k + 7 : 8 * k + 8, :] = blank_row
        own[k] = jnp.zeros((16, BS), F32)
        own[k, 0:3, :] = x[:, at]
        own[k, 3:4, :] = mass[:, at]
        own[k, 4:7, :] = v[:, at]
        own[k, 8:14, :] = fr[:, at]
    for b in range(1, rates.shape[0]):
        rates[b] = rates[0]


def first_kernel(me, col, table, mine, lev, partner, state, pay, turned, plan):
    me = me[0]
    col = pl.multiple_of(col[0] * 8, 8)
    fill_slots(lev, TOP[0], CAPS[0], plan)
    for k in range(NB):
        turned[k, :, 0:16] = mine[k].T
    for k in range(NB):
        state[k] = turned[k, pl.ds(col, 8), :]
    masses = []
    seen = jnp.int32(0)
    for k in range(NB):
        one = lev[k] == 1
        masses.append((7, jnp.where(one, seen, -1000), state[k][:, MS : MS + 1]))
        seen = seen + one.astype(jnp.int32)

    def close(s, e, part):
        k = plan[BLOCK, s]
        b = partner[k] // NB if part else me
        rows, mass = tile_rows(table, b, 7 * k)
        return rows, mass, b != me if part else jnp.bool_(True)

    tiles = slot_pairs(
        CAPS[0], state, plan,
        sweep_table(table.shape[0], lambda b, k: tile_rows(table, b, 7 * k)),
        lambda p: None, close, corrector(0, state, plan, None),
        tuple(fill_tiles(masses, blank(2), 32)),
    )
    send(place_tiles(tiles), pay)


def ahead_kernel(step, me, table, rates, lev, levall, partner, state, sums, plan, *rest):
    later = None
    if step == 2:
        later, *rest = rest
    predicted, near = rest
    me = me[0]
    cap = CAPS[step]
    fill_slots(lev, TOP[step], cap, plan)
    fill_near(plan, cap, me, levall, partner, SENT[step])
    ahead = Forecast(step * TICK)
    used = fill_sources(table, rates, predicted, ahead, levall, SENT[step])
    lane = lax.broadcasted_iota(jnp.int32, (8, 128), 1)

    def prepare(p):
        for item in range(4):
            k = plan[BLOCK, 2 * p + item // 2]
            near[item] = ahead(table, rates, plan[SHARD, 4 * p + item], k)

    def close(s, e, part):
        rows, mass = tile_rows(near, 2 * e + part)
        other = plan[SHARD, 2 * s + 1] != me if part else jnp.bool_(True)
        return rows, mass, other & (plan[HERE, 2 * s + part] == 0)

    def sink(s, total, inner, carry):
        tile = jnp.zeros((8, 128), F32)
        for at, group in ((0, total), (8, inner)):
            for c in range(6):
                tile = jnp.where(lane == at + c, group[c], tile)
        sums[s] = tile
        return carry

    groups = (used + NB - 1) // NB
    sweep = sweep_table(groups, lambda b, k: tile_rows(predicted, b * NB + k))
    slot_pairs(cap, state, plan, sweep, prepare, close, sink, 0)
    if step == 2:
        fill_later(state, lev, later)
    if step == 1:

        def shard(b, most):
            here = jnp.int32(0)
            for k in range(NB):
                here = here + (levall[b, k] == 1).astype(jnp.int32)
            return jnp.maximum(most, here)

        plan[COUNT, 1] = lax.fori_loop(0, table.shape[0], shard, jnp.int32(0))


def after_kernel(step, got, state_in, sums, plan, *rest):
    later = None
    used = SLOTS[step]
    if step > 1:
        masses, before, *rest = rest
        used = jnp.minimum(4 + before[COUNT, 1], used)
    if step == 2:
        later, *rest = rest
    if step == 3:
        state = state_in
    else:
        state, *rest = rest
    pay, *rest = rest
    if step == 1:
        masses, *rest = rest
    near, turned = rest
    if step < 3:
        state[...] = state_in[...]
    fill_received(got, turned)
    if step == 1:
        masses[0:4] = turned[24:28]
        masses[4:8] = turned[28:32]

    def close(s, e, part):
        rows, mass = tile_rows(near, 2 * e + part)
        return rows, mass, plan[HERE, 2 * s + part] == 1

    tiles = slot_pairs(
        CAPS[step], state, plan,
        sweep_received(turned, masses, SLOTS[step], used),
        lambda p: gather_blocks(turned, masses, SLOTS[step], plan, near, p),
        close, corrector(step, state, plan, sums),
        tuple([later[t] for t in range(3)] if step == 2 else blank(9 if step == 3 else 3)),
    )
    send(place_tiles(tiles), pay)


def last_kernel(got, ps, fr, irr, plan, kin, comb, close):
    count = plan[COUNT, 0]
    kin[...] = ps[...]
    comb[...] = fr[...]
    close[...] = irr[...]
    senders = got.shape[0]
    lane = lax.broadcasted_iota(jnp.int32, (senders, 128), 1)
    row = lax.broadcasted_iota(jnp.int32, (senders, 128), 0)
    spread = [pltpu.roll(got[:, 0, pl.ds(t * 128, 128)], 0, 1, stride=8, stride_axis=0) for t in range(9)]
    for s in range(CAPS[3]):
        rows = []
        for f in range(18):
            t, e = divmod(f, 2)
            start = e * 64 + s * 8
            keep = (lane + (128 - start)) % 128 // 8 == row
            value = jnp.sum(jnp.where(keep, spread[t], 0.0), axis=0, keepdims=True)
            rows.append(pltpu.roll(value, (128 - start) % 128, 1))
        at = pl.ds(pl.multiple_of(plan[BLOCK, s] * BS, BS), BS)

        @pl.when(s < count)
        def _(at=at, rows=rows):
            for f, value in enumerate(rows):
                out = (kin, comb, close)[f // 6]
                out[f % 6 : f % 6 + 1, at] = value


def body(phase_space, force_rates, irregular, stellar_masses, levels, active, partner):
    shards = lax.axis_size("blk")
    columns_ = lax.axis_size("grp")
    everyone = shards * columns_
    me = lax.axis_index("blk").astype(jnp.int32).reshape(1)
    col = lax.axis_index("grp").astype(jnp.int32).reshape(1)
    tiles = lambda count: pltpu.VMEM((count, 8, 128), F32)
    array = lambda *shape: jax.ShapeDtypeStruct(shape, F32)
    plan_shape = jax.ShapeDtypeStruct((8, 32), jnp.int32)
    state_shape = array(NB + 1, 8, 128)

    def exchange(pay, axis):
        return lax.all_to_all(pay, axis, split_axis=0, concat_axis=0, tiled=True)

    packed, rates, mine = pl.pallas_call(
        pack_kernel,
        out_shape=(array(7 * NB + 8, BS), array(shards, 8 * NB, BS), array(NB, 16, BS)),
        in_specs=[VMEM, VMEM, VMEM, SMEM],
        out_specs=(VMEM, VMEM, VMEM),
        name="pack",
    )(phase_space, force_rates, stellar_masses[None, :], levels)
    table = lax.all_gather(packed, "blk", axis=0, tiled=False)
    levall = table[:, 7 * NB, :NB].astype(jnp.int32)
    table, rates = lax.optimization_barrier((table, rates))
    rates = exchange(rates, "blk")
    state, pay = pl.pallas_call(
        first_kernel,
        out_shape=(state_shape, array(everyone, 1, 256)),
        in_specs=[SMEM, SMEM, VMEM, VMEM, SMEM, SMEM],
        out_specs=(VMEM, VMEM),
        scratch_shapes=[pltpu.VMEM((NB, 128, 128), F32), pltpu.SMEM((8, 32), jnp.int32)],
        name="first",
    )(me, col, table, mine, levels, partner)
    masses = before = None
    for step in (1, 2, 3):
        cap = CAPS[step]
        lanes = (0, 256, 384, 384)[step]
        got = exchange(pay, ("blk", "grp"))
        outs = pl.pallas_call(
            functools.partial(ahead_kernel, step),
            out_shape=(array(cap, 8, 128), plan_shape) + ((array(3, 8, 128),) if step == 2 else ()),
            in_specs=[SMEM, VMEM, VMEM, SMEM, SMEM, SMEM, VMEM],
            out_specs=(VMEM, SMEM) + ((VMEM,) if step == 2 else ()),
            scratch_shapes=[tiles(shards * NB + NB), tiles(4)],
            name=f"ahead{step}",
        )(me, table, rates, levels, levall, partner, state)
        sums, plan = outs[:2]
        ins = (got, state, sums, plan)
        specs = [VMEM, VMEM, VMEM, SMEM]
        if step > 1:
            ins += (masses, before)
            specs += [VMEM, SMEM]
        if step == 2:
            ins += (outs[2],)
            specs += [VMEM]
        pay_shape = array(everyone if step < 3 else columns_, 1, (0, 384, 384, 1152)[step])
        out_shape = {
            1: (state_shape, pay_shape, array(8, 8, everyone)), 2: (state_shape, pay_shape), 3: (pay_shape,),
        }[step]
        outs = pl.pallas_call(
            functools.partial(after_kernel, step),
            out_shape=out_shape,
            in_specs=specs,
            out_specs=tuple(VMEM for _ in out_shape),
            scratch_shapes=[
                tiles(4),
                pltpu.VMEM((lanes // 8, 8, everyone), F32),
            ],
            name=f"after{step}",
        )(*ins)
        if step == 1:
            state, pay, masses = outs
            before = plan
        elif step == 2:
            state, pay = outs
        else:
            (pay,) = outs
    got = exchange(pay, "grp")
    shape = array(6, W)
    return tuple(
        pl.pallas_call(
            last_kernel,
            out_shape=(shape, shape, shape),
            in_specs=[VMEM, VMEM, VMEM, VMEM, SMEM],
            out_specs=(VMEM, VMEM, VMEM),
            name="last",
        )(got, phase_space, force_rates, irregular, plan)
    )


def solution(mesh):
    in_specs = (
        P(None, "blk"), P(None, "blk"), P(None, "blk"), P("blk"), P("blk"), P(None, "blk"), P("blk"),
    )
    out_specs = (P(None, "blk"), P(None, "blk"), P(None, "blk"))
    return jax.shard_map(body, mesh=mesh, in_specs=in_specs, out_specs=out_specs, check_vma=False)
```

time: 184 us -> 174 us (0.946)
  Pallas kernels: 76.4 us -> 72.3 us
  blocking collectives: 44.5 us -> 40.7 us
  waiting for transfers between devices: 19.2 us -> 21.6 us
    pallas_call x3, Pallas kernels: 30.6 us -> 22.9 us  [body(): pl.pallas_call(functools.partial(after_kernel, step), out_shape=out_shape...]
    all_gather x1, blocking collectives: 30.7 us -> 25.4 us  [body(): table = lax.all_gather(packed, 'blk', axis=0, tiled=False)]
    pallas_call x3, Pallas kernels: 31.6 us -> 34.8 us  [body(): pl.pallas_call(functools.partial(ahead_kernel, step), out_shape=(array(ca...]
    all_to_all x4, waiting for transfers between devices: 19.2 us -> 21.6 us  [exchange(): return lax.all_to_all(pay, axis, split_axis=0, concat_axis=0, tiled=True)]
    broadcast_in_dim x1 -> x0, local copies, waits for them, and re-layouts: 1.85 us -> none  [body(): rates = exchange(jnp.broadcast_to(rates[None], (shards, 7 * NB, BS)), 'blk')]
  transfers between devices with their start and end apart: 4 -> 4, of which waited for: 3 -> 4; matrix products, arithmetic and copies ran while one was open for 1% -> 1% of each run, Pallas kernels for 23% -> 26%
where the time goes in v4:
time: 174 us; the launch traced here: 173 us
  Pallas kernels  72.3 us (42%)
  blocking collectives  40.7 us (23%)
  starting transfers between devices  34.5 us (20%)
  waiting for transfers between devices  21.6 us (12%)
  local copies, waits for them, and re-layouts  3.06 us (2%)
    pallas_call x3, Pallas kernels, body(): pl.pallas_call(functools.partial(ahead_kernel, step), out_shape=(array(ca...  34.8 us
    all_to_all x4, starting transfers between devices, exchange(): return lax.all_to_all(pay, axis, split_axis=0, concat_axis=0, tiled=True)  34.5 us
    all_gather x1, blocking collectives, body(): table = lax.all_gather(packed, 'blk', axis=0, tiled=False)  25.4 us
    pallas_call x3, Pallas kernels, body(): pl.pallas_call(functools.partial(after_kernel, step), out_shape=out_shape...  22.9 us
    all_to_all x4, waiting for transfers between devices, exchange(): return lax.all_to_all(pay, axis, split_axis=0, concat_axis=0, tiled=True)  21.6 us
    all_to_all x1, blocking collectives, exchange(): return lax.all_to_all(pay, axis, split_axis=0, concat_axis=0, tiled=True)  15.3 us
    pallas_call x1, Pallas kernels, body(): pl.pallas_call(first_kernel, out_shape=(state_shape, array(everyone, 1, 2...  10.1 us
  transfers between devices with their start and end apart: 4, of which 4 were waited for; matrix products, arithmetic and copies ran while one was open for 1% of the time, Pallas kernels for 26%

profile of v4, /device:TPU:1, one launch (start us, length us, event | category | flops | bytes accessed | tf_op | source)
XLA Modules:
  0.0 173.5 jit_solution(10678103384450098117)
XLA Ops:
  0.6 2.0 %pack.1 = (f32[120,128]{1,0:T(8,128)}, f32[16,128,128]{2,1,0:T(8,128)}, f32[16,16,128]{2,1,0:T(8,128)}) custom-call(f32[6,2048]{1,0:T(8,128)} %ps.3, f32[6,2048]{1,0:T(8,128)} %fr.3, f32[1,2048]{1,0:T(1,128)} %bitcast.13, s32[16]{0:T(128)} %lev.9), custom_call_target="tpu_custom_call" | custom-call | tf_op jit(solution)/shard_map/pack/pallas_call | solution.py:499
  2.7 25.4 %all-gather = f32[1920,128]{1,0:T(8,128)} all-gather(f32[120,128]{1,0:T(8,128)} %get-tuple-element.22), channel_id=2, replica_groups=mesh['blk'=16,'grp'=16] {'blk'}, dimensions={0}, use_global_device_ids=true | all-gather | bytes 1044480 | tf_op jit(solution)/shard_map/all_gather | solution.py:506
  28.1 3.6 %all-to-all-start.1 = ((f32[16,128,128]{2,1,0:T(8,128)}), f32[16,128,128]{2,1,0:T(8,128)S(1)}, u32[]{:S(2)}, u32[]{:S(2)}) async-start(f32[16,128,128]{2,1,0:T(8,128)} %get-tuple-element.28), calls=%async_computation.1 | async-start | bytes 2097152 | tf_op jit(solution)/shard_map/all_to_all | solution.py:497
  31.7 10.1 %first.1 = (f32[17,8,128]{2,1,0:T(8,128)}, f32[256,1,256]{2,1,0:T(1,128)}) custom-call(s32[1]{0:T(128)} %bitcast.me, s32[1]{0:T(128)} %bitcast.1.col, f32[16,120,128]{2,1,0:T(8,128)} %bitcast.7, f32[16,16,128]{2,1,0:T(8,128)} %get-tuple-element.25.mine, s32[16]{0:T(128)} %lev.9, s32[16]{0:T(128)} %partner.7), custom_call_target="tpu_custom_call" | custom-call | tf_op jit(solution)/shard_map/first/pallas_call | solution.py:510
  41.7 5.5 %all-to-all-done.1.rates = f32[16,128,128]{2,1,0:T(8,128)S(1)} async-done(((f32[16,128,128]{2,1,0:T(8,128)}), f32[16,128,128]{2,1,0:T(8,128)S(1)}, u32[]{:S(2)}, u32[]{:S(2)}) %all-to-all-start.1) | async-done | bytes 1048608 | tf_op jit(solution)/shard_map/all_to_all | solution.py:497
  47.2 0.0 copy-start
  47.2 13.1 %all-to-all-start = ((f32[256,1,256]{2,1,0:T(1,128)}), f32[256,1,256]{2,1,0:T(1,128)S(1)}, u32[]{:S(2)}, u32[]{:S(2)}) async-start(f32[256,1,256]{2,1,0:T(1,128)} %get-tuple-element.26), calls=%async_computation | async-start | bytes 524288 | tf_op jit(solution)/shard_map/all_to_all | solution.py:497
  60.4 0.8 slice.4
  61.2 0.6 convert_bitcast_fusion.levall
  61.8 0.0 copy-done
  61.8 12.2 %ahead1.1 = (f32[6,8,128]{2,1,0:T(8,128)}, s32[8,32]{1,0:T(8,128)}) custom-call(s32[1]{0:T(128)} %bitcast.me, f32[16,120,128]{2,1,0:T(8,128)} %bitcast.9, f32[16,128,128]{2,1,0:T(8,128)} %copy-done, s32[16]{0:T(128)} %lev.9, s32[16,16]{1,0:T(8,128)} %convert_bitcast_fusion.levall, s32[16]{0:T(128)} %partner.7, f32[17,8,128]{2,1,0:T(8,128)} %get-tuple-element.27.state.state_in), custom_call_target="tpu_custom_call" | custom-call | tf_op jit(solution)/shard_map/ahead1/pallas_call | solution.py:523
  74.0 1.9 %all-to-all-done.got = f32[256,1,256]{2,1,0:T(1,128)S(1)} async-done(((f32[256,1,256]{2,1,0:T(1,128)}), f32[256,1,256]{2,1,0:T(1,128)S(1)}, u32[]{:S(2)}, u32[]{:S(2)}) %all-to-all-start) | async-done | bytes 262176 | tf_op jit(solution)/shard_map/all_to_all | solution.py:497
  76.0 0.0 copy-start.3
  76.0 0.7 copy-done.3
  76.7 7.2 %after1.1 = (f32[17,8,128]{2,1,0:T(8,128)}, f32[256,1,384]{2,1,0:T(1,128)}, f32[8,8,256]{2,1,0:T(8,128)}) custom-call(f32[256,1,256]{2,1,0:T(1,128)} %copy-done.3, f32[17,8,128]{2,1,0:T(8,128)} %get-tuple-element.27.state.state_in, f32[6,8,128]{2,1,0:T(8,128)} %get-tuple-element.29.sums, s32[8,32]{1,0:T(8,128)} %get-tuple-element.30.plan.rest_1_), custom_call_target="tpu_custom_call" | custom-call | tf_op jit(solution)/shard_map/after1/pallas_call | solution.py:544
  83.9 11.8 %all-to-all-start.2 = ((f32[256,1,384]{2,1,0:T(1,128)}), f32[256,1,384]{2,1,0:T(1,128)S(1)}, u32[]{:S(2)}, u32[]{:S(2)}) async-start(f32[256,1,384]{2,1,0:T(1,128)} %get-tuple-element.31), calls=%async_computation.2 | async-start | bytes 786432 | tf_op jit(solution)/shard_map/all_to_all | solution.py:497
  95.7 8.7 %ahead2.1 = (f32[4,8,128]{2,1,0:T(8,128)}, s32[8,32]{1,0:T(8,128)}, f32[3,8,128]{2,1,0:T(8,128)}) custom-call(s32[1]{0:T(128)} %bitcast.me, f32[16,120,128]{2,1,0:T(8,128)} %bitcast.10, f32[16,128,128]{2,1,0:T(8,128)} %copy-done, s32[16]{0:T(128)} %lev.9, s32[16,16]{1,0:T(8,128)} %convert_bitcast_fusion.levall, s32[16]{0:T(128)} %partner.7, ...), custom_call_target="tpu_custom_call" | custom-call | tf_op jit(solution)/shard_map/ahead2/pallas_call | solution.py:523
  104.4 9.6 %all-to-all-done.2.got = f32[256,1,384]{2,1,0:T(1,128)S(1)} async-done(((f32[256,1,384]{2,1,0:T(1,128)}), f32[256,1,384]{2,1,0:T(1,128)S(1)}, u32[]{:S(2)}, u32[]{:S(2)}) %all-to-all-start.2) | async-done | bytes 393248 | tf_op jit(solution)/shard_map/all_to_all | solution.py:497
  114.0 0.0 copy-start.2
  114.0 0.8 copy-done.2
  114.8 6.5 %after2.1 = (f32[17,8,128]{2,1,0:T(8,128)}, f32[256,1,384]{2,1,0:T(1,128)}) custom-call(f32[256,1,384]{2,1,0:T(1,128)} %copy-done.2, f32[17,8,128]{2,1,0:T(8,128)} %get-tuple-element.32.state.state_in, f32[4,8,128]{2,1,0:T(8,128)} %get-tuple-element.33.sums, s32[8,32]{1,0:T(8,128)} %get-tuple-element.34.plan, f32[8,8,256]{2,1,0:T(8,128)} %get-tuple-element.35.rest_0_, ...), custom_call_target="tpu_custom_call" | custom-call | tf_op jit(solution)/shard_map/after2/pallas_call | solution.py:544
  121.3 5.9 %all-to-all-start.3 = ((f32[256,1,384]{2,1,0:T(1,128)}), f32[256,1,384]{2,1,0:T(1,128)S(1)}, u32[]{:S(2)}, u32[]{:S(2)}) async-start(f32[256,1,384]{2,1,0:T(1,128)} %get-tuple-element.37), calls=%async_computation.3 | async-start | bytes 786432 | tf_op jit(solution)/shard_map/all_to_all | solution.py:497
  127.2 13.9 %ahead3.1 = (f32[8,8,128]{2,1,0:T(8,128)}, s32[8,32]{1,0:T(8,128)}) custom-call(s32[1]{0:T(128)} %bitcast.me, f32[16,120,128]{2,1,0:T(8,128)} %bitcast.11, f32[16,128,128]{2,1,0:T(8,128)} %copy-done, s32[16]{0:T(128)} %lev.9, s32[16,16]{1,0:T(8,128)} %convert_bitcast_fusion.levall, s32[16]{0:T(128)} %partner.7, f32[17,8,128]{2,1,0:T(8,128)} %get-tuple-element.38.state.state_in), custom_call_target="tpu_custom_call" | custom-call | tf_op jit(solution)/shard_map/ahead3/pallas_call | solution.py:523
  141.2 4.5 %all-to-all-done.3.got = f32[256,1,384]{2,1,0:T(1,128)S(1)} async-done(((f32[256,1,384]{2,1,0:T(1,128)}), f32[256,1,384]{2,1,0:T(1,128)S(1)}, u32[]{:S(2)}, u32[]{:S(2)}) %all-to-all-start.3) | async-done | bytes 393248 | tf_op jit(solution)/shard_map/all_to_all | solution.py:497
  145.7 0.0 copy-start.1
  145.7 0.8 copy-done.1
  146.5 9.2 %after3.1 = f32[16,1,1152]{2,1,0:T(1,128)} custom-call(f32[256,1,384]{2,1,0:T(1,128)} %copy-done.1, f32[17,8,128]{2,1,0:T(8,128)} %get-tuple-element.38.state.state_in, f32[8,8,128]{2,1,0:T(8,128)} %get-tuple-element.39.sums, s32[8,32]{1,0:T(8,128)} %get-tuple-element.40.plan, f32[8,8,256]{2,1,0:T(8,128)} %get-tuple-element.35.rest_0_, ...), custom_call_target="tpu_custom_call" | custom-call | tf_op jit(solution)/shard_map/after3/pallas_call | solution.py:544
  155.7 15.3 %all_to_all.25.got = f32[16,1,1152]{2,1,0:T(1,128)} all-to-all(f32[16,1,1152]{2,1,0:T(1,128)} %after3.1), channel_id=1, replica_groups=mesh['blk'=16,'grp'=16] {'grp'}, dimensions={0} | all-to-all | bytes 147456 | tf_op jit(solution)/shard_map/all_to_all | solution.py:497
  171.0 2.5 %last.1 = (f32[6,2048]{1,0:T(8,128)}, f32[6,2048]{1,0:T(8,128)}, f32[6,2048]{1,0:T(8,128)}) custom-call(f32[16,1,1152]{2,1,0:T(1,128)} %all_to_all.25.got, f32[6,2048]{1,0:T(8,128)} %ps.3, f32[6,2048]{1,0:T(8,128)} %fr.3, f32[6,2048]{1,0:T(8,128)} %irr.1, s32[8,32]{1,0:T(8,128)} %get-tuple-element.40.plan), custom_call_target="tpu_custom_call" | custom-call | tf_op jit(solution)/shard_map/last/pallas_call | solution.py:565
Async XLA Ops:
  28.1 19.2 %all-to-all-start.1 = ((f32[16,128,128]{2,1,0:T(8,128)}), f32[16,128,128]{2,1,0:T(8,128)S(1)}, u32[]{:S(2)}, u32[]{:S(2)}) async-start(f32[16,128,128]{2,1,0:T(8,128)} %get-tuple-element.28), calls=%async_computation.1 | async-start | bytes 2097152 | tf_op jit(solution)/shard_map/all_to_all | solution.py:497
  47.2 14.6 %copy-start = (f32[16,128,128]{2,1,0:T(8,128)}, f32[16,128,128]{2,1,0:T(8,128)S(1)}, u32[]{:S(2)}) copy-start(f32[16,128,128]{2,1,0:T(8,128)S(1)} %all-to-all-done.1.rates) | copy-start | bytes 3145732
  47.2 28.7 %all-to-all-start = ((f32[256,1,256]{2,1,0:T(1,128)}), f32[256,1,256]{2,1,0:T(1,128)S(1)}, u32[]{:S(2)}, u32[]{:S(2)}) async-start(f32[256,1,256]{2,1,0:T(1,128)} %get-tuple-element.26), calls=%async_computation | async-start | bytes 524288 | tf_op jit(solution)/shard_map/all_to_all | solution.py:497
  76.0 0.7 copy-start.3
  83.9 30.2 %all-to-all-start.2 = ((f32[256,1,384]{2,1,0:T(1,128)}), f32[256,1,384]{2,1,0:T(1,128)S(1)}, u32[]{:S(2)}, u32[]{:S(2)}) async-start(f32[256,1,384]{2,1,0:T(1,128)} %get-tuple-element.31), calls=%async_computation.2 | async-start | bytes 786432 | tf_op jit(solution)/shard_map/all_to_all | solution.py:497
  114.0 0.8 copy-start.2
  121.3 24.4 %all-to-all-start.3 = ((f32[256,1,384]{2,1,0:T(1,128)}), f32[256,1,384]{2,1,0:T(1,128)S(1)}, u32[]{:S(2)}, u32[]{:S(2)}) async-start(f32[256,1,384]{2,1,0:T(1,128)} %get-tuple-element.37), calls=%async_computation.3 | async-start | bytes 786432 | tf_op jit(solution)/shard_map/all_to_all | solution.py:497
  145.7 0.8 copy-start.1

commit v5 on v4

--- a/solution.py
+++ b/solution.py
@@ -67,17 +67,20 @@
         plan[PLACE, s] = -1000
         plan[LEVEL, s] = 0
     count = jnp.int32(0)
-    ones = [jnp.int32(0), jnp.int32(4)]
-    for k in range(NB):
-        level = lev[k]
-        live = level <= top
-        place = jnp.where(level == 0, ones[0], jnp.where(level == 1, ones[1], -1000))
-        plan[BLOCK, count] = k
-        plan[PLACE, count] = jnp.where(live, place, -1000)
-        plan[LEVEL, count] = jnp.where(live, level, 0)
-        count = count + live.astype(jnp.int32)
-        ones[0] = ones[0] + (level == 0).astype(jnp.int32)
-        ones[1] = ones[1] + (level == 1).astype(jnp.int32)
+    for group in ((2,), (0, 1)) if top == 2 else ((0, 1),):
+        ones = [jnp.int32(0), jnp.int32(4)]
+        for k in range(NB):
+            level = lev[k]
+            place = jnp.where(level == 0, ones[0], jnp.where(level == 1, ones[1], -1000))
+            live = (level == 2) if group == (2,) else level <= min(top, 1)
+            plan[BLOCK, count] = k
+            plan[PLACE, count] = jnp.where(live, place, -1000)
+            plan[LEVEL, count] = jnp.where(live, level, 0)
+            count = count + live.astype(jnp.int32)
+            ones[0] = ones[0] + (level == 0).astype(jnp.int32)
+            ones[1] = ones[1] + (level == 1).astype(jnp.int32)
+        if group == (2,):
+            plan[COUNT, 2] = count
     plan[COUNT, 0] = count
 
 
@@ -121,36 +124,40 @@
     return xp + vp
 
 
-class Forecast:
-    def __init__(self, t):
-        row = lax.broadcasted_iota(jnp.int32, (8, 128), 0)
-        zero = jnp.zeros((8, 128), F32)
-        low = row < 3
-        high = (row > 3) & (row < 7)
-        t2 = t * t * 0.5
-        t3 = t * t * t / 6.0
-        self.c1 = jnp.where(low, t, zero)
-        self.c2 = jnp.where(low | high, t2, zero)
-        self.c3 = jnp.where(low, t3, jnp.where(high, t, zero))
-
-    def __call__(self, table, rates, b, k):
-        first = table[b, pl.ds(7 * k, 8), :]
-        second = rates[b, pl.ds(pl.multiple_of(8 * k, 8), 8), :]
-        value = first + self.c1 * pltpu.roll(first, 4, 0)
-        return value + self.c2 * second + self.c3 * pltpu.roll(second, 4, 0)
-
-
-def fill_sources(table, rates, predicted, ahead, levall, sent):
+QUANTITIES = 7
+
+
+def fill_sources(table, rates, predicted, t):
+    t2 = t * t * 0.5
+    t3 = t * t * t / 6.0
+
+    def shard(b, _):
+        x, m, v = [[table[b, pl.ds(NB * f, NB), :] for f in group] for group in ((0, 1, 2), (3,), (4, 5, 6))]
+        a, j = [[rates[b, pl.ds(NB * f, NB), :] for f in group] for group in ((0, 1, 2), (3, 4, 5))]
+        for c in range(3):
+            predicted[b, c] = x[c] + v[c] * t + a[c] * t2 + j[c] * t3
+            predicted[b, 4 + c] = v[c] + a[c] * t + j[c] * t2
+        predicted[b, 3] = m[0]
+        return 0
+
+    lax.fori_loop(0, table.shape[0], shard, 0)
+    for f in range(QUANTITIES):
+        predicted[table.shape[0], f] = jnp.zeros((NB, BS), F32)
+
+
+def fill_order(levall, sent, order):
+    shards = levall.shape[0]
+
     def shard(b, count):
         for k in range(NB):
-            predicted[count] = ahead(table, rates, b, k)
+            order[count] = b * NB + k
             count = count + (levall[b, k] > sent).astype(jnp.int32)
         return count
 
-    count = lax.fori_loop(0, table.shape[0], shard, jnp.int32(0))
+    count = lax.fori_loop(0, shards, shard, jnp.int32(0))
     for e in range(NB):
-        predicted[count + e] = jnp.zeros((8, 128), F32)
-    return count
+        order[count + e] = shards * NB
+    order[(shards + 2) * NB] = count
 
 
 def target_of(state, plan, s):
@@ -163,12 +170,19 @@
     return jnp.broadcast_to(row, (8, 128))
 
 
-def tile_rows(tiles, at, start=0):
-    rows = [broad(tiles[at, pl.ds(start + r, 1), :]) for r in (0, 1, 2, 4, 5, 6)]
-    return rows, broad(tiles[at, pl.ds(start + 3, 1), :])
-
-
-def slot_pairs(cap, state, plan, sweep, prepare, close, sink, carry):
+def tile_rows(tile):
+    return [broad(tile(r)) for r in (0, 1, 2, 4, 5, 6)], broad(tile(3))
+
+
+def from_table(table, b, k):
+    return tile_rows(lambda r: table[b, pl.ds(NB * r + k, 1), :])
+
+
+def from_predicted(predicted, b, k):
+    return tile_rows(lambda r: predicted[b, r, pl.ds(k, 1), :])
+
+
+def slot_pairs(first, last, state, plan, sweep, prepare, close, sink, carry):
     def two(p, carry):
         goal = [target_of(state, plan, 2 * p + e) for e in range(2)]
         prepare(p)
@@ -185,7 +199,11 @@
             carry = sink(s, total, inner, carry)
         return carry
 
-    return lax.fori_loop(0, cap // 2, two, carry)
+    return lax.fori_loop(first, last, two, carry)
+
+
+def pairs_of(plan):
+    return (plan[COUNT, 0] + 1) // 2
 
 
 def sweep_table(groups, load):
@@ -323,16 +341,14 @@
     for k in range(NB):
         levels = jnp.where(lane == k, lev[k].astype(F32), levels)
     first[7 * NB : 7 * NB + 8, :] = levels
-    blank_row = jnp.zeros((1, BS), F32)
     for k in range(NB):
         at = slice(k * BS, k * BS + BS)
-        first[7 * k : 7 * k + 3, :] = xp[:, at]
-        first[7 * k + 3 : 7 * k + 4, :] = mass[:, at]
-        first[7 * k + 4 : 7 * k + 7, :] = vp[:, at]
-        rates[0, 8 * k : 8 * k + 3, :] = ap[:, at]
-        rates[0, 8 * k + 3 : 8 * k + 4, :] = blank_row
-        rates[0, 8 * k + 4 : 8 * k + 7, :] = j[:, at]
-        rates[0, 8 * k + 7 : 8 * k + 8, :] = blank_row
+        for c in range(3):
+            first[NB * c + k : NB * c + k + 1, :] = xp[c : c + 1, at]
+            first[NB * (4 + c) + k : NB * (4 + c) + k + 1, :] = vp[c : c + 1, at]
+            rates[0, NB * c + k : NB * c + k + 1, :] = ap[c : c + 1, at]
+            rates[0, NB * (3 + c) + k : NB * (3 + c) + k + 1, :] = j[c : c + 1, at]
+        first[NB * 3 + k : NB * 3 + k + 1, :] = mass[:, at]
         own[k] = jnp.zeros((16, BS), F32)
         own[k, 0:3, :] = x[:, at]
         own[k, 3:4, :] = mass[:, at]
@@ -342,7 +358,7 @@
         rates[b] = rates[0]
 
 
-def first_kernel(me, col, table, mine, lev, partner, state, pay, turned, plan):
+def first_kernel(me, col, table, mine, lev, levall, partner, state, pay, turned, plan):
     me = me[0]
     col = pl.multiple_of(col[0] * 8, 8)
     fill_slots(lev, TOP[0], CAPS[0], plan)
@@ -360,38 +376,27 @@
     def close(s, e, part):
         k = plan[BLOCK, s]
         b = partner[k] // NB if part else me
-        rows, mass = tile_rows(table, b, 7 * k)
+        rows, mass = from_table(table, b, k)
         return rows, mass, b != me if part else jnp.bool_(True)
 
     tiles = slot_pairs(
-        CAPS[0], state, plan,
-        sweep_table(table.shape[0], lambda b, k: tile_rows(table, b, 7 * k)),
+        0, pairs_of(plan), state, plan,
+        sweep_table(table.shape[0], lambda b, k: from_table(table, b, k)),
         lambda p: None, close, corrector(0, state, plan, None),
         tuple(fill_tiles(masses, blank(2), 32)),
     )
     send(place_tiles(tiles), pay)
 
 
-def ahead_kernel(step, me, table, rates, lev, levall, partner, state, sums, plan, *rest):
-    later = None
-    if step == 2:
-        later, *rest = rest
-    predicted, near = rest
-    me = me[0]
-    cap = CAPS[step]
-    fill_slots(lev, TOP[step], cap, plan)
-    fill_near(plan, cap, me, levall, partner, SENT[step])
-    ahead = Forecast(step * TICK)
-    used = fill_sources(table, rates, predicted, ahead, levall, SENT[step])
+def ahead_sums(step, first, last, me, plan, order, predicted, state, sums):
     lane = lax.broadcasted_iota(jnp.int32, (8, 128), 1)
 
-    def prepare(p):
-        for item in range(4):
-            k = plan[BLOCK, 2 * p + item // 2]
-            near[item] = ahead(table, rates, plan[SHARD, 4 * p + item], k)
+    def load(g, e):
+        index = order[g * NB + e]
+        return from_predicted(predicted, index // NB, lax.rem(index, NB))
 
     def close(s, e, part):
-        rows, mass = tile_rows(near, 2 * e + part)
+        rows, mass = from_predicted(predicted, plan[SHARD, 2 * s + part], plan[BLOCK, s])
         other = plan[SHARD, 2 * s + 1] != me if part else jnp.bool_(True)
         return rows, mass, other & (plan[HERE, 2 * s + part] == 0)
 
@@ -403,11 +408,39 @@
         sums[s] = tile
         return carry
 
-    groups = (used + NB - 1) // NB
-    sweep = sweep_table(groups, lambda b, k: tile_rows(predicted, b * NB + k))
-    slot_pairs(cap, state, plan, sweep, prepare, close, sink, 0)
+    groups = (order[order.shape[0] - NB] + NB - 1) // NB
+    slot_pairs(first, last, state, plan, sweep_table(groups, load), lambda p: None, close, sink, 0)
+
+
+def early_pairs(plan):
+    return jnp.minimum(plan[COUNT, 2] // 2, 2)
+
+
+def ahead_kernel(step, me, table, rates, lev, levall, partner, state, *rest):
+    if step == 1:
+        sums, plan, predicted, order = rest
+    elif step == 2:
+        sums, plan, later, early, order, predicted, plan3 = rest
+    else:
+        early, order, sums, plan, predicted = rest
+    me = me[0]
+    fill_slots(lev, TOP[step], CAPS[step], plan)
+    fill_near(plan, CAPS[step], me, levall, partner, SENT[step])
+    if step < 3:
+        fill_order(levall, SENT[step], order)
+    fill_sources(table, rates, predicted, step * TICK)
+    first = 0
+    if step == 3:
+        first = early_pairs(plan)
+        sums[0:4] = early[...]
+    ahead_sums(step, first, pairs_of(plan), me, plan, order, predicted, state, sums)
     if step == 2:
         fill_later(state, lev, later)
+        fill_slots(lev, TOP[3], CAPS[3], plan3)
+        fill_near(plan3, CAPS[3], me, levall, partner, SENT[3])
+        fill_sources(table, rates, predicted, 3 * TICK)
+        early[...] = jnp.zeros((4, 8, 128), F32)
+        ahead_sums(3, 0, early_pairs(plan3), me, plan3, order, predicted, state, early)
     if step == 1:
 
         def shard(b, most):
@@ -443,11 +476,11 @@
         masses[4:8] = turned[28:32]
 
     def close(s, e, part):
-        rows, mass = tile_rows(near, 2 * e + part)
+        rows, mass = tile_rows(lambda r: near[2 * e + part, r : r + 1, :])
         return rows, mass, plan[HERE, 2 * s + part] == 1
 
     tiles = slot_pairs(
-        CAPS[step], state, plan,
+        0, pairs_of(plan), state, plan,
         sweep_received(turned, masses, SLOTS[step], used),
         lambda p: gather_blocks(turned, masses, SLOTS[step], plan, near, p),
         close, corrector(step, state, plan, sums),
@@ -498,7 +531,7 @@
 
     packed, rates, mine = pl.pallas_call(
         pack_kernel,
-        out_shape=(array(7 * NB + 8, BS), array(shards, 8 * NB, BS), array(NB, 16, BS)),
+        out_shape=(array(7 * NB + 8, BS), array(shards, 6 * NB, BS), array(NB, 16, BS)),
         in_specs=[VMEM, VMEM, VMEM, SMEM],
         out_specs=(VMEM, VMEM, VMEM),
         name="pack",
@@ -510,25 +543,42 @@
     state, pay = pl.pallas_call(
         first_kernel,
         out_shape=(state_shape, array(everyone, 1, 256)),
-        in_specs=[SMEM, SMEM, VMEM, VMEM, SMEM, SMEM],
+        in_specs=[SMEM, SMEM, VMEM, VMEM, SMEM, SMEM, SMEM],
         out_specs=(VMEM, VMEM),
         scratch_shapes=[pltpu.VMEM((NB, 128, 128), F32), pltpu.SMEM((8, 32), jnp.int32)],
         name="first",
-    )(me, col, table, mine, levels, partner)
+    )(me, col, table, mine, levels, levall, partner)
     masses = before = None
     for step in (1, 2, 3):
         cap = CAPS[step]
         lanes = (0, 256, 384, 384)[step]
         got = exchange(pay, ("blk", "grp"))
+        order_shape = ((shards + 3) * NB,)
+        ins = (me, table, rates, levels, levall, partner, state)
+        specs = [SMEM, VMEM, VMEM, SMEM, SMEM, SMEM, VMEM]
+        out_shape = (array(cap, 8, 128), plan_shape)
+        out_specs = (VMEM, SMEM)
+        scratch = [pltpu.VMEM((shards + 1, QUANTITIES, NB, BS), F32)]
+        if step == 1:
+            scratch += [pltpu.SMEM(order_shape, jnp.int32)]
+        elif step == 2:
+            out_shape += (array(3, 8, 128), array(4, 8, 128), jax.ShapeDtypeStruct(order_shape, jnp.int32))
+            out_specs += (VMEM, VMEM, SMEM)
+            scratch += [pltpu.SMEM((8, 32), jnp.int32)]
+        else:
+            ins += (early, order)
+            specs += [VMEM, SMEM]
         outs = pl.pallas_call(
             functools.partial(ahead_kernel, step),
-            out_shape=(array(cap, 8, 128), plan_shape) + ((array(3, 8, 128),) if step == 2 else ()),
-            in_specs=[SMEM, VMEM, VMEM, SMEM, SMEM, SMEM, VMEM],
-            out_specs=(VMEM, SMEM) + ((VMEM,) if step == 2 else ()),
-            scratch_shapes=[tiles(shards * NB + NB), tiles(4)],
+            out_shape=out_shape,
+            in_specs=specs,
+            out_specs=out_specs,
+            scratch_shapes=scratch,
             name=f"ahead{step}",
-        )(me, table, rates, levels, levall, partner, state)
+        )(*ins)
         sums, plan = outs[:2]
+        if step == 2:
+            early, order = outs[3:]
         ins = (got, state, sums, plan)
         specs = [VMEM, VMEM, VMEM, SMEM]
         if step > 1:

time: 174 us -> 168 us (0.966)
  the two profiles are of different devices: /device:TPU:1 before, /device:TPU:15 now
where the time goes in v5:
time: 168 us; the launch traced here: 166 us
  Pallas kernels  73.1 us (44%)
  starting transfers between devices  45.1 us (27%)
  blocking collectives  36.1 us (21%)
  waiting for transfers between devices  8.61 us (5%)
  local copies, waits for them, and re-layouts  2.21 us (1%)
    all_to_all x4, starting transfers between devices, exchange(): return lax.all_to_all(pay, axis, split_axis=0, concat_axis=0, tiled=True)  45.1 us
    pallas_call x3, Pallas kernels, body(): pl.pallas_call(functools.partial(ahead_kernel, step), out_shape=out_shape...  35.6 us
    pallas_call x3, Pallas kernels, body(): pl.pallas_call(functools.partial(after_kernel, step), out_shape=out_shape...  23 us
    all_gather x1, blocking collectives, body(): table = lax.all_gather(packed, 'blk', axis=0, tiled=False)  19.5 us
    all_to_all x1, blocking collectives, exchange(): return lax.all_to_all(pay, axis, split_axis=0, concat_axis=0, tiled=True)  16.6 us
    pallas_call x1, Pallas kernels, body(): pl.pallas_call(first_kernel, out_shape=(state_shape, array(everyone, 1, 2...  10.1 us
    all_to_all x4, waiting for transfers between devices, exchange(): return lax.all_to_all(pay, axis, split_axis=0, concat_axis=0, tiled=True)  8.61 us
  transfers between devices with their start and end apart: 4, of which 3 were waited for; matrix products, arithmetic and copies ran while one was open for 0% of the time, Pallas kernels for 27%

profile of v5, /device:TPU:15, one launch (start us, length us, event | category | flops | bytes accessed | tf_op | source)
XLA Modules:
  0.0 166.4 jit_solution(3438052189614153249)
XLA Ops:
  0.6 2.0 %pack.1 = (f32[120,128]{1,0:T(8,128)}, f32[16,96,128]{2,1,0:T(8,128)}, f32[16,16,128]{2,1,0:T(8,128)}) custom-call(f32[6,2048]{1,0:T(8,128)} %ps.3, f32[6,2048]{1,0:T(8,128)} %fr.3, f32[1,2048]{1,0:T(1,128)} %bitcast.13, s32[16]{0:T(128)} %lev.9), custom_call_target="tpu_custom_call" | custom-call | tf_op jit(solution)/shard_map/pack/pallas_call | solution.py:532
  2.6 19.5 %all-gather = f32[1920,128]{1,0:T(8,128)S(1)} all-gather(f32[120,128]{1,0:T(8,128)} %get-tuple-element.24), channel_id=2, replica_groups=mesh['blk'=16,'grp'=16] {'blk'}, dimensions={0}, use_global_device_ids=true | all-gather | bytes 1044480 | tf_op jit(solution)/shard_map/all_gather | solution.py:539
  22.1 0.0 copy-start
  22.1 7.5 %all-to-all-start.1 = ((f32[16,96,128]{2,1,0:T(8,128)}), f32[16,96,128]{2,1,0:T(8,128)S(1)}, u32[]{:S(2)}, u32[]{:S(2)}) async-start(f32[16,96,128]{2,1,0:T(8,128)} %get-tuple-element.30), calls=%async_computation.1 | async-start | bytes 1572864 | tf_op jit(solution)/shard_map/all_to_all | solution.py:530
  29.6 0.6 convert_bitcast_fusion.levall
  30.2 0.0 copy-done
  30.2 10.1 %first.1 = (f32[17,8,128]{2,1,0:T(8,128)}, f32[256,1,256]{2,1,0:T(1,128)}) custom-call(s32[1]{0:T(128)} %bitcast.me, s32[1]{0:T(128)} %bitcast.1.col, f32[16,120,128]{2,1,0:T(8,128)} %bitcast.8, f32[16,16,128]{2,1,0:T(8,128)} %get-tuple-element.27.mine, s32[16]{0:T(128)} %lev.9, s32[16,16]{1,0:T(8,128)} %convert_bitcast_fusion.levall, s32[16]{0:T(128)} %partner.7), custom_call_target="tpu_custom_call" | custom-call | tf_op jit(solution)/shard_map/first/pallas_call | solution.py:543
  40.3 0.0 all-to-all-done.1.rates
  40.3 0.0 copy-start.1
  40.3 14.8 %all-to-all-start = ((f32[256,1,256]{2,1,0:T(1,128)}), f32[256,1,256]{2,1,0:T(1,128)S(1)}, u32[]{:S(2)}, u32[]{:S(2)}) async-start(f32[256,1,256]{2,1,0:T(1,128)} %get-tuple-element.28), calls=%async_computation | async-start | bytes 524288 | tf_op jit(solution)/shard_map/all_to_all | solution.py:530
  55.1 0.0 copy-done.1
  55.1 12.4 %ahead1.1 = (f32[6,8,128]{2,1,0:T(8,128)}, s32[8,32]{1,0:T(8,128)}) custom-call(s32[1]{0:T(128)} %bitcast.me, f32[16,120,128]{2,1,0:T(8,128)} %bitcast.9, f32[16,96,128]{2,1,0:T(8,128)} %copy-done.1, s32[16]{0:T(128)} %lev.9, s32[16,16]{1,0:T(8,128)} %convert_bitcast_fusion.levall, s32[16]{0:T(128)} %partner.7, f32[17,8,128]{2,1,0:T(8,128)} %get-tuple-element.29.state.state_in), custom_call_target="tpu_custom_call" | custom-call | tf_op jit(solution)/shard_map/ahead1/pallas_call | solution.py:571
  67.5 0.6 all-to-all-done.got
  68.0 0.0 copy-start.4
  68.0 0.7 copy-done.4
  68.7 7.2 %after1.1 = (f32[17,8,128]{2,1,0:T(8,128)}, f32[256,1,384]{2,1,0:T(1,128)}, f32[8,8,256]{2,1,0:T(8,128)}) custom-call(f32[256,1,256]{2,1,0:T(1,128)} %copy-done.4, f32[17,8,128]{2,1,0:T(8,128)} %get-tuple-element.29.state.state_in, f32[6,8,128]{2,1,0:T(8,128)} %get-tuple-element.31.sums, s32[8,32]{1,0:T(8,128)} %get-tuple-element.32.plan.rest_1_), custom_call_target="tpu_custom_call" | custom-call | tf_op jit(solution)/shard_map/after1/pallas_call | solution.py:594
  76.0 12.9 %all-to-all-start.2 = ((f32[256,1,384]{2,1,0:T(1,128)}), f32[256,1,384]{2,1,0:T(1,128)S(1)}, u32[]{:S(2)}, u32[]{:S(2)}) async-start(f32[256,1,384]{2,1,0:T(1,128)} %get-tuple-element.33), calls=%async_computation.2 | async-start | bytes 786432 | tf_op jit(solution)/shard_map/all_to_all | solution.py:530
  88.9 9.7 %ahead2.1 = (f32[4,8,128]{2,1,0:T(8,128)}, s32[8,32]{1,0:T(8,128)}, f32[3,8,128]{2,1,0:T(8,128)}, f32[4,8,128]{2,1,0:T(8,128)}, s32[304]{0:T(512)}) custom-call(s32[1]{0:T(128)} %bitcast.me, f32[16,120,128]{2,1,0:T(8,128)} %bitcast.10, f32[16,96,128]{2,1,0:T(8,128)} %copy-done.1, s32[16]{0:T(128)} %lev.9, s32[16,16]{1,0:T(8,128)} %convert_bitcast_fusion.levall, ...), custom_call_target="tpu_custom_call" | custom-call | tf_op jit(solution)/shard_map/ahead2/pallas_call | solution.py:571
  98.6 5.9 %all-to-all-done.2.got = f32[256,1,384]{2,1,0:T(1,128)S(1)} async-done(((f32[256,1,384]{2,1,0:T(1,128)}), f32[256,1,384]{2,1,0:T(1,128)S(1)}, u32[]{:S(2)}, u32[]{:S(2)}) %all-to-all-start.2) | async-done | bytes 393248 | tf_op jit(solution)/shard_map/all_to_all | solution.py:530
  104.5 0.0 copy-start.3
  104.5 0.7 copy-done.3
  105.3 6.5 %after2.1 = (f32[17,8,128]{2,1,0:T(8,128)}, f32[256,1,384]{2,1,0:T(1,128)}) custom-call(f32[256,1,384]{2,1,0:T(1,128)} %copy-done.3, f32[17,8,128]{2,1,0:T(8,128)} %get-tuple-element.34.state.state_in, f32[4,8,128]{2,1,0:T(8,128)} %get-tuple-element.35.sums, s32[8,32]{1,0:T(8,128)} %get-tuple-element.36.plan, f32[8,8,256]{2,1,0:T(8,128)} %get-tuple-element.37.rest_0_, ...), custom_call_target="tpu_custom_call" | custom-call | tf_op jit(solution)/shard_map/after2/pallas_call | solution.py:594
  111.7 9.9 %all-to-all-start.3 = ((f32[256,1,384]{2,1,0:T(1,128)}), f32[256,1,384]{2,1,0:T(1,128)S(1)}, u32[]{:S(2)}, u32[]{:S(2)}) async-start(f32[256,1,384]{2,1,0:T(1,128)} %get-tuple-element.39), calls=%async_computation.3 | async-start | bytes 786432 | tf_op jit(solution)/shard_map/all_to_all | solution.py:530
  121.7 13.5 %ahead3.1 = (f32[8,8,128]{2,1,0:T(8,128)}, s32[8,32]{1,0:T(8,128)}) custom-call(s32[1]{0:T(128)} %bitcast.me, f32[16,120,128]{2,1,0:T(8,128)} %bitcast.11, f32[16,96,128]{2,1,0:T(8,128)} %copy-done.1, s32[16]{0:T(128)} %lev.9, s32[16,16]{1,0:T(8,128)} %convert_bitcast_fusion.levall, s32[16]{0:T(128)} %partner.7, ...), custom_call_target="tpu_custom_call" | custom-call | tf_op jit(solution)/shard_map/ahead3/pallas_call | solution.py:571
  135.2 2.2 %all-to-all-done.3.got = f32[256,1,384]{2,1,0:T(1,128)S(1)} async-done(((f32[256,1,384]{2,1,0:T(1,128)}), f32[256,1,384]{2,1,0:T(1,128)S(1)}, u32[]{:S(2)}, u32[]{:S(2)}) %all-to-all-start.3) | async-done | bytes 393248 | tf_op jit(solution)/shard_map/all_to_all | solution.py:530
  137.3 0.0 copy-start.2
  137.3 0.7 copy-done.2
  138.1 9.2 %after3.1 = f32[16,1,1152]{2,1,0:T(1,128)} custom-call(f32[256,1,384]{2,1,0:T(1,128)} %copy-done.2, f32[17,8,128]{2,1,0:T(8,128)} %get-tuple-element.40.state.state_in, f32[8,8,128]{2,1,0:T(8,128)} %get-tuple-element.43.sums, s32[8,32]{1,0:T(8,128)} %get-tuple-element.44.plan, f32[8,8,256]{2,1,0:T(8,128)} %get-tuple-element.37.rest_0_, ...), custom_call_target="tpu_custom_call" | custom-call | tf_op jit(solution)/shard_map/after3/pallas_call | solution.py:594
  147.3 16.6 %all_to_all.25.got = f32[16,1,1152]{2,1,0:T(1,128)} all-to-all(f32[16,1,1152]{2,1,0:T(1,128)} %after3.1), channel_id=1, replica_groups=mesh['blk'=16,'grp'=16] {'grp'}, dimensions={0} | all-to-all | bytes 147456 | tf_op jit(solution)/shard_map/all_to_all | solution.py:530
  163.9 2.5 %last.1 = (f32[6,2048]{1,0:T(8,128)}, f32[6,2048]{1,0:T(8,128)}, f32[6,2048]{1,0:T(8,128)}) custom-call(f32[16,1,1152]{2,1,0:T(1,128)} %all_to_all.25.got, f32[6,2048]{1,0:T(8,128)} %ps.3, f32[6,2048]{1,0:T(8,128)} %fr.3, f32[6,2048]{1,0:T(8,128)} %irr.1, s32[8,32]{1,0:T(8,128)} %get-tuple-element.44.plan), custom_call_target="tpu_custom_call" | custom-call | tf_op jit(solution)/shard_map/last/pallas_call | solution.py:615
  (1 shorter events, 0.0 us)
Async XLA Ops:
  22.1 8.1 %copy-start = (f32[1920,128]{1,0:T(8,128)}, f32[1920,128]{1,0:T(8,128)S(1)}, u32[]{:S(2)}) copy-start(f32[1920,128]{1,0:T(8,128)S(1)} %all-gather) | copy-start | bytes 2949124
  22.1 18.2 %all-to-all-start.1 = ((f32[16,96,128]{2,1,0:T(8,128)}), f32[16,96,128]{2,1,0:T(8,128)S(1)}, u32[]{:S(2)}, u32[]{:S(2)}) async-start(f32[16,96,128]{2,1,0:T(8,128)} %get-tuple-element.30), calls=%async_computation.1 | async-start | bytes 1572864 | tf_op jit(solution)/shard_map/all_to_all | solution.py:530
  40.3 14.8 %copy-start.1 = (f32[16,96,128]{2,1,0:T(8,128)}, f32[16,96,128]{2,1,0:T(8,128)S(1)}, u32[]{:S(2)}) copy-start(f32[16,96,128]{2,1,0:T(8,128)S(1)} %all-to-all-done.1.rates) | copy-start | bytes 2359300
  40.3 27.7 %all-to-all-start = ((f32[256,1,256]{2,1,0:T(1,128)}), f32[256,1,256]{2,1,0:T(1,128)S(1)}, u32[]{:S(2)}, u32[]{:S(2)}) async-start(f32[256,1,256]{2,1,0:T(1,128)} %get-tuple-element.28), calls=%async_computation | async-start | bytes 524288 | tf_op jit(solution)/shard_map/all_to_all | solution.py:530
  68.0 0.7 copy-start.4
  76.0 28.5 %all-to-all-start.2 = ((f32[256,1,384]{2,1,0:T(1,128)}), f32[256,1,384]{2,1,0:T(1,128)S(1)}, u32[]{:S(2)}, u32[]{:S(2)}) async-start(f32[256,1,384]{2,1,0:T(1,128)} %get-tuple-element.33), calls=%async_computation.2 | async-start | bytes 786432 | tf_op jit(solution)/shard_map/all_to_all | solution.py:530
  104.5 0.7 copy-start.3
  111.7 25.6 %all-to-all-start.3 = ((f32[256,1,384]{2,1,0:T(1,128)}), f32[256,1,384]{2,1,0:T(1,128)S(1)}, u32[]{:S(2)}, u32[]{:S(2)}) async-start(f32[256,1,384]{2,1,0:T(1,128)} %get-tuple-element.39), calls=%async_computation.3 | async-start | bytes 786432 | tf_op jit(solution)/shard_map/all_to_all | solution.py:530
  137.3 0.7 copy-start.2
